TPU v7x, 256 devices: a whole 4x4x8 slice. The times are simulated.
256 devices in a mesh: dp: 64 (over z, x, core), tensor: 4 (over y).
Axes of the slice: x: 4, y: 4, z: 8, core: 2. Of those that a mesh axis runs over, the one named last changes fastest.
Arguments:
- hidden: bfloat16 [8192, 4096], P('dp', 'tensor'), may hold values from -6 to 6
- grad_out: bfloat16 [8192, 4096], P('dp', 'tensor'), may hold values from -0.59765625 to 0.59765625
- query_weight: bfloat16 [4096, 4096], P(None, 'tensor'), may hold values from -0.09375 to 0.09375
- key_weight: bfloat16 [768, 4096], P(None, 'tensor'), may hold values from -0.21875 to 0.21875
- value_weight: bfloat16 [768, 4096], P(None, 'tensor'), may hold values from -0.21875 to 0.21875
- out_weight: bfloat16 [4096, 4096], P('tensor', 'dp'), may hold values from -0.75 to 0.75
- neighbour_states: bfloat16 [256, 128, 768], P('dp', None, 'tensor'), may hold values from -6 to 6
- block_owner: int32 [64, 4], P('dp'), may hold values from 0 to 63, as said below
- slot_target: int32 [64, 4], P('dp'), may hold values from 0 to 63, as said below
Outputs:
- cross_out: bfloat16 [8192, 4096], P('dp', 'tensor')
- grad_hidden: bfloat16 [8192, 4096], P('dp', 'tensor')
- grad_states: bfloat16 [256, 128, 768], P('dp', None, 'tensor')
Inputs may be any that keep to these rules, and one draw needn't show every extreme that they name: block_owner[d, t] = o exactly when slot_target[o, t] = d. The blocks 2k and 2k+1 of a dp index share their holder; the difference (holder - d) modulo the dp count is the same for every d, lies in 1 to 4, and differs between k. So a dp index holds exactly 2 blocks for each of 2 other indices. `slot_target`: the inverse map of block_owner, as stated there.
All inputs are finite; a program needn't handle non-finite values.
Results may differ from a plain program's by a relative error of at most 0.012.
Values may be sent and summed in bfloat16 or wider, within the bound.
No kernel may reach another device: no remote copies, remote signals or barrier semaphores. Data moves between devices by JAX's collectives and lax.ppermute only.
A program may use at most 128 MiB of HBM per device.

v0:
```python
import functools
import math

import jax
import jax.numpy as jnp
from jax import lax
from jax.experimental import pallas as pl
from jax.experimental.pallas import tpu as pltpu
from jax.sharding import Mesh, PartitionSpec as P

HEAD = 128
SPAN = 64
NBR = 128
WINDOW = 4
DP = ("z", "x", "core")
MIB = 1024 * 1024
F32, BF16 = jnp.float32, jnp.bfloat16

NN = (((1,), (0,)), ((), ()))
NT = (((1,), (1,)), ((), ()))
TN = (((0,), (0,)), ((), ()))


def dot(a, b, dims=NN):
    return lax.dot_general(a, b, dims, preferred_element_type=F32)


def params(mib):
    return pltpu.CompilerParams(vmem_limit_bytes=mib * MIB)


ANY = pl.BlockSpec(memory_space=pl.ANY)
SMEM = pl.BlockSpec(memory_space=pltpu.SMEM)


def whole(shape):
    return pl.BlockSpec(shape, lambda *_: (0,) * len(shape))


def cost(flops, nbytes):
    return pl.CostEstimate(flops=int(flops), bytes_accessed=int(nbytes), transcendentals=0)


def from_peers(x):
    n = lax.axis_size("tensor")
    got = [x]
    for r in range(1, n):
        got.append(lax.ppermute(x, "tensor", [((i + r) % n, i) for i in range(n)]))
    return got


def to_peers(pieces):
    n = lax.axis_size("tensor")
    got = [pieces[0]]
    for r in range(1, n):
        got.append(lax.ppermute(pieces[r], "tensor", [(i, (i + r) % n) for i in range(n)]))
    return got


def exchanged(x):
    return lax.all_to_all(x, "tensor", split_axis=0, concat_axis=0, tiled=True)


def summed(parts):
    total = parts[0].astype(F32)
    for part in parts[1:]:
        total = total + part.astype(F32)
    return total.astype(BF16)


def nothing(*_):
    pass


def tied(x, *after):
    return pl.pallas_call(
        nothing,
        out_shape=jax.ShapeDtypeStruct(x.shape, x.dtype),
        in_specs=[ANY] * (1 + len(after)),
        out_specs=ANY,
        input_output_aliases={0: 0},
        name="tied",
    )(x, *after)


def query_kernel(h_ref, w_ref, q_ref, acc):
    i, last = pl.program_id(0), pl.num_programs(0) - 1
    part = dot(h_ref[0], w_ref[...])

    @pl.when(i == 0)
    def _():
        acc[...] = part

    @pl.when(jnp.logical_and(i > 0, i < last))
    def _():
        acc[...] += part

    @pl.when(i == last)
    def _():
        q_ref[...] = (acc[...] + part).astype(BF16)


def query_of(pieces, weight):
    steps, rows, width = pieces.shape
    rows, cols = rows // 2, weight.shape[1]
    return pl.pallas_call(
        query_kernel,
        out_shape=jax.ShapeDtypeStruct((rows, cols), BF16),
        grid=(steps,),
        in_specs=[
            pl.BlockSpec((1, rows, width), lambda i: (i, 0, 0)),
            pl.BlockSpec((width, cols), lambda i: (i, 0)),
        ],
        out_specs=whole((rows, cols)),
        scratch_shapes=[pltpu.VMEM((rows, cols), F32)],
        compiler_params=params(56),
        cost_estimate=cost(2 * rows * steps * width * cols, 2 * steps * width * cols),
        name="query",
    )(pieces, weight)


def forward_kernel(
    scale, t_ref, q_ref, n0, n1, n2, n3, kw_ref, vw_ref, k_ref, v_ref, p_ref, a_ref, flipped, rows
):
    blocks, part, length = n0.shape

    @pl.when(pl.program_id(0) == 0)
    def _():
        for r, n in enumerate((n0, n1, n2, n3)):
            at = pl.multiple_of(((t_ref[0] + r) % 4) * part, part)
            for b in range(blocks):
                flipped[pl.ds(at, part), b * length : (b + 1) * length] = n[b]
        rows[...] = flipped[...].T

    k_ref[...] = dot(rows[...], kw_ref[...]).astype(BF16)
    v_ref[...] = dot(rows[...], vw_ref[...]).astype(BF16)
    spans = q_ref.shape[0] // SPAN
    keys = k_ref.shape[0] // spans
    for j in range(q_ref.shape[1] // HEAD):
        c = slice(j * HEAD, (j + 1) * HEAD)
        for s in range(spans):
            qs = slice(s * SPAN, (s + 1) * SPAN)
            ks = slice(s * keys, (s + 1) * keys)
            scores = dot(q_ref[qs, c], k_ref[ks, c], NT) * scale
            e = jnp.exp(scores - jnp.max(scores, axis=-1, keepdims=True))
            probs = e / jnp.sum(e, axis=-1, keepdims=True)
            p_ref[j, s] = probs
            a_ref[qs, c] = dot(probs.astype(BF16), v_ref[ks, c]).astype(BF16)


def forward_of(t, query, pieces, key_weight, value_weight):
    rows, cols = query.shape
    blocks, part, length = pieces[0].shape
    tokens, width = blocks * length, key_weight.shape[0]
    spans = rows // SPAN
    step = 2 * HEAD
    col = lambda n: pl.BlockSpec((n, step), lambda j, t: (0, j))
    return pl.pallas_call(
        functools.partial(forward_kernel, 1.0 / math.sqrt(HEAD)),
        out_shape=(
            jax.ShapeDtypeStruct((tokens, cols), BF16),
            jax.ShapeDtypeStruct((tokens, cols), BF16),
            jax.ShapeDtypeStruct((cols // HEAD, spans, SPAN, tokens // spans), F32),
            jax.ShapeDtypeStruct((rows, cols), BF16),
        ),
        grid_spec=pltpu.PrefetchScalarGridSpec(
            num_scalar_prefetch=1,
            grid=(cols // step,),
            in_specs=[col(rows)] + [whole(pieces[0].shape)] * 4 + [col(width)] * 2,
            out_specs=[
                col(tokens),
                col(tokens),
                pl.BlockSpec((2, spans, SPAN, tokens // spans), lambda j, t: (j, 0, 0, 0)),
                col(rows),
            ],
            scratch_shapes=[pltpu.VMEM((width, tokens), BF16), pltpu.VMEM((tokens, width), BF16)],
        ),
        compiler_params=params(56),
        cost_estimate=cost(4 * tokens * width * cols, 10e6),
        name="forward",
    )(t, query, *pieces, key_weight, value_weight)


def output_kernel(t_ref, a_ref, g_ref, own, other, o_ref, ga_ref, w_ref, sems):
    core, x = t_ref[1], t_ref[2]
    steps, _, width = g_ref.shape
    chips = own.shape[1]
    deep = own.shape[0] // steps
    copies = []
    for i in range(steps):
        for s in range(chips):
            at = (x - s + chips) % chips
            for n, (plane, c) in enumerate(((own, core), (other, 1 - core))):
                copies.append(
                    pltpu.make_async_copy(
                        plane.at[pl.ds(i * deep, deep), s], w_ref.at[i, :, at, c], sems.at[i, 2 * s + n]
                    )
                )
    for copy in copies:
        copy.start()
    total = None
    for i in range(steps):
        for copy in copies[i * 2 * chips : (i + 1) * 2 * chips]:
            copy.wait()
        w = w_ref[i].reshape(width, a_ref.shape[1])
        part = dot(g_ref[i], w)
        total = part if total is None else total + part
        o_ref[i] = dot(a_ref[...], w, NT).astype(BF16)
    ga_ref[...] = total.astype(BF16)


def output_of(t, attended, pieces, own, other):
    rows, cols = attended.shape
    steps, _, width = pieces.shape
    deep, chips = own.shape[0] // steps, own.shape[1]
    return pl.pallas_call(
        output_kernel,
        out_shape=(
            jax.ShapeDtypeStruct((steps, rows, width), BF16),
            jax.ShapeDtypeStruct((rows, cols), BF16),
        ),
        grid=(1,),
        in_specs=[
            SMEM,
            whole((rows, cols)),
            pl.BlockSpec((steps, rows, width), lambda i: (0, 1, 0)),
            ANY,
            ANY,
        ],
        out_specs=(whole((steps, rows, width)), whole((rows, cols))),
        scratch_shapes=[
            pltpu.VMEM((steps, deep, chips, 2, *own.shape[2:]), BF16),
            pltpu.SemaphoreType.DMA((steps, 2 * chips)),
        ],
        compiler_params=params(28),
        cost_estimate=cost(4 * rows * steps * width * cols, 2 * steps * width * cols),
        name="output",
    )(t, attended, pieces, own, other)


def backward_kernel(
    scale, t_ref, ga_ref, q_ref, k_ref, v_ref, p_ref, kw_ref, vw_ref, gq_ref, s0, s1, s2, s3, gk, gv, acc
):
    j, last = pl.program_id(0), pl.num_programs(0) - 1
    spans = q_ref.shape[0] // SPAN
    keys = k_ref.shape[0] // spans
    for h in range(q_ref.shape[1] // HEAD):
        c = slice(h * HEAD, (h + 1) * HEAD)
        for s in range(spans):
            qs = slice(s * SPAN, (s + 1) * SPAN)
            ks = slice(s * keys, (s + 1) * keys)
            probs, ga = p_ref[h, s], ga_ref[qs, c]
            gp = dot(ga, v_ref[ks, c], NT)
            inner = jnp.sum(probs * gp, axis=-1, keepdims=True)
            gs = (probs * (gp - inner) * scale).astype(BF16)
            gq_ref[qs, c] = dot(gs, k_ref[ks, c]).astype(BF16)
            gk[ks, c] = dot(gs, q_ref[qs, c], TN).astype(BF16)
            gv[ks, c] = dot(probs.astype(BF16), ga, TN).astype(BF16)
    part = dot(kw_ref[...], gk[...], NT) + dot(vw_ref[...], gv[...], NT)

    @pl.when(j == 0)
    def _():
        acc[...] = part

    @pl.when(j > 0)
    def _():
        acc[...] += part

    @pl.when(j == last)
    def _():
        blocks, rows, length = s0.shape
        for r, out in enumerate((s0, s1, s2, s3)):
            at = pl.multiple_of(((t_ref[0] + r) % 4) * rows, rows)
            for b in range(blocks):
                out[b] = acc[pl.ds(at, rows), b * length : (b + 1) * length].astype(BF16)


def backward_of(t, ga, query, key, value, probs, key_weight, value_weight, piece):
    rows, cols = query.shape
    tokens, width = key.shape[0], key_weight.shape[0]
    spans = rows // SPAN
    step = 2 * HEAD
    col = lambda n: pl.BlockSpec((n, step), lambda j, t: (0, j))
    return pl.pallas_call(
        functools.partial(backward_kernel, 1.0 / math.sqrt(HEAD)),
        out_shape=[jax.ShapeDtypeStruct((rows, cols), BF16)] + [jax.ShapeDtypeStruct(piece, BF16)] * 4,
        grid_spec=pltpu.PrefetchScalarGridSpec(
            num_scalar_prefetch=1,
            grid=(cols // step,),
            in_specs=[
                col(rows),
                col(rows),
                col(tokens),
                col(tokens),
                pl.BlockSpec((2, spans, SPAN, tokens // spans), lambda j, t: (j, 0, 0, 0)),
                col(width),
                col(width),
            ],
            out_specs=[col(rows)] + [whole(piece)] * 4,
            scratch_shapes=[
                pltpu.VMEM((tokens, step), BF16),
                pltpu.VMEM((tokens, step), BF16),
                pltpu.VMEM((width, tokens), F32),
            ],
        ),
        compiler_params=params(56),
        cost_estimate=cost(4 * tokens * width * cols, 10e6),
        name="backward",
    )(t, ga, query, key, value, probs, key_weight, value_weight)


def hidden_kernel(g_ref, w_ref, o_ref):
    o_ref[0] = dot(g_ref[...], w_ref[...], NT).astype(BF16)


def hidden_of(grad_query, weight):
    rows, cols = grad_query.shape
    width = weight.shape[0] // 4
    return pl.pallas_call(
        hidden_kernel,
        out_shape=jax.ShapeDtypeStruct((4, rows, width), BF16),
        grid=(4,),
        in_specs=[whole((rows, cols)), pl.BlockSpec((width, cols), lambda i: (i, 0))],
        out_specs=pl.BlockSpec((1, rows, width), lambda i: (i, 0, 0)),
        compiler_params=params(56),
        cost_estimate=cost(2 * rows * 4 * width * cols, 8 * width * cols),
        name="hidden",
    )(grad_query, weight)


def pairs_moved(blocks, gaps, sign):
    n = math.prod(lax.axis_size(a) for a in DP)
    pairs = blocks[:2], blocks[2:]
    got = [None, None]
    for by in range(1, WINDOW + 1):
        sent = jnp.where(gaps[0] == by, *pairs)
        came = lax.ppermute(sent, DP, [(i, (i + sign * by) % n) for i in range(n)])
        got = [came if g is None else jnp.where(gaps[k] == by, came, g) for k, g in enumerate(got)]
    return jnp.concatenate(got, axis=0)


def gathered_plane(rows):
    n = lax.axis_size("x")
    along = [rows]
    for s in range(1, n):
        along.append(lax.ppermute(rows, "x", [(i, (i + s) % n) for i in range(n)]))
    return lax.all_gather(jnp.stack(along), "z", axis=0)


def shards(
    hidden,
    grad_out,
    query_weight,
    key_weight,
    value_weight,
    out_weight,
    neighbour_states,
    block_owner,
    slot_target,
):
    n_dp = math.prod(lax.axis_size(a) for a in DP)
    t = jnp.stack([lax.axis_index(a) for a in ("tensor", "core", "x")]).astype(jnp.int32)
    plane = gathered_plane(out_weight.T)

    gap = (block_owner[0] - lax.axis_index(DP) + n_dp) % n_dp
    gaps = (gap[0], gap[2])
    both = jnp.concatenate([hidden, grad_out], axis=0)
    pieces = exchanged(jnp.broadcast_to(both, (lax.axis_size("tensor"), *both.shape)))
    pieces = pieces.reshape(-1, *both.shape)
    mine = pairs_moved(jnp.swapaxes(neighbour_states, 1, 2), gaps, -1)
    neighbours = from_peers(mine)

    query = query_of(pieces, query_weight)
    key, value, probs, attended = forward_of(t, query, neighbours, key_weight, value_weight)
    plane = tied(plane, attended)
    other_plane = lax.ppermute(plane, "core", [(0, 1), (1, 0)])
    out_parts, grad_attended = output_of(t, attended, pieces, plane, other_plane)
    cross_out = summed(exchanged(out_parts))
    grad_query, *state_parts = backward_of(
        t, grad_attended, query, key, value, probs, key_weight, value_weight, mine.shape
    )
    grad_hidden = summed(exchanged(hidden_of(grad_query, query_weight)))
    grads = summed(to_peers(state_parts))
    grad_states = jnp.swapaxes(pairs_moved(grads, gaps, 1), 1, 2)
    return cross_out, grad_hidden, grad_states


def solution(mesh):
    grid = Mesh(mesh.devices.reshape(8, 4, 2, 4), DP + ("tensor",))
    placed = (
        P(DP, "tensor"),
        P(DP, "tensor"),
        P(None, "tensor"),
        P(None, "tensor"),
        P(None, "tensor"),
        P("tensor", DP),
        P(DP, None, "tensor"),
        P(DP, None),
        P(DP, None),
    )
    return jax.shard_map(
        shards,
        mesh=grid,
        in_specs=placed,
        out_specs=(P(DP, "tensor"), P(DP, "tensor"), P(DP, None, "tensor")),
        check_vma=False,
    )
```

profile of v0, /device:TPU:96, one launch (start us, length us, event | category | flops | bytes accessed | tf_op | source)
XLA Modules:
  0.0 155.2 jit_solution(16305908365858800893)
XLA Ops:
  7.2 3.1 %collective-permute-start.8 = (bf16[64,1024]{1,0:T(8,128)(2,1)}, bf16[64,1024]{1,0:T(8,128)(2,1)S(1)}, u32[]{:S(2)}, u32[]{:S(2)}) collective-permute-start(bf16[64,1024]{1,0:T(8,128)(2,1)} %bitcast.28), channel_id=1, source_target_pairs={{0,16},{8,24},{16,0},{24,8},{1,17},{9,25},{17,1},{25,9},{2,18},{10... | collective-permute-start | bytes 393224 | tf_op jit(solution)/shard_map/ppermute | solution.py:346
  10.9 2.6 %collective-permute-start.9 = (bf16[64,1024]{1,0:T(8,128)(2,1)}, bf16[64,1024]{1,0:T(8,128)(2,1)S(1)}, u32[]{:S(2)}, u32[]{:S(2)}) collective-permute-start(bf16[64,1024]{1,0:T(8,128)(2,1)} %bitcast.30), channel_id=1, source_target_pairs={{0,24},{8,0},{16,8},{24,16},{1,25},{9,1},{17,9},{25,17},{2,26},{10... | collective-permute-start | bytes 393224 | tf_op jit(solution)/shard_map/ppermute | solution.py:346
  15.3 2.1 %collective-permute-done.7 = bf16[64,1024]{1,0:T(8,128)(2,1)S(1)} collective-permute-done((bf16[64,1024]{1,0:T(8,128)(2,1)}, bf16[64,1024]{1,0:T(8,128)(2,1)S(1)}, u32[]{:S(2)}, u32[]{:S(2)}) %collective-permute-start.7) | collective-permute-done | bytes 131104 | tf_op jit(solution)/shard_map/ppermute | solution.py:346
  22.0 4.5 %all-to-all-start = ((bf16[4,256,1024]{2,1,0:T(8,128)(2,1)}), bf16[4,256,1024]{2,1,0:T(8,128)(2,1)S(1)}, u32[]{:S(2)}, u32[]{:S(2)}) async-start(bf16[4,256,1024]{2,1,0:T(8,128)(2,1)} %broadcast_in_dim.3), calls=%async_computation | async-start | bytes 4194304 | tf_op jit(solution)/shard_map/all_to_all | solution.py:61
  32.6 2.2 %collective-permute-start.1 = (bf16[2,192,128]{2,1,0:T(8,128)(2,1)S(1)}, bf16[2,192,128]{2,1,0:T(8,128)(2,1)S(1)}, u32[]{:S(2)}, u32[]{:S(2)}) collective-permute-start(bf16[2,192,128]{2,1,0:T(8,128)(2,1)S(1)} %get-tuple-element.36), channel_id=1, source_target_pairs={{0,244},{4,248},{8,252},{12,0},{16,4},{20,8},{24,12},{28,16},{32,2... | collective-permute-start | bytes 294920 | tf_op jit(solution)/shard_map/ppermute | solution.py:337
  38.1 4.2 %collective-permute-done = bf16[2,192,128]{2,1,0:T(8,128)(2,1)S(1)} collective-permute-done((bf16[2,192,128]{2,1,0:T(8,128)(2,1)S(1)}, bf16[2,192,128]{2,1,0:T(8,128)(2,1)S(1)}, u32[]{:S(2)}, u32[]{:S(2)}) %collective-permute-start) | collective-permute-done | bytes 98336 | tf_op jit(solution)/shard_map/ppermute | solution.py:337
  42.3 3.8 %collective-permute-done.1 = bf16[2,192,128]{2,1,0:T(8,128)(2,1)S(1)} collective-permute-done((bf16[2,192,128]{2,1,0:T(8,128)(2,1)S(1)}, bf16[2,192,128]{2,1,0:T(8,128)(2,1)S(1)}, u32[]{:S(2)}, u32[]{:S(2)}) %collective-permute-start.1) | collective-permute-done | bytes 98336 | tf_op jit(solution)/shard_map/ppermute | solution.py:337
  46.2 2.4 %collective-permute-start.6 = (bf16[4,192,128]{2,1,0:T(8,128)(2,1)S(1)}, bf16[4,192,128]{2,1,0:T(8,128)(2,1)S(1)}, u32[]{:S(2)}, u32[]{:S(2)}) collective-permute-start(bf16[4,192,128]{2,1,0:T(8,128)(2,1)S(1)} %pad_maximum_fusion.2.n0), channel_id=1, source_target_pairs={{3,0},{0,1},{1,2},{2,3},{7,4},{4,5},{5,6},{6,7},{11,8},{8,9},{9,10... | collective-permute-start | bytes 589832 | tf_op jit(solution)/shard_map/ppermute | solution.py:48
  48.6 2.6 %collective-permute-start.5 = (bf16[4,192,128]{2,1,0:T(8,128)(2,1)S(1)}, bf16[4,192,128]{2,1,0:T(8,128)(2,1)S(1)}, u32[]{:S(2)}, u32[]{:S(2)}) collective-permute-start(bf16[4,192,128]{2,1,0:T(8,128)(2,1)S(1)} %pad_maximum_fusion.2.n0), channel_id=1, source_target_pairs={{2,0},{3,1},{0,2},{1,3},{6,4},{7,5},{4,6},{5,7},{10,8},{11,9},{8,1... | collective-permute-start | bytes 589832 | tf_op jit(solution)/shard_map/ppermute | solution.py:48
  55.4 6.0 %query.1.q_ref = bf16[128,1024]{1,0:T(8,128)(2,1)} custom-call(bf16[4,256,1024]{2,1,0:T(8,128)(2,1)} %copy-done, bf16[4096,1024]{1,0:T(8,128)(2,1)} %w_ref.3), custom_call_target="tpu_custom_call" | custom-call | flops 1073741824 | bytes 8388608 | tf_op jit(solution)/shard_map/query/pallas_call | solution.py:106
  62.8 10.1 %forward.1 = (bf16[512,1024]{1,0:T(8,128)(2,1)}, bf16[512,1024]{1,0:T(8,128)(2,1)}, f32[8,2,64,256]{3,2,1,0:T(8,128)}, bf16[128,1024]{1,0:T(8,128)(2,1)}) custom-call(s32[3]{0:T(128)} %pad_add_fusion.t_ref, bf16[128,1024]{1,0:T(8,128)(2,1)} %query.1.q_ref, bf16[4,192,128]{2,1,0:T(8,128)(2,1)} %copy-done.6, bf16[4,192,128]{2,1,0:T(8,128)(2,1)} %copy-done.11, ...), custom_call_target="tpu_custom_call" | custom-call | flops 1610612736 | bytes 10000000 | tf_op jit(solution)/shard_map/forward/pallas_call | solution.py:158
  72.9 9.6 %all-gather.3.cloned.1.call-done = bf16[32,64,1024]{2,1,0:T(8,128)(2,1)} async-done(((bf16[4,64,1024]{2,1,0:T(8,128)(2,1)}), bf16[32,64,1024]{2,1,0:T(8,128)(2,1)}) %all-gather.3.cloned.1.call-update) | async-done | bytes 4194320 | tf_op jit(solution)/shard_map/all_gather | solution.py:347
  82.5 7.3 %collective-permute-done.10.other = bf16[8,4,64,1024]{3,2,1,0:T(8,128)(2,1)S(1)} collective-permute-done((bf16[8,4,64,1024]{3,2,1,0:T(8,128)(2,1)}, bf16[8,4,64,1024]{3,2,1,0:T(8,128)(2,1)S(1)}, u32[]{:S(2)}, u32[]{:S(2)}) %collective-permute-start.10) | collective-permute-done | bytes 4194336 | tf_op jit(solution)/shard_map/ppermute | solution.py:376
  89.9 2.2 %copy-done.2 = bf16[8,4,64,1024]{3,2,1,0:T(8,128)(2,1)S(1)} copy-done((bf16[8,4,64,1024]{3,2,1,0:T(8,128)(2,1)S(1)}, bf16[8,4,64,1024]{3,2,1,0:T(8,128)(2,1)}, u32[]{:S(2)}) %copy-start.2) | copy-done | bytes 4194328
  92.0 7.0 %output.1 = (bf16[4,128,1024]{2,1,0:T(8,128)(2,1)}, bf16[128,1024]{1,0:T(8,128)(2,1)S(1)}) custom-call(s32[3]{0:T(128)S(1)} %copy-done.5, bf16[128,1024]{1,0:T(8,128)(2,1)S(1)} %copy-done.3, bf16[4,256,1024]{2,1,0:T(8,128)(2,1)S(1)} %copy-done.1, bf16[8,4,64,1024]{3,2,1,0:T(8,128)(2,1)S(1)} %copy-done.2, ...), custom_call_target="tpu_custom_call" | custom-call | flops 2147483648 | bytes 8388608 | tf_op jit(solution)/shard_map/output/pallas_call | solution.py:216
  99.7 4.5 %all-to-all-start.1 = ((bf16[4,128,1024]{2,1,0:T(8,128)(2,1)}), bf16[4,128,1024]{2,1,0:T(8,128)(2,1)S(1)}, u32[]{:S(2)}, u32[]{:S(2)}) async-start(bf16[4,128,1024]{2,1,0:T(8,128)(2,1)} %get-tuple-element.15), calls=%async_computation.1 | async-start | bytes 2097152 | tf_op jit(solution)/shard_map/all_to_all | solution.py:61
  104.2 11.4 %backward.1 = (bf16[128,1024]{1,0:T(8,128)(2,1)}, bf16[4,192,128]{2,1,0:T(8,128)(2,1)}, bf16[4,192,128]{2,1,0:T(8,128)(2,1)}, bf16[4,192,128]{2,1,0:T(8,128)(2,1)}, bf16[4,192,128]{2,1,0:T(8,128)(2,1)}) custom-call(s32[3]{0:T(128)} %pad_add_fusion.t_ref, bf16[128,1024]{1,0:T(8,128)(2,1)} %copy-done.4, bf16[128,1024]{1,0:T(8,128)(2,1)} %query.1.q_ref, ...), custom_call_target="tpu_custom_call" | custom-call | flops 1610612736 | bytes 10000000 | tf_op jit(solution)/shard_map/backward/pallas_call | solution.py:284
  115.6 2.1 %collective-permute-start.11 = (bf16[4,192,128]{2,1,0:T(8,128)(2,1)}, bf16[4,192,128]{2,1,0:T(8,128)(2,1)S(1)}, u32[]{:S(2)}, u32[]{:S(2)}) collective-permute-start(bf16[4,192,128]{2,1,0:T(8,128)(2,1)} %get-tuple-element.22), channel_id=1, source_target_pairs={{0,1},{1,2},{2,3},{3,0},{4,5},{5,6},{6,7},{7,4},{8,9},{9,10},{10,1... | collective-permute-start | bytes 589832 | tf_op jit(solution)/shard_map/ppermute | solution.py:56
  117.7 2.7 %collective-permute-start.12 = (bf16[4,192,128]{2,1,0:T(8,128)(2,1)}, bf16[4,192,128]{2,1,0:T(8,128)(2,1)S(1)}, u32[]{:S(2)}, u32[]{:S(2)}) collective-permute-start(bf16[4,192,128]{2,1,0:T(8,128)(2,1)} %get-tuple-element.23), channel_id=1, source_target_pairs={{0,2},{1,3},{2,0},{3,1},{4,6},{5,7},{6,4},{7,5},{8,10},{9,11},{10,... | collective-permute-start | bytes 589832 | tf_op jit(solution)/shard_map/ppermute | solution.py:56
  121.8 6.7 %hidden.1 = bf16[4,128,1024]{2,1,0:T(8,128)(2,1)} custom-call(bf16[128,1024]{1,0:T(8,128)(2,1)} %get-tuple-element.20.g_ref, bf16[4096,1024]{1,0:T(8,128)(2,1)} %w_ref.3), custom_call_target="tpu_custom_call" | custom-call | flops 1073741824 | bytes 8388608 | tf_op jit(solution)/shard_map/hidden/pallas_call | solution.py:319
  129.3 4.0 %all-to-all-start.2 = ((bf16[4,128,1024]{2,1,0:T(8,128)(2,1)}), bf16[4,128,1024]{2,1,0:T(8,128)(2,1)S(1)}, u32[]{:S(2)}, u32[]{:S(2)}) async-start(bf16[4,128,1024]{2,1,0:T(8,128)(2,1)} %hidden.1), calls=%async_computation.2 | async-start | bytes 2097152 | tf_op jit(solution)/shard_map/all_to_all | solution.py:61
  133.6 3.5 %collective-permute-start.15 = (bf16[2,192,128]{2,1,0:T(8,128)(2,1)S(1)}, bf16[2,192,128]{2,1,0:T(8,128)(2,1)S(1)}, u32[]{:S(2)}, u32[]{:S(2)}) collective-permute-start(bf16[2,192,128]{2,1,0:T(8,128)(2,1)S(1)} %get-tuple-element.32), channel_id=1, source_target_pairs={{0,12},{4,16},{8,20},{12,24},{16,28},{20,32},{24,36},{28,40},{32,4... | collective-permute-start | bytes 294920 | tf_op jit(solution)/shard_map/ppermute | solution.py:337
  137.0 3.3 %collective-permute-done.17 = bf16[2,192,128]{2,1,0:T(8,128)(2,1)S(1)} collective-permute-done((bf16[2,192,128]{2,1,0:T(8,128)(2,1)S(1)}, bf16[2,192,128]{2,1,0:T(8,128)(2,1)S(1)}, u32[]{:S(2)}, u32[]{:S(2)}) %collective-permute-start.17) | collective-permute-done | bytes 98336 | tf_op jit(solution)/shard_map/ppermute | solution.py:337
  140.3 2.7 %collective-permute-done.16 = bf16[2,192,128]{2,1,0:T(8,128)(2,1)S(1)} collective-permute-done((bf16[2,192,128]{2,1,0:T(8,128)(2,1)S(1)}, bf16[2,192,128]{2,1,0:T(8,128)(2,1)S(1)}, u32[]{:S(2)}, u32[]{:S(2)}) %collective-permute-start.16) | collective-permute-done | bytes 98336 | tf_op jit(solution)/shard_map/ppermute | solution.py:337
  (68 shorter events, 26.2 us)
Async XLA Ops:
  7.2 75.3 %all-gather.3.cloned.1.call-start = ((), (), s32[]{:S(2)}) async-start(), calls=%async_computation.3 | async-start | bytes 4718592 | tf_op jit(solution)/shard_map/all_gather | solution.py:347
  7.2 8.1 %collective-permute-start.8 = (bf16[64,1024]{1,0:T(8,128)(2,1)}, bf16[64,1024]{1,0:T(8,128)(2,1)S(1)}, u32[]{:S(2)}, u32[]{:S(2)}) collective-permute-start(bf16[64,1024]{1,0:T(8,128)(2,1)} %bitcast.28), channel_id=1, source_target_pairs={{0,16},{8,24},{16,0},{24,8},{1,17},{9,25},{17,1},{25,9},{2,18},{10... | collective-permute-start | bytes 393224 | tf_op jit(solution)/shard_map/ppermute | solution.py:346
  10.3 7.1 %collective-permute-start.7 = (bf16[64,1024]{1,0:T(8,128)(2,1)}, bf16[64,1024]{1,0:T(8,128)(2,1)S(1)}, u32[]{:S(2)}, u32[]{:S(2)}) collective-permute-start(bf16[64,1024]{1,0:T(8,128)(2,1)} %bitcast.29), channel_id=1, source_target_pairs={{0,8},{8,16},{16,24},{24,0},{1,9},{9,17},{17,25},{25,1},{2,10},{10... | collective-permute-start | bytes 393224 | tf_op jit(solution)/shard_map/ppermute | solution.py:346
  10.9 6.5 %collective-permute-start.9 = (bf16[64,1024]{1,0:T(8,128)(2,1)}, bf16[64,1024]{1,0:T(8,128)(2,1)S(1)}, u32[]{:S(2)}, u32[]{:S(2)}) collective-permute-start(bf16[64,1024]{1,0:T(8,128)(2,1)} %bitcast.30), channel_id=1, source_target_pairs={{0,24},{8,0},{16,8},{24,16},{1,25},{9,1},{17,9},{25,17},{2,26},{10... | collective-permute-start | bytes 393224 | tf_op jit(solution)/shard_map/ppermute | solution.py:346
  19.2 10.4 %copy-start.7 = (bf16[4,128,192]{1,2,0:T(8,128)(2,1)S(1)}, bf16[4,128,192]{1,2,0:T(8,128)(2,1)}, u32[]{:S(2)}) copy-start(bf16[4,128,192]{1,2,0:T(8,128)(2,1)} %param.15) | copy-start | bytes 589828
  22.0 32.0 %all-to-all-start = ((bf16[4,256,1024]{2,1,0:T(8,128)(2,1)}), bf16[4,256,1024]{2,1,0:T(8,128)(2,1)S(1)}, u32[]{:S(2)}, u32[]{:S(2)}) async-start(bf16[4,256,1024]{2,1,0:T(8,128)(2,1)} %broadcast_in_dim.3), calls=%async_computation | async-start | bytes 4194304 | tf_op jit(solution)/shard_map/all_to_all | solution.py:61
  29.6 7.1 %collective-permute-start.3 = (bf16[2,192,128]{2,1,0:T(8,128)(2,1)S(1)}, bf16[2,192,128]{2,1,0:T(8,128)(2,1)S(1)}, u32[]{:S(2)}, u32[]{:S(2)}) collective-permute-start(bf16[2,192,128]{2,1,0:T(8,128)(2,1)S(1)} %get-tuple-element.33), channel_id=1, source_target_pairs={{0,252},{4,0},{8,4},{12,8},{16,12},{20,16},{24,20},{28,24},{32,28}... | collective-permute-start | bytes 294920 | tf_op jit(solution)/shard_map/ppermute | solution.py:337
  30.5 7.6 %collective-permute-start.2 = (bf16[2,192,128]{2,1,0:T(8,128)(2,1)S(1)}, bf16[2,192,128]{2,1,0:T(8,128)(2,1)S(1)}, u32[]{:S(2)}, u32[]{:S(2)}) collective-permute-start(bf16[2,192,128]{2,1,0:T(8,128)(2,1)S(1)} %get-tuple-element.34), channel_id=1, source_target_pairs={{0,248},{4,252},{8,0},{12,4},{16,8},{20,12},{24,16},{28,20},{32,24... | collective-permute-start | bytes 294920 | tf_op jit(solution)/shard_map/ppermute | solution.py:337
  32.3 10.1 %collective-permute-start = (bf16[2,192,128]{2,1,0:T(8,128)(2,1)S(1)}, bf16[2,192,128]{2,1,0:T(8,128)(2,1)S(1)}, u32[]{:S(2)}, u32[]{:S(2)}) collective-permute-start(bf16[2,192,128]{2,1,0:T(8,128)(2,1)S(1)} %get-tuple-element.35), channel_id=1, source_target_pairs={{0,240},{4,244},{8,248},{12,252},{16,0},{20,4},{24,8},{28,12},{32,... | collective-permute-start | bytes 294920 | tf_op jit(solution)/shard_map/ppermute | solution.py:337
  32.6 13.5 %collective-permute-start.1 = (bf16[2,192,128]{2,1,0:T(8,128)(2,1)S(1)}, bf16[2,192,128]{2,1,0:T(8,128)(2,1)S(1)}, u32[]{:S(2)}, u32[]{:S(2)}) collective-permute-start(bf16[2,192,128]{2,1,0:T(8,128)(2,1)S(1)} %get-tuple-element.36), channel_id=1, source_target_pairs={{0,244},{4,248},{8,252},{12,0},{16,4},{20,8},{24,12},{28,16},{32,2... | collective-permute-start | bytes 294920 | tf_op jit(solution)/shard_map/ppermute | solution.py:337
  46.2 15.2 %copy-start.6 = (bf16[4,192,128]{2,1,0:T(8,128)(2,1)}, bf16[4,192,128]{2,1,0:T(8,128)(2,1)S(1)}, u32[]{:S(2)}) copy-start(bf16[4,192,128]{2,1,0:T(8,128)(2,1)S(1)} %pad_maximum_fusion.2.n0) | copy-start | bytes 589828
  46.2 15.2 %collective-permute-start.6 = (bf16[4,192,128]{2,1,0:T(8,128)(2,1)S(1)}, bf16[4,192,128]{2,1,0:T(8,128)(2,1)S(1)}, u32[]{:S(2)}, u32[]{:S(2)}) collective-permute-start(bf16[4,192,128]{2,1,0:T(8,128)(2,1)S(1)} %pad_maximum_fusion.2.n0), channel_id=1, source_target_pairs={{3,0},{0,1},{1,2},{2,3},{7,4},{4,5},{5,6},{6,7},{11,8},{8,9},{9,10... | collective-permute-start | bytes 589832 | tf_op jit(solution)/shard_map/ppermute | solution.py:48
  48.6 12.8 %collective-permute-start.5 = (bf16[4,192,128]{2,1,0:T(8,128)(2,1)S(1)}, bf16[4,192,128]{2,1,0:T(8,128)(2,1)S(1)}, u32[]{:S(2)}, u32[]{:S(2)}) collective-permute-start(bf16[4,192,128]{2,1,0:T(8,128)(2,1)S(1)} %pad_maximum_fusion.2.n0), channel_id=1, source_target_pairs={{2,0},{3,1},{0,2},{1,3},{6,4},{7,5},{4,6},{5,7},{10,8},{11,9},{8,1... | collective-permute-start | bytes 589832 | tf_op jit(solution)/shard_map/ppermute | solution.py:48
  51.2 10.3 %collective-permute-start.4 = (bf16[4,192,128]{2,1,0:T(8,128)(2,1)S(1)}, bf16[4,192,128]{2,1,0:T(8,128)(2,1)S(1)}, u32[]{:S(2)}, u32[]{:S(2)}) collective-permute-start(bf16[4,192,128]{2,1,0:T(8,128)(2,1)S(1)} %pad_maximum_fusion.2.n0), channel_id=1, source_target_pairs={{1,0},{2,1},{3,2},{0,3},{5,4},{6,5},{7,6},{4,7},{9,8},{10,9},{11,1... | collective-permute-start | bytes 589832 | tf_op jit(solution)/shard_map/ppermute | solution.py:48
  82.5 7.4 %collective-permute-start.10 = (bf16[8,4,64,1024]{3,2,1,0:T(8,128)(2,1)}, bf16[8,4,64,1024]{3,2,1,0:T(8,128)(2,1)S(1)}, u32[]{:S(2)}, u32[]{:S(2)}) collective-permute-start(bf16[8,4,64,1024]{3,2,1,0:T(8,128)(2,1)} %tied.1.own), channel_id=1, source_target_pairs={{0,4},{4,0},{1,5},{5,1},{2,6},{6,2},{3,7},{7,3},{8,12},{12,8},{9,1... | collective-permute-start | bytes 12582920 | tf_op jit(solution)/shard_map/ppermute | solution.py:376
  99.7 29.6 %all-to-all-start.1 = ((bf16[4,128,1024]{2,1,0:T(8,128)(2,1)}), bf16[4,128,1024]{2,1,0:T(8,128)(2,1)S(1)}, u32[]{:S(2)}, u32[]{:S(2)}) async-start(bf16[4,128,1024]{2,1,0:T(8,128)(2,1)} %get-tuple-element.15), calls=%async_computation.1 | async-start | bytes 2097152 | tf_op jit(solution)/shard_map/all_to_all | solution.py:61
  115.6 12.9 %collective-permute-start.11 = (bf16[4,192,128]{2,1,0:T(8,128)(2,1)}, bf16[4,192,128]{2,1,0:T(8,128)(2,1)S(1)}, u32[]{:S(2)}, u32[]{:S(2)}) collective-permute-start(bf16[4,192,128]{2,1,0:T(8,128)(2,1)} %get-tuple-element.22), channel_id=1, source_target_pairs={{0,1},{1,2},{2,3},{3,0},{4,5},{5,6},{6,7},{7,4},{8,9},{9,10},{10,1... | collective-permute-start | bytes 589832 | tf_op jit(solution)/shard_map/ppermute | solution.py:56
  117.7 11.5 %collective-permute-start.12 = (bf16[4,192,128]{2,1,0:T(8,128)(2,1)}, bf16[4,192,128]{2,1,0:T(8,128)(2,1)S(1)}, u32[]{:S(2)}, u32[]{:S(2)}) collective-permute-start(bf16[4,192,128]{2,1,0:T(8,128)(2,1)} %get-tuple-element.23), channel_id=1, source_target_pairs={{0,2},{1,3},{2,0},{3,1},{4,6},{5,7},{6,4},{7,5},{8,10},{9,11},{10,... | collective-permute-start | bytes 589832 | tf_op jit(solution)/shard_map/ppermute | solution.py:56
  120.4 8.8 %collective-permute-start.13 = (bf16[4,192,128]{2,1,0:T(8,128)(2,1)}, bf16[4,192,128]{2,1,0:T(8,128)(2,1)S(1)}, u32[]{:S(2)}, u32[]{:S(2)}) collective-permute-start(bf16[4,192,128]{2,1,0:T(8,128)(2,1)} %get-tuple-element.24), channel_id=1, source_target_pairs={{0,3},{1,0},{2,1},{3,2},{4,7},{5,4},{6,5},{7,6},{8,11},{9,8},{10,9... | collective-permute-start | bytes 589832 | tf_op jit(solution)/shard_map/ppermute | solution.py:56
  129.3 18.2 %all-to-all-start.2 = ((bf16[4,128,1024]{2,1,0:T(8,128)(2,1)}), bf16[4,128,1024]{2,1,0:T(8,128)(2,1)S(1)}, u32[]{:S(2)}, u32[]{:S(2)}) async-start(bf16[4,128,1024]{2,1,0:T(8,128)(2,1)} %hidden.1), calls=%async_computation.2 | async-start | bytes 2097152 | tf_op jit(solution)/shard_map/all_to_all | solution.py:61
  133.3 7.0 %collective-permute-start.17 = (bf16[2,192,128]{2,1,0:T(8,128)(2,1)S(1)}, bf16[2,192,128]{2,1,0:T(8,128)(2,1)S(1)}, u32[]{:S(2)}, u32[]{:S(2)}) collective-permute-start(bf16[2,192,128]{2,1,0:T(8,128)(2,1)S(1)} %get-tuple-element.29), channel_id=1, source_target_pairs={{0,4},{4,8},{8,12},{12,16},{16,20},{20,24},{24,28},{28,32},{32,36}... | collective-permute-start | bytes 294920 | tf_op jit(solution)/shard_map/ppermute | solution.py:337
  133.4 9.6 %collective-permute-start.16 = (bf16[2,192,128]{2,1,0:T(8,128)(2,1)S(1)}, bf16[2,192,128]{2,1,0:T(8,128)(2,1)S(1)}, u32[]{:S(2)}, u32[]{:S(2)}) collective-permute-start(bf16[2,192,128]{2,1,0:T(8,128)(2,1)S(1)} %get-tuple-element.30), channel_id=1, source_target_pairs={{0,8},{4,12},{8,16},{12,20},{16,24},{20,28},{24,32},{28,36},{32,40... | collective-permute-start | bytes 294920 | tf_op jit(solution)/shard_map/ppermute | solution.py:337
  133.5 9.8 %collective-permute-start.14 = (bf16[2,192,128]{2,1,0:T(8,128)(2,1)S(1)}, bf16[2,192,128]{2,1,0:T(8,128)(2,1)S(1)}, u32[]{:S(2)}, u32[]{:S(2)}) collective-permute-start(bf16[2,192,128]{2,1,0:T(8,128)(2,1)S(1)} %get-tuple-element.31), channel_id=1, source_target_pairs={{0,16},{4,20},{8,24},{12,28},{16,32},{20,36},{24,40},{28,44},{32,4... | collective-permute-start | bytes 294920 | tf_op jit(solution)/shard_map/ppermute | solution.py:337
  133.6 11.4 %collective-permute-start.15 = (bf16[2,192,128]{2,1,0:T(8,128)(2,1)S(1)}, bf16[2,192,128]{2,1,0:T(8,128)(2,1)S(1)}, u32[]{:S(2)}, u32[]{:S(2)}) collective-permute-start(bf16[2,192,128]{2,1,0:T(8,128)(2,1)S(1)} %get-tuple-element.32), channel_id=1, source_target_pairs={{0,12},{4,16},{8,20},{12,24},{16,28},{20,32},{24,36},{28,40},{32,4... | collective-permute-start | bytes 294920 | tf_op jit(solution)/shard_map/ppermute | solution.py:337
  (11 other events, 43.1 us)
Sparse Core Ops, SparseCore 0:
  19.3 63.0 all-gather.2
where the time goes:
time: 157 us; the launch traced here: 155 us
  Pallas kernels  41.1 us (26%)
  starting transfers between devices  41 us (26%)
  waiting for transfers between devices  40.3 us (26%)
  between operations  18.7 us (12%)
  local copies, waits for them, and re-layouts  7.9 us (5%)
  other arithmetic  6.22 us (4%)
    ppermute x8, waiting for transfers between devices, pairs_moved(): came = lax.ppermute(sent, DP, [(i, (i + sign * by) % n) for i in range(n)])  17.2 us
    all_to_all x3, starting transfers between devices, exchanged(): return lax.all_to_all(x, 'tensor', split_axis=0, concat_axis=0, tiled=True)  13 us
    pallas_call x1, Pallas kernels, backward_of(): pl.pallas_call(functools.partial(backward_kernel, 1.0 / math.sqrt(HEAD)),...  11.4 us
    pallas_call x1, Pallas kernels, forward_of(): pl.pallas_call(functools.partial(forward_kernel, 1.0 / math.sqrt(HEAD)),...  10.1 us
    all_gather x1, waiting for transfers between devices, gathered_plane(): return lax.all_gather(jnp.stack(along), 'z', axis=0)  9.56 us
    ppermute x8, starting transfers between devices, pairs_moved(): came = lax.ppermute(sent, DP, [(i, (i + sign * by) % n) for i in range(n)])  8.91 us
    ppermute x1, waiting for transfers between devices, shards(): other_plane = lax.ppermute(plane, 'core', [(0, 1), (1, 0)])  7.33 us
    pallas_call x1, Pallas kernels, output_of(): pl.pallas_call(output_kernel, out_shape=(jax.ShapeDtypeStruct((steps, row...  6.95 us
  transfers between devices with their start and end apart: 22, of which 14 were waited for; matrix products, arithmetic and copies ran while one was open for 4% of the time, Pallas kernels for 22%

commit v1 on v0

--- a/solution.py
+++ b/solution.py
@@ -181,61 +181,75 @@
     )(t, query, *pieces, key_weight, value_weight)
 
 
-def output_kernel(t_ref, a_ref, g_ref, own, other, o_ref, ga_ref, w_ref, sems):
-    core, x = t_ref[1], t_ref[2]
-    steps, _, width = g_ref.shape
-    chips = own.shape[1]
-    deep = own.shape[0] // steps
-    copies = []
-    for i in range(steps):
-        for s in range(chips):
-            at = (x - s + chips) % chips
-            for n, (plane, c) in enumerate(((own, core), (other, 1 - core))):
-                copies.append(
-                    pltpu.make_async_copy(
-                        plane.at[pl.ds(i * deep, deep), s], w_ref.at[i, :, at, c], sems.at[i, 2 * s + n]
+def output_kernel(steps, first, t_ref, a_ref, g_ref, *refs):
+    pieces = sum(len(firsts) for _, firsts in steps)
+    own, other, refs = refs[:pieces], refs[pieces : 2 * pieces], refs[2 * pieces :]
+    if not first:
+        o_before, ga_before, *refs = refs
+    o_ref, ga_ref, w_ref, sems = refs
+    core, x, z = t_ref[1], t_ref[2], t_ref[3]
+    chips, deep = w_ref.shape[1], 2 * g_ref.shape[0]
+    width = g_ref.shape[2] // 2
+    groups = []
+    n = 0
+    for i, (_, firsts) in enumerate(steps):
+        copies = []
+        for start in firsts:
+            for s in range(own[n].shape[0]):
+                at = (x - start - s + chips) % chips
+                for plane, c in ((own[n], core), (other[n], 1 - core)):
+                    copies.append(
+                        pltpu.make_async_copy(plane.at[s], w_ref.at[i, at, c], sems.at[i, len(copies)])
                     )
-                )
-    for copy in copies:
-        copy.start()
-    total = None
-    for i in range(steps):
-        for copy in copies[i * 2 * chips : (i + 1) * 2 * chips]:
+            n += 1
+        groups.append(copies)
+    for copies in groups:
+        for copy in copies:
+            copy.start()
+    total = None if first else ga_before[...]
+    if not first:
+        o_ref[...] = o_before[...]
+    for i, (step, _) in enumerate(steps):
+        for copy in groups[i]:
             copy.wait()
         w = w_ref[i].reshape(width, a_ref.shape[1])
-        part = dot(g_ref[i], w)
+        row = (z + step + deep) % deep
+        cols = pl.ds(pl.multiple_of((row % 2) * width, width), width)
+        part = dot(g_ref[row // 2, :, cols], w)
         total = part if total is None else total + part
-        o_ref[i] = dot(a_ref[...], w, NT).astype(BF16)
-    ga_ref[...] = total.astype(BF16)
-
-
-def output_of(t, attended, pieces, own, other):
+        o_ref[row // 2, :, cols] = dot(a_ref[...], w, NT).astype(BF16)
+    ga_ref[...] = total.astype(ga_ref.dtype)
+
+
+def output_of(t, attended, grads, steps, own, other, before=()):
     rows, cols = attended.shape
-    steps, _, width = pieces.shape
-    deep, chips = own.shape[0] // steps, own.shape[1]
-    return pl.pallas_call(
-        output_kernel,
-        out_shape=(
-            jax.ShapeDtypeStruct((steps, rows, width), BF16),
-            jax.ShapeDtypeStruct((rows, cols), BF16),
-        ),
+    groups, _, width = grads.shape
+    first = not before
+    chips = 4
+    out = (
+        jax.ShapeDtypeStruct((groups, rows, width), BF16),
+        jax.ShapeDtypeStruct((rows, cols), F32 if first else BF16),
+    )
+    return pl.pallas_call(
+        functools.partial(output_kernel, steps, first),
+        out_shape=out,
         grid=(1,),
         in_specs=[
             SMEM,
             whole((rows, cols)),
-            pl.BlockSpec((steps, rows, width), lambda i: (0, 1, 0)),
-            ANY,
-            ANY,
-        ],
-        out_specs=(whole((steps, rows, width)), whole((rows, cols))),
+            pl.BlockSpec((groups, rows, width), lambda i: (0, 1, 0)),
+        ]
+        + [ANY] * (len(own) + len(other))
+        + [whole(b.shape) for b in before],
+        out_specs=[whole(o.shape) for o in out],
         scratch_shapes=[
-            pltpu.VMEM((steps, deep, chips, 2, *own.shape[2:]), BF16),
-            pltpu.SemaphoreType.DMA((steps, 2 * chips)),
+            pltpu.VMEM((len(steps), chips, 2, *own[0].shape[1:]), BF16),
+            pltpu.SemaphoreType.DMA((len(steps), 2 * chips)),
         ],
         compiler_params=params(28),
-        cost_estimate=cost(4 * rows * steps * width * cols, 2 * steps * width * cols),
+        cost_estimate=cost(2 * rows * len(steps) * width * cols, len(steps) * width * cols),
         name="output",
-    )(t, attended, pieces, own, other)
+    )(t, attended, grads, *own, *other, *before)
 
 
 def backward_kernel(
@@ -339,12 +353,24 @@
     return jnp.concatenate(got, axis=0)
 
 
-def gathered_plane(rows):
-    n = lax.axis_size("x")
-    along = [rows]
-    for s in range(1, n):
-        along.append(lax.ppermute(rows, "x", [(i, (i + s) % n) for i in range(n)]))
-    return lax.all_gather(jnp.stack(along), "z", axis=0)
+def shifted(x, axis, by):
+    n = lax.axis_size(axis)
+    return lax.ppermute(x, axis, [(i, (i + by) % n) for i in range(n)])
+
+
+def swapped(x):
+    return lax.ppermute(x, "core", [(0, 1), (1, 0)])
+
+
+def plane_blocks(rows):
+    block = jnp.stack([rows] + [shifted(rows, "x", s) for s in range(1, lax.axis_size("x"))])
+    up, down = [block], [block]
+    for _ in range(lax.axis_size("z") // 2 - 1):
+        up.append(shifted(up[-1], "z", 1))
+        down.append(shifted(down[-1], "z", -1))
+    half = block.shape[0] // 2
+    far = shifted(up[-1][:half], "z", 1), shifted(down[-1][half:], "z", -1)
+    return up, down, far
 
 
 def shards(
@@ -359,8 +385,10 @@
     slot_target,
 ):
     n_dp = math.prod(lax.axis_size(a) for a in DP)
-    t = jnp.stack([lax.axis_index(a) for a in ("tensor", "core", "x")]).astype(jnp.int32)
-    plane = gathered_plane(out_weight.T)
+    t = jnp.stack([lax.axis_index(a) for a in ("tensor", "core", "x", "z")]).astype(jnp.int32)
+    up, down, far = plane_blocks(out_weight.T)
+    early = [up[0], up[1], down[1], up[2], down[2]]
+    late = [up[3], down[3], *far]
 
     gap = (block_owner[0] - lax.axis_index(DP) + n_dp) % n_dp
     gaps = (gap[0], gap[2])
@@ -372,14 +400,16 @@
 
     query = query_of(pieces, query_weight)
     key, value, probs, attended = forward_of(t, query, neighbours, key_weight, value_weight)
-    plane = tied(plane, attended)
-    other_plane = lax.ppermute(plane, "core", [(0, 1), (1, 0)])
-    out_parts, grad_attended = output_of(t, attended, pieces, plane, other_plane)
+    steps = [(0, [0]), (-1, [0]), (1, [0]), (-2, [0]), (2, [0])], [(-3, [0]), (3, [0]), (4, [0, 2])]
+    before = output_of(t, attended, pieces, steps[0], early, [swapped(b) for b in early])
+    out_parts, grad_attended = output_of(
+        t, attended, pieces, steps[1], late, [swapped(b) for b in late], before
+    )
     cross_out = summed(exchanged(out_parts))
     grad_query, *state_parts = backward_of(
         t, grad_attended, query, key, value, probs, key_weight, value_weight, mine.shape
     )
-    grad_hidden = summed(exchanged(hidden_of(grad_query, query_weight)))
+    grad_hidden = summed(exchanged(tied(hidden_of(grad_query, query_weight), cross_out)))
     grads = summed(to_peers(state_parts))
     grad_states = jnp.swapaxes(pairs_moved(grads, gaps, 1), 1, 2)
     return cross_out, grad_hidden, grad_states

time: 157 us -> 171 us (1.089)
  between operations: 18.7 us -> 5.61 us
  starting transfers between devices: 41 us -> 50.3 us
  Pallas kernels: 41.1 us -> 49.1 us
  local copies, waits for them, and re-layouts: 7.9 us -> 15.5 us
  waiting for transfers between devices: 40.3 us -> 42.1 us
    ppermute x4 -> x20, waiting for transfers between devices: 11.2 us -> 27.3 us  [the longest x11 27.3 us: shifted(): return lax.ppermute(x, axis, [(i, (i + by) % n) for i in range(n)])]
    ppermute x4 -> x20, starting transfers between devices: 6.38 us -> 20.3 us  [the longest x11 18.8 us: shifted(): return lax.ppermute(x, axis, [(i, (i + by) % n) for i in range(n)])]
    all_gather x1 -> x0, waiting for transfers between devices: 9.56 us -> none  [gathered_plane(): return lax.all_gather(jnp.stack(along), 'z', axis=0)]
    pallas_call x1 -> x2, Pallas kernels: 6.95 us -> 15 us  [output_of(): pl.pallas_call(functools.partial(output_kernel, steps, first), out_shape=...]
    unnamed x26 -> x52, local copies, waits for them, and re-layouts: 5.66 us -> 11 us
    ppermute x8, waiting for transfers between devices: 17.2 us -> 12.2 us  [pairs_moved(): came = lax.ppermute(sent, DP, [(i, (i + sign * by) % n) for i in range(n)])]
    ppermute x8, starting transfers between devices: 8.91 us -> 6.39 us  [pairs_moved(): came = lax.ppermute(sent, DP, [(i, (i + sign * by) % n) for i in range(n)])]
    slice x0 -> x2, local copies, waits for them, and re-layouts: none -> 2.39 us  [plane_blocks(): far = (shifted(up[-1][:half], 'z', 1), shifted(down[-1][half:], 'z', -1))]
  transfers between devices with their start and end apart: 22 -> 37, of which waited for: 14 -> 13; matrix products, arithmetic and copies ran while one was open for 4% -> 5% of each run, Pallas kernels for 22% -> 26%
where the time goes in v1:
time: 171 us; the launch traced here: 168 us
  starting transfers between devices  50.3 us (29%)
  Pallas kernels  49.1 us (29%)
  waiting for transfers between devices  42.1 us (25%)
  local copies, waits for them, and re-layouts  15.5 us (9%)
  between operations  5.61 us (3%)
  other arithmetic  5.31 us (3%)
    ppermute x11, waiting for transfers between devices, shifted(): return lax.ppermute(x, axis, [(i, (i + by) % n) for i in range(n)])  27.3 us
    ppermute x11, starting transfers between devices, shifted(): return lax.ppermute(x, axis, [(i, (i + by) % n) for i in range(n)])  18.8 us
    pallas_call x2, Pallas kernels, output_of(): pl.pallas_call(functools.partial(output_kernel, steps, first), out_shape=...  15 us
    all_to_all x3, starting transfers between devices, exchanged(): return lax.all_to_all(x, 'tensor', split_axis=0, concat_axis=0, tiled=True)  12.7 us
    ppermute x8, waiting for transfers between devices, pairs_moved(): came = lax.ppermute(sent, DP, [(i, (i + sign * by) % n) for i in range(n)])  12.2 us
    pallas_call x1, Pallas kernels, backward_of(): pl.pallas_call(functools.partial(backward_kernel, 1.0 / math.sqrt(HEAD)),...  11.4 us
    unnamed x52, local copies, waits for them, and re-layouts  11 us
    pallas_call x1, Pallas kernels, forward_of(): pl.pallas_call(functools.partial(forward_kernel, 1.0 / math.sqrt(HEAD)),...  10.2 us
  transfers between devices with their start and end apart: 37, of which 13 were waited for; matrix products, arithmetic and copies ran while one was open for 5% of the time, Pallas kernels for 26%

profile of v1, /device:TPU:96, one launch (start us, length us, event | category | flops | bytes accessed | tf_op | source)
XLA Modules:
  0.0 168.0 jit_solution(1939187252549768376)
XLA Ops:
  2.2 2.7 %collective-permute-start.8 = (bf16[64,1024]{1,0:T(8,128)(2,1)}, bf16[64,1024]{1,0:T(8,128)(2,1)S(1)}, u32[]{:S(2)}, u32[]{:S(2)}) collective-permute-start(bf16[64,1024]{1,0:T(8,128)(2,1)} %bitcast.28), channel_id=1, source_target_pairs={{0,16},{8,24},{16,0},{24,8},{1,17},{9,25},{17,1},{25,9},{2,18},{10... | collective-permute-start | bytes 393224 | tf_op jit(solution)/shard_map/ppermute | solution.py:358
  7.5 3.6 %collective-permute-done.8 = bf16[64,1024]{1,0:T(8,128)(2,1)S(1)} collective-permute-done((bf16[64,1024]{1,0:T(8,128)(2,1)}, bf16[64,1024]{1,0:T(8,128)(2,1)S(1)}, u32[]{:S(2)}, u32[]{:S(2)}) %collective-permute-start.8) | collective-permute-done | bytes 131104 | tf_op jit(solution)/shard_map/ppermute | solution.py:358
  12.1 3.2 %collective-permute-start.10 = (bf16[4,64,1024]{2,1,0:T(8,128)(2,1)S(1)}, bf16[4,64,1024]{2,1,0:T(8,128)(2,1)S(1)}, u32[]{:S(2)}, u32[]{:S(2)}) collective-permute-start(bf16[4,64,1024]{2,1,0:T(8,128)(2,1)S(1)} %pad_maximum_fusion.1.refs_0_), channel_id=1, source_target_pairs={{0,32},{32,64},{64,96},{96,128},{128,160},{160,192},{192,224},{224... | collective-permute-start | bytes 1572872 | tf_op jit(solution)/shard_map/ppermute | solution.py:358
  18.0 4.6 %all-to-all-start = ((bf16[4,256,1024]{2,1,0:T(8,128)(2,1)}), bf16[4,256,1024]{2,1,0:T(8,128)(2,1)S(1)}, u32[]{:S(2)}, u32[]{:S(2)}) async-start(bf16[4,256,1024]{2,1,0:T(8,128)(2,1)} %broadcast_in_dim.3), calls=%async_computation | async-start | bytes 4194304 | tf_op jit(solution)/shard_map/all_to_all | solution.py:61
  22.6 3.0 %collective-permute-done.10.refs_1_ = bf16[4,64,1024]{2,1,0:T(8,128)(2,1)S(1)} collective-permute-done((bf16[4,64,1024]{2,1,0:T(8,128)(2,1)S(1)}, bf16[4,64,1024]{2,1,0:T(8,128)(2,1)S(1)}, u32[]{:S(2)}, u32[]{:S(2)}) %collective-permute-start.10) | collective-permute-done | bytes 524320 | tf_op jit(solution)/shard_map/ppermute | solution.py:358
  25.7 3.7 %collective-permute-start.11 = (bf16[4,64,1024]{2,1,0:T(8,128)(2,1)S(1)}, bf16[4,64,1024]{2,1,0:T(8,128)(2,1)S(1)}, u32[]{:S(2)}, u32[]{:S(2)}) collective-permute-start(bf16[4,64,1024]{2,1,0:T(8,128)(2,1)S(1)} %collective-permute-done.10.refs_1_), channel_id=1, source_target_pairs={{0,32},{32,64},{64,96},{96,128},{128,160},{160,192},{192,224},{224... | collective-permute-start | bytes 1572872 | tf_op jit(solution)/shard_map/ppermute | solution.py:358
  34.6 4.2 %collective-permute-done = bf16[2,192,128]{2,1,0:T(8,128)(2,1)S(1)} collective-permute-done((bf16[2,192,128]{2,1,0:T(8,128)(2,1)S(1)}, bf16[2,192,128]{2,1,0:T(8,128)(2,1)S(1)}, u32[]{:S(2)}, u32[]{:S(2)}) %collective-permute-start) | collective-permute-done | bytes 98336 | tf_op jit(solution)/shard_map/ppermute | solution.py:351
  40.9 4.1 %collective-permute-start.12 = (bf16[4,64,1024]{2,1,0:T(8,128)(2,1)S(1)}, bf16[4,64,1024]{2,1,0:T(8,128)(2,1)S(1)}, u32[]{:S(2)}, u32[]{:S(2)}) collective-permute-start(bf16[4,64,1024]{2,1,0:T(8,128)(2,1)S(1)} %collective-permute-done.11.refs_3_), channel_id=1, source_target_pairs={{0,32},{32,64},{64,96},{96,128},{128,160},{160,192},{192,224},{224... | collective-permute-start | bytes 1572872 | tf_op jit(solution)/shard_map/ppermute | solution.py:358
  45.1 3.0 %collective-permute-start.4 = (bf16[4,192,128]{2,1,0:T(8,128)(2,1)S(1)}, bf16[4,192,128]{2,1,0:T(8,128)(2,1)}, u32[]{:S(2)}, u32[]{:S(2)}) collective-permute-start(bf16[4,192,128]{2,1,0:T(8,128)(2,1)S(1)} %pad_maximum_fusion.2.n0), channel_id=1, source_target_pairs={{1,0},{2,1},{3,2},{0,3},{5,4},{6,5},{7,6},{4,7},{9,8},{10,9},{11,1... | collective-permute-start | bytes 589832 | tf_op jit(solution)/shard_map/ppermute | solution.py:48
  49.8 7.5 %collective-permute-done.14.refs_4_ = bf16[4,64,1024]{2,1,0:T(8,128)(2,1)} collective-permute-done((bf16[4,64,1024]{2,1,0:T(8,128)(2,1)S(1)}, bf16[4,64,1024]{2,1,0:T(8,128)(2,1)}, u32[]{:S(2)}, u32[]{:S(2)}) %collective-permute-start.14) | collective-permute-done | bytes 524320 | tf_op jit(solution)/shard_map/ppermute | solution.py:358
  60.1 11.9 %collective-permute-done.15.refs_1_ = bf16[4,64,1024]{2,1,0:T(8,128)(2,1)} collective-permute-done((bf16[4,64,1024]{2,1,0:T(8,128)(2,1)}, bf16[4,64,1024]{2,1,0:T(8,128)(2,1)}, u32[]{:S(2)}, u32[]{:S(2)}) %collective-permute-start.15) | collective-permute-done | bytes 524320 | tf_op jit(solution)/shard_map/ppermute | solution.py:358
  76.1 2.0 %collective-permute-start.17 = (bf16[2,64,1024]{2,1,0:T(8,128)(2,1)}, bf16[2,64,1024]{2,1,0:T(8,128)(2,1)}, u32[]{:S(2)}, u32[]{:S(2)}) collective-permute-start(bf16[2,64,1024]{2,1,0:T(8,128)(2,1)} %slice.51), channel_id=1, source_target_pairs={{0,224},{32,0},{64,32},{96,64},{128,96},{160,128},{192,160},{224,1... | collective-permute-start | bytes 786440 | tf_op jit(solution)/shard_map/ppermute | solution.py:358
  82.1 5.9 %query.1.q_ref = bf16[128,1024]{1,0:T(8,128)(2,1)} custom-call(bf16[4,256,1024]{2,1,0:T(8,128)(2,1)} %copy-done, bf16[4096,1024]{1,0:T(8,128)(2,1)} %w_ref.3), custom_call_target="tpu_custom_call" | custom-call | flops 1073741824 | bytes 8388608 | tf_op jit(solution)/shard_map/query/pallas_call | solution.py:106
  88.7 10.2 %forward.1 = (bf16[512,1024]{1,0:T(8,128)(2,1)}, bf16[512,1024]{1,0:T(8,128)(2,1)}, f32[8,2,64,256]{3,2,1,0:T(8,128)}, bf16[128,1024]{1,0:T(8,128)(2,1)}) custom-call(s32[4]{0:T(128)} %pad_add_fusion.t_ref, bf16[128,1024]{1,0:T(8,128)(2,1)} %query.1.q_ref, bf16[4,192,128]{2,1,0:T(8,128)(2,1)} %copy-done.21, bf16[4,192,128]{2,1,0:T(8,128)(2,1)} %collective-permute-done.4.n1, ...), custom_call_target="tpu_custom_call" | custom-call | flops 1610612736 | bytes 10000000 | tf_op jit(solution)/shard_map/forward/pallas_call | solution.py:158
  103.0 9.6 %output.2 = (bf16[4,128,1024]{2,1,0:T(8,128)(2,1)S(1)}, f32[128,1024]{1,0:T(8,128)S(1)}) custom-call(s32[4]{0:T(128)S(1)} %copy-done.20, bf16[128,1024]{1,0:T(8,128)(2,1)S(1)} %copy-done.2, bf16[4,256,1024]{2,1,0:T(8,128)(2,1)S(1)} %copy-done.1, bf16[4,64,1024]{2,1,0:T(8,128)(2,1)S(1)} %pad_maximum_fusion.1.refs_0_, bf16[4,64,1024]{2,1,0:T(8,128)(2,1)S(1)} %copy-done.4, ...), custom_call_target="tpu_custom_call" | custom-call | flops 1342177280 | bytes 5242880 | tf_op jit(solution)/shard_map/output/pallas_call | solution.py:233
  114.3 5.4 %output.3 = (bf16[4,128,1024]{2,1,0:T(8,128)(2,1)}, bf16[128,1024]{1,0:T(8,128)(2,1)S(1)}) custom-call(s32[4]{0:T(128)S(1)} %copy-done.20, bf16[128,1024]{1,0:T(8,128)(2,1)S(1)} %copy-done.2, bf16[4,256,1024]{2,1,0:T(8,128)(2,1)S(1)} %copy-done.1, bf16[4,64,1024]{2,1,0:T(8,128)(2,1)S(1)} %collective-permute-done.12.refs_0_, ...), custom_call_target="tpu_custom_call" | custom-call | flops 805306368 | bytes 3145728 | tf_op jit(solution)/shard_map/output/pallas_call | solution.py:233
  119.7 4.4 %all-to-all-start.1 = ((bf16[4,128,1024]{2,1,0:T(8,128)(2,1)}), bf16[4,128,1024]{2,1,0:T(8,128)(2,1)S(1)}, u32[]{:S(2)}, u32[]{:S(2)}) async-start(bf16[4,128,1024]{2,1,0:T(8,128)(2,1)} %get-tuple-element.19), calls=%async_computation.1 | async-start | bytes 2097152 | tf_op jit(solution)/shard_map/all_to_all | solution.py:61
  124.2 11.4 %backward.1 = (bf16[128,1024]{1,0:T(8,128)(2,1)}, bf16[4,192,128]{2,1,0:T(8,128)(2,1)}, bf16[4,192,128]{2,1,0:T(8,128)(2,1)}, bf16[4,192,128]{2,1,0:T(8,128)(2,1)}, bf16[4,192,128]{2,1,0:T(8,128)(2,1)}) custom-call(s32[4]{0:T(128)} %pad_add_fusion.t_ref, bf16[128,1024]{1,0:T(8,128)(2,1)} %copy-done.19, bf16[128,1024]{1,0:T(8,128)(2,1)} %query.1.q_ref, ...), custom_call_target="tpu_custom_call" | custom-call | flops 1610612736 | bytes 10000000 | tf_op jit(solution)/shard_map/backward/pallas_call | solution.py:298
  135.6 2.1 %collective-permute-start.27 = (bf16[4,192,128]{2,1,0:T(8,128)(2,1)}, bf16[4,192,128]{2,1,0:T(8,128)(2,1)S(1)}, u32[]{:S(2)}, u32[]{:S(2)}) collective-permute-start(bf16[4,192,128]{2,1,0:T(8,128)(2,1)} %get-tuple-element.26), channel_id=1, source_target_pairs={{0,1},{1,2},{2,3},{3,0},{4,5},{5,6},{6,7},{7,4},{8,9},{9,10},{10,1... | collective-permute-start | bytes 589832 | tf_op jit(solution)/shard_map/ppermute | solution.py:56
  137.7 2.7 %collective-permute-start.28 = (bf16[4,192,128]{2,1,0:T(8,128)(2,1)}, bf16[4,192,128]{2,1,0:T(8,128)(2,1)S(1)}, u32[]{:S(2)}, u32[]{:S(2)}) collective-permute-start(bf16[4,192,128]{2,1,0:T(8,128)(2,1)} %get-tuple-element.27), channel_id=1, source_target_pairs={{0,2},{1,3},{2,0},{3,1},{4,6},{5,7},{6,4},{7,5},{8,10},{9,11},{10,... | collective-permute-start | bytes 589832 | tf_op jit(solution)/shard_map/ppermute | solution.py:56
  141.8 6.6 %hidden.1.__0_ = bf16[4,128,1024]{2,1,0:T(8,128)(2,1)} custom-call(bf16[128,1024]{1,0:T(8,128)(2,1)} %get-tuple-element.24.g_ref, bf16[4096,1024]{1,0:T(8,128)(2,1)} %w_ref.3), custom_call_target="tpu_custom_call" | custom-call | flops 1073741824 | bytes 8388608 | tf_op jit(solution)/shard_map/hidden/pallas_call | solution.py:333
  149.3 3.6 %all-to-all-start.2 = ((bf16[4,128,1024]{2,1,0:T(8,128)(2,1)}), bf16[4,128,1024]{2,1,0:T(8,128)(2,1)S(1)}, u32[]{:S(2)}, u32[]{:S(2)}) async-start(bf16[4,128,1024]{2,1,0:T(8,128)(2,1)} %tied.1), calls=%async_computation.2 | async-start | bytes 2097152 | tf_op jit(solution)/shard_map/all_to_all | solution.py:61
  157.5 3.9 %collective-permute-done.30 = bf16[2,192,128]{2,1,0:T(8,128)(2,1)S(1)} collective-permute-done((bf16[2,192,128]{2,1,0:T(8,128)(2,1)S(1)}, bf16[2,192,128]{2,1,0:T(8,128)(2,1)S(1)}, u32[]{:S(2)}, u32[]{:S(2)}) %collective-permute-start.30) | collective-permute-done | bytes 98336 | tf_op jit(solution)/shard_map/ppermute | solution.py:351
  163.5 2.1 %collective-permute-done.33 = bf16[2,192,128]{2,1,0:T(8,128)(2,1)S(1)} collective-permute-done((bf16[2,192,128]{2,1,0:T(8,128)(2,1)S(1)}, bf16[2,192,128]{2,1,0:T(8,128)(2,1)S(1)}, u32[]{:S(2)}, u32[]{:S(2)}) %collective-permute-start.33) | collective-permute-done | bytes 98336 | tf_op jit(solution)/shard_map/ppermute | solution.py:351
  (126 shorter events, 40.8 us)
Async XLA Ops:
  12.1 13.5 %collective-permute-start.10 = (bf16[4,64,1024]{2,1,0:T(8,128)(2,1)S(1)}, bf16[4,64,1024]{2,1,0:T(8,128)(2,1)S(1)}, u32[]{:S(2)}, u32[]{:S(2)}) collective-permute-start(bf16[4,64,1024]{2,1,0:T(8,128)(2,1)S(1)} %pad_maximum_fusion.1.refs_0_), channel_id=1, source_target_pairs={{0,32},{32,64},{64,96},{96,128},{128,160},{160,192},{192,224},{224... | collective-permute-start | bytes 1572872 | tf_op jit(solution)/shard_map/ppermute | solution.py:358
  18.0 62.8 %all-to-all-start = ((bf16[4,256,1024]{2,1,0:T(8,128)(2,1)}), bf16[4,256,1024]{2,1,0:T(8,128)(2,1)S(1)}, u32[]{:S(2)}, u32[]{:S(2)}) async-start(bf16[4,256,1024]{2,1,0:T(8,128)(2,1)} %broadcast_in_dim.3), calls=%async_computation | async-start | bytes 4194304 | tf_op jit(solution)/shard_map/all_to_all | solution.py:61
  22.6 16.2 %collective-permute-start.13 = (bf16[4,64,1024]{2,1,0:T(8,128)(2,1)S(1)}, bf16[4,64,1024]{2,1,0:T(8,128)(2,1)S(1)}, u32[]{:S(2)}, u32[]{:S(2)}) collective-permute-start(bf16[4,64,1024]{2,1,0:T(8,128)(2,1)S(1)} %pad_maximum_fusion.1.refs_0_), channel_id=1, source_target_pairs={{0,224},{32,0},{64,32},{96,64},{128,96},{160,128},{192,160},{224,1... | collective-permute-start | bytes 1572872 | tf_op jit(solution)/shard_map/ppermute | solution.py:358
  25.7 15.2 %collective-permute-start.11 = (bf16[4,64,1024]{2,1,0:T(8,128)(2,1)S(1)}, bf16[4,64,1024]{2,1,0:T(8,128)(2,1)S(1)}, u32[]{:S(2)}, u32[]{:S(2)}) collective-permute-start(bf16[4,64,1024]{2,1,0:T(8,128)(2,1)S(1)} %collective-permute-done.10.refs_1_), channel_id=1, source_target_pairs={{0,32},{32,64},{64,96},{96,128},{128,160},{160,192},{192,224},{224... | collective-permute-start | bytes 1572872 | tf_op jit(solution)/shard_map/ppermute | solution.py:358
  32.7 12.3 %collective-permute-start.1 = (bf16[2,192,128]{2,1,0:T(8,128)(2,1)S(1)}, bf16[2,192,128]{2,1,0:T(8,128)(2,1)S(1)}, u32[]{:S(2)}, u32[]{:S(2)}) collective-permute-start(bf16[2,192,128]{2,1,0:T(8,128)(2,1)S(1)} %get-tuple-element.40), channel_id=1, source_target_pairs={{0,244},{4,248},{8,252},{12,0},{16,4},{20,8},{24,12},{28,16},{32,2... | collective-permute-start | bytes 294920 | tf_op jit(solution)/shard_map/ppermute | solution.py:351
  38.8 18.6 %collective-permute-start.14 = (bf16[4,64,1024]{2,1,0:T(8,128)(2,1)S(1)}, bf16[4,64,1024]{2,1,0:T(8,128)(2,1)}, u32[]{:S(2)}, u32[]{:S(2)}) collective-permute-start(bf16[4,64,1024]{2,1,0:T(8,128)(2,1)S(1)} %collective-permute-done.13.refs_2_), channel_id=1, source_target_pairs={{0,224},{32,0},{64,32},{96,64},{128,96},{160,128},{192,160},{224,1... | collective-permute-start | bytes 1572872 | tf_op jit(solution)/shard_map/ppermute | solution.py:358
  40.9 18.6 %collective-permute-start.12 = (bf16[4,64,1024]{2,1,0:T(8,128)(2,1)S(1)}, bf16[4,64,1024]{2,1,0:T(8,128)(2,1)S(1)}, u32[]{:S(2)}, u32[]{:S(2)}) collective-permute-start(bf16[4,64,1024]{2,1,0:T(8,128)(2,1)S(1)} %collective-permute-done.11.refs_3_), channel_id=1, source_target_pairs={{0,32},{32,64},{64,96},{96,128},{128,160},{160,192},{192,224},{224... | collective-permute-start | bytes 1572872 | tf_op jit(solution)/shard_map/ppermute | solution.py:358
  45.1 12.3 %collective-permute-start.4 = (bf16[4,192,128]{2,1,0:T(8,128)(2,1)S(1)}, bf16[4,192,128]{2,1,0:T(8,128)(2,1)}, u32[]{:S(2)}, u32[]{:S(2)}) collective-permute-start(bf16[4,192,128]{2,1,0:T(8,128)(2,1)S(1)} %pad_maximum_fusion.2.n0), channel_id=1, source_target_pairs={{1,0},{2,1},{3,2},{0,3},{5,4},{6,5},{7,6},{4,7},{9,8},{10,9},{11,1... | collective-permute-start | bytes 589832 | tf_op jit(solution)/shard_map/ppermute | solution.py:48
  57.3 14.7 %collective-permute-start.15 = (bf16[4,64,1024]{2,1,0:T(8,128)(2,1)}, bf16[4,64,1024]{2,1,0:T(8,128)(2,1)}, u32[]{:S(2)}, u32[]{:S(2)}) collective-permute-start(bf16[4,64,1024]{2,1,0:T(8,128)(2,1)} %collective-permute-done.14.refs_4_), channel_id=1, source_target_pairs={{0,224},{32,0},{64,32},{96,64},{128,96},{160,128},{192,160},{224,1... | collective-permute-start | bytes 1572872 | tf_op jit(solution)/shard_map/ppermute | solution.py:358
  57.4 17.1 %collective-permute-start.22 = (bf16[4,64,1024]{2,1,0:T(8,128)(2,1)S(1)}, bf16[4,64,1024]{2,1,0:T(8,128)(2,1)S(1)}, u32[]{:S(2)}, u32[]{:S(2)}) collective-permute-start(bf16[4,64,1024]{2,1,0:T(8,128)(2,1)S(1)} %pad_maximum_fusion.1.refs_0_), channel_id=1, source_target_pairs={{0,4},{4,0},{1,5},{5,1},{2,6},{6,2},{3,7},{7,3},{8,12},{12,8},{9,1... | collective-permute-start | bytes 1572872 | tf_op jit(solution)/shard_map/ppermute | solution.py:362
  57.5 17.8 %collective-permute-start.23 = (bf16[4,64,1024]{2,1,0:T(8,128)(2,1)}, bf16[4,64,1024]{2,1,0:T(8,128)(2,1)S(1)}, u32[]{:S(2)}, u32[]{:S(2)}) collective-permute-start(bf16[4,64,1024]{2,1,0:T(8,128)(2,1)} %copy-done.3), channel_id=1, source_target_pairs={{0,4},{4,0},{1,5},{5,1},{2,6},{6,2},{3,7},{7,3},{8,12},{12,8},{9,1... | collective-permute-start | bytes 1572872 | tf_op jit(solution)/shard_map/ppermute | solution.py:362
  59.5 18.6 %collective-permute-start.24 = (bf16[4,64,1024]{2,1,0:T(8,128)(2,1)S(1)}, bf16[4,64,1024]{2,1,0:T(8,128)(2,1)S(1)}, u32[]{:S(2)}, u32[]{:S(2)}) collective-permute-start(bf16[4,64,1024]{2,1,0:T(8,128)(2,1)S(1)} %collective-permute-done.13.refs_2_), channel_id=1, source_target_pairs={{0,4},{4,0},{1,5},{5,1},{2,6},{6,2},{3,7},{7,3},{8,12},{12,8},{9,1... | collective-permute-start | bytes 1572872 | tf_op jit(solution)/shard_map/ppermute | solution.py:362
  60.1 18.8 %collective-permute-start.25 = (bf16[4,64,1024]{2,1,0:T(8,128)(2,1)S(1)}, bf16[4,64,1024]{2,1,0:T(8,128)(2,1)S(1)}, u32[]{:S(2)}, u32[]{:S(2)}) collective-permute-start(bf16[4,64,1024]{2,1,0:T(8,128)(2,1)S(1)} %collective-permute-done.11.refs_3_), channel_id=1, source_target_pairs={{0,4},{4,0},{1,5},{5,1},{2,6},{6,2},{3,7},{7,3},{8,12},{12,8},{9,1... | collective-permute-start | bytes 1572872 | tf_op jit(solution)/shard_map/ppermute | solution.py:362
  72.1 26.8 %collective-permute-start.26 = (bf16[4,64,1024]{2,1,0:T(8,128)(2,1)}, bf16[4,64,1024]{2,1,0:T(8,128)(2,1)}, u32[]{:S(2)}, u32[]{:S(2)}) collective-permute-start(bf16[4,64,1024]{2,1,0:T(8,128)(2,1)} %collective-permute-done.14.refs_4_), channel_id=1, source_target_pairs={{0,4},{4,0},{1,5},{5,1},{2,6},{6,2},{3,7},{7,3},{8,12},{12,8},{9,1... | collective-permute-start | bytes 1572872 | tf_op jit(solution)/shard_map/ppermute | solution.py:362
  75.3 12.8 %collective-permute-start.16 = (bf16[2,64,1024]{2,1,0:T(8,128)(2,1)}, bf16[2,64,1024]{2,1,0:T(8,128)(2,1)S(1)}, u32[]{:S(2)}, u32[]{:S(2)}) collective-permute-start(bf16[2,64,1024]{2,1,0:T(8,128)(2,1)} %slice.50), channel_id=1, source_target_pairs={{0,32},{32,64},{64,96},{96,128},{128,160},{160,192},{192,224},{224... | collective-permute-start | bytes 786440 | tf_op jit(solution)/shard_map/ppermute | solution.py:358
  78.9 34.4 %collective-permute-start.18 = (bf16[4,64,1024]{2,1,0:T(8,128)(2,1)S(1)}, bf16[4,64,1024]{2,1,0:T(8,128)(2,1)}, u32[]{:S(2)}, u32[]{:S(2)}) collective-permute-start(bf16[4,64,1024]{2,1,0:T(8,128)(2,1)S(1)} %collective-permute-done.12.refs_0_), channel_id=1, source_target_pairs={{0,4},{4,0},{1,5},{5,1},{2,6},{6,2},{3,7},{7,3},{8,12},{12,8},{9,1... | collective-permute-start | bytes 1572872 | tf_op jit(solution)/shard_map/ppermute | solution.py:362
  79.7 33.6 %collective-permute-start.19 = (bf16[4,64,1024]{2,1,0:T(8,128)(2,1)}, bf16[4,64,1024]{2,1,0:T(8,128)(2,1)}, u32[]{:S(2)}, u32[]{:S(2)}) collective-permute-start(bf16[4,64,1024]{2,1,0:T(8,128)(2,1)} %collective-permute-done.15.refs_1_), channel_id=1, source_target_pairs={{0,4},{4,0},{1,5},{5,1},{2,6},{6,2},{3,7},{7,3},{8,12},{12,8},{9,1... | collective-permute-start | bytes 1572872 | tf_op jit(solution)/shard_map/ppermute | solution.py:362
  88.1 24.5 %collective-permute-start.20 = (bf16[2,64,1024]{2,1,0:T(8,128)(2,1)S(1)}, bf16[2,64,1024]{2,1,0:T(8,128)(2,1)S(1)}, u32[]{:S(2)}, u32[]{:S(2)}) collective-permute-start(bf16[2,64,1024]{2,1,0:T(8,128)(2,1)S(1)} %collective-permute-done.16.refs_2_), channel_id=1, source_target_pairs={{0,4},{4,0},{1,5},{5,1},{2,6},{6,2},{3,7},{7,3},{8,12},{12,8},{9,1... | collective-permute-start | bytes 786440 | tf_op jit(solution)/shard_map/ppermute | solution.py:362
  88.2 25.1 %collective-permute-start.21 = (bf16[2,64,1024]{2,1,0:T(8,128)(2,1)}, bf16[2,64,1024]{2,1,0:T(8,128)(2,1)}, u32[]{:S(2)}, u32[]{:S(2)}) collective-permute-start(bf16[2,64,1024]{2,1,0:T(8,128)(2,1)} %collective-permute-done.17.refs_3_), channel_id=1, source_target_pairs={{0,4},{4,0},{1,5},{5,1},{2,6},{6,2},{3,7},{7,3},{8,12},{12,8},{9,1... | collective-permute-start | bytes 786440 | tf_op jit(solution)/shard_map/ppermute | solution.py:362
  119.7 28.7 %all-to-all-start.1 = ((bf16[4,128,1024]{2,1,0:T(8,128)(2,1)}), bf16[4,128,1024]{2,1,0:T(8,128)(2,1)S(1)}, u32[]{:S(2)}, u32[]{:S(2)}) async-start(bf16[4,128,1024]{2,1,0:T(8,128)(2,1)} %get-tuple-element.19), calls=%async_computation.1 | async-start | bytes 2097152 | tf_op jit(solution)/shard_map/all_to_all | solution.py:61
  135.6 17.4 %collective-permute-start.27 = (bf16[4,192,128]{2,1,0:T(8,128)(2,1)}, bf16[4,192,128]{2,1,0:T(8,128)(2,1)S(1)}, u32[]{:S(2)}, u32[]{:S(2)}) collective-permute-start(bf16[4,192,128]{2,1,0:T(8,128)(2,1)} %get-tuple-element.26), channel_id=1, source_target_pairs={{0,1},{1,2},{2,3},{3,0},{4,5},{5,6},{6,7},{7,4},{8,9},{9,10},{10,1... | collective-permute-start | bytes 589832 | tf_op jit(solution)/shard_map/ppermute | solution.py:56
  137.7 15.3 %collective-permute-start.28 = (bf16[4,192,128]{2,1,0:T(8,128)(2,1)}, bf16[4,192,128]{2,1,0:T(8,128)(2,1)S(1)}, u32[]{:S(2)}, u32[]{:S(2)}) collective-permute-start(bf16[4,192,128]{2,1,0:T(8,128)(2,1)} %get-tuple-element.27), channel_id=1, source_target_pairs={{0,2},{1,3},{2,0},{3,1},{4,6},{5,7},{6,4},{7,5},{8,10},{9,11},{10,... | collective-permute-start | bytes 589832 | tf_op jit(solution)/shard_map/ppermute | solution.py:56
  140.3 12.6 %collective-permute-start.29 = (bf16[4,192,128]{2,1,0:T(8,128)(2,1)}, bf16[4,192,128]{2,1,0:T(8,128)(2,1)S(1)}, u32[]{:S(2)}, u32[]{:S(2)}) collective-permute-start(bf16[4,192,128]{2,1,0:T(8,128)(2,1)} %get-tuple-element.28), channel_id=1, source_target_pairs={{0,3},{1,0},{2,1},{3,2},{4,7},{5,4},{6,5},{7,6},{8,11},{9,8},{10,9... | collective-permute-start | bytes 589832 | tf_op jit(solution)/shard_map/ppermute | solution.py:56
  149.3 17.9 %all-to-all-start.2 = ((bf16[4,128,1024]{2,1,0:T(8,128)(2,1)}), bf16[4,128,1024]{2,1,0:T(8,128)(2,1)S(1)}, u32[]{:S(2)}, u32[]{:S(2)}) async-start(bf16[4,128,1024]{2,1,0:T(8,128)(2,1)} %tied.1), calls=%async_computation.2 | async-start | bytes 2097152 | tf_op jit(solution)/shard_map/all_to_all | solution.py:61
  (39 other events, 321.2 us)

commit v2 on v1

--- a/solution.py
+++ b/solution.py
@@ -79,6 +79,7 @@
         in_specs=[ANY] * (1 + len(after)),
         out_specs=ANY,
         input_output_aliases={0: 0},
+        compiler_params=params(1),
         name="tied",
     )(x, *after)
 
@@ -368,9 +369,12 @@
     for _ in range(lax.axis_size("z") // 2 - 1):
         up.append(shifted(up[-1], "z", 1))
         down.append(shifted(down[-1], "z", -1))
-    half = block.shape[0] // 2
-    far = shifted(up[-1][:half], "z", 1), shifted(down[-1][half:], "z", -1)
-    return up, down, far
+    return up, down
+
+
+def far_pieces(up, down, *after):
+    half = up.shape[0] // 2
+    return shifted(tied(up[:half], *after), "z", 1), shifted(tied(down[half:], *after), "z", -1)
 
 
 def shards(
@@ -386,9 +390,8 @@
 ):
     n_dp = math.prod(lax.axis_size(a) for a in DP)
     t = jnp.stack([lax.axis_index(a) for a in ("tensor", "core", "x", "z")]).astype(jnp.int32)
-    up, down, far = plane_blocks(out_weight.T)
+    up, down = plane_blocks(out_weight.T)
     early = [up[0], up[1], down[1], up[2], down[2]]
-    late = [up[3], down[3], *far]
 
     gap = (block_owner[0] - lax.axis_index(DP) + n_dp) % n_dp
     gaps = (gap[0], gap[2])
@@ -400,6 +403,7 @@
 
     query = query_of(pieces, query_weight)
     key, value, probs, attended = forward_of(t, query, neighbours, key_weight, value_weight)
+    late = [up[3], down[3], *far_pieces(up[3], down[3], attended)]
     steps = [(0, [0]), (-1, [0]), (1, [0]), (-2, [0]), (2, [0])], [(-3, [0]), (3, [0]), (4, [0, 2])]
     before = output_of(t, attended, pieces, steps[0], early, [swapped(b) for b in early])
     out_parts, grad_attended = output_of(

time: 171 us -> 169 us (0.988)
  local copies, waits for them, and re-layouts: 15.5 us -> 11.2 us
  waiting for transfers between devices: 42.1 us -> 44.6 us
  starting transfers between devices: 50.3 us -> 52.1 us
    ppermute x11, waiting for transfers between devices: 27.3 us -> 20.9 us  [shifted(): return lax.ppermute(x, axis, [(i, (i + by) % n) for i in range(n)])]
    ppermute x3, waiting for transfers between devices: 1.73 us -> 7.16 us  [from_peers(): got.append(lax.ppermute(x, 'tensor', [((i + r) % n, i) for i in range(n)]))]
    ppermute x8, waiting for transfers between devices: 12.2 us -> 16.5 us  [pairs_moved(): came = lax.ppermute(sent, DP, [(i, (i + sign * by) % n) for i in range(n)])]
    unnamed x52 -> x38, local copies, waits for them, and re-layouts: 11 us -> 7.96 us
  transfers between devices with their start and end apart: 37 -> 37, of which waited for: 13 -> 17; matrix products, arithmetic and copies ran while one was open for 5% -> 4% of each run, Pallas kernels for 26% -> 24%
where the time goes in v2:
time: 169 us; the launch traced here: 166 us
  starting transfers between devices  52.1 us (31%)
  Pallas kernels  47.8 us (28%)
  waiting for transfers between devices  44.6 us (26%)
  local copies, waits for them, and re-layouts  11.2 us (7%)
  between operations  5.43 us (3%)
  other arithmetic  4.7 us (3%)
    ppermute x11, waiting for transfers between devices, shifted(): return lax.ppermute(x, axis, [(i, (i + by) % n) for i in range(n)])  20.9 us
    ppermute x11, starting transfers between devices, shifted(): return lax.ppermute(x, axis, [(i, (i + by) % n) for i in range(n)])  19.5 us
    ppermute x8, waiting for transfers between devices, pairs_moved(): came = lax.ppermute(sent, DP, [(i, (i + sign * by) % n) for i in range(n)])  16.5 us
    pallas_call x2, Pallas kernels, output_of(): pl.pallas_call(functools.partial(output_kernel, steps, first), out_shape=...  13.6 us
    all_to_all x3, starting transfers between devices, exchanged(): return lax.all_to_all(x, 'tensor', split_axis=0, concat_axis=0, tiled=True)  11.8 us
    pallas_call x1, Pallas kernels, backward_of(): pl.pallas_call(functools.partial(backward_kernel, 1.0 / math.sqrt(HEAD)),...  11.4 us
    pallas_call x1, Pallas kernels, forward_of(): pl.pallas_call(functools.partial(forward_kernel, 1.0 / math.sqrt(HEAD)),...  10.2 us
    unnamed x38, local copies, waits for them, and re-layouts  7.96 us
  transfers between devices with their start and end apart: 37, of which 17 were waited for; matrix products, arithmetic and copies ran while one was open for 4% of the time, Pallas kernels for 24%

profile of v2, /device:TPU:96, one launch (start us, length us, event | category | flops | bytes accessed | tf_op | source)
XLA Modules:
  0.0 165.7 jit_solution(15296176533064261737)
XLA Ops:
  2.2 2.7 %collective-permute-start.8 = (bf16[64,1024]{1,0:T(8,128)(2,1)}, bf16[64,1024]{1,0:T(8,128)(2,1)S(1)}, u32[]{:S(2)}, u32[]{:S(2)}) collective-permute-start(bf16[64,1024]{1,0:T(8,128)(2,1)} %bitcast.28), channel_id=1, source_target_pairs={{0,16},{8,24},{16,0},{24,8},{1,17},{9,25},{17,1},{25,9},{2,18},{10... | collective-permute-start | bytes 393224 | tf_op jit(solution)/shard_map/ppermute | solution.py:359
  7.5 3.6 %collective-permute-done.8 = bf16[64,1024]{1,0:T(8,128)(2,1)S(1)} collective-permute-done((bf16[64,1024]{1,0:T(8,128)(2,1)}, bf16[64,1024]{1,0:T(8,128)(2,1)S(1)}, u32[]{:S(2)}, u32[]{:S(2)}) %collective-permute-start.8) | collective-permute-done | bytes 131104 | tf_op jit(solution)/shard_map/ppermute | solution.py:359
  12.1 3.2 %collective-permute-start.10 = (bf16[4,64,1024]{2,1,0:T(8,128)(2,1)S(1)}, bf16[4,64,1024]{2,1,0:T(8,128)(2,1)S(1)}, u32[]{:S(2)}, u32[]{:S(2)}) collective-permute-start(bf16[4,64,1024]{2,1,0:T(8,128)(2,1)S(1)} %pad_maximum_fusion.1.refs_0_), channel_id=1, source_target_pairs={{0,32},{32,64},{64,96},{96,128},{128,160},{160,192},{192,224},{224... | collective-permute-start | bytes 1572872 | tf_op jit(solution)/shard_map/ppermute | solution.py:359
  18.0 4.6 %all-to-all-start = ((bf16[4,256,1024]{2,1,0:T(8,128)(2,1)}), bf16[4,256,1024]{2,1,0:T(8,128)(2,1)S(1)}, u32[]{:S(2)}, u32[]{:S(2)}) async-start(bf16[4,256,1024]{2,1,0:T(8,128)(2,1)} %broadcast_in_dim.3), calls=%async_computation | async-start | bytes 4194304 | tf_op jit(solution)/shard_map/all_to_all | solution.py:61
  22.7 3.0 %collective-permute-done.10.refs_1_ = bf16[4,64,1024]{2,1,0:T(8,128)(2,1)S(1)} collective-permute-done((bf16[4,64,1024]{2,1,0:T(8,128)(2,1)S(1)}, bf16[4,64,1024]{2,1,0:T(8,128)(2,1)S(1)}, u32[]{:S(2)}, u32[]{:S(2)}) %collective-permute-start.10) | collective-permute-done | bytes 524320 | tf_op jit(solution)/shard_map/ppermute | solution.py:359
  25.7 3.7 %collective-permute-start.11 = (bf16[4,64,1024]{2,1,0:T(8,128)(2,1)S(1)}, bf16[4,64,1024]{2,1,0:T(8,128)(2,1)}, u32[]{:S(2)}, u32[]{:S(2)}) collective-permute-start(bf16[4,64,1024]{2,1,0:T(8,128)(2,1)S(1)} %collective-permute-done.10.refs_1_), channel_id=1, source_target_pairs={{0,32},{32,64},{64,96},{96,128},{128,160},{160,192},{192,224},{224... | collective-permute-start | bytes 1572872 | tf_op jit(solution)/shard_map/ppermute | solution.py:359
  32.6 4.5 %collective-permute-done.13.refs_2_ = bf16[4,64,1024]{2,1,0:T(8,128)(2,1)} collective-permute-done((bf16[4,64,1024]{2,1,0:T(8,128)(2,1)S(1)}, bf16[4,64,1024]{2,1,0:T(8,128)(2,1)}, u32[]{:S(2)}, u32[]{:S(2)}) %collective-permute-start.13) | collective-permute-done | bytes 524320 | tf_op jit(solution)/shard_map/ppermute | solution.py:359
  41.3 3.6 %collective-permute-start.12 = (bf16[4,64,1024]{2,1,0:T(8,128)(2,1)}, bf16[4,64,1024]{2,1,0:T(8,128)(2,1)S(1)}, u32[]{:S(2)}, u32[]{:S(2)}) collective-permute-start(bf16[4,64,1024]{2,1,0:T(8,128)(2,1)} %collective-permute-done.11.refs_3_), channel_id=1, source_target_pairs={{0,32},{32,64},{64,96},{96,128},{128,160},{160,192},{192,224},{224... | collective-permute-start | bytes 1572872 | tf_op jit(solution)/shard_map/ppermute | solution.py:359
  44.9 4.3 %collective-permute-done.1 = bf16[2,192,128]{2,1,0:T(8,128)(2,1)S(1)} collective-permute-done((bf16[2,192,128]{2,1,0:T(8,128)(2,1)S(1)}, bf16[2,192,128]{2,1,0:T(8,128)(2,1)S(1)}, u32[]{:S(2)}, u32[]{:S(2)}) %collective-permute-start.1) | collective-permute-done | bytes 98336 | tf_op jit(solution)/shard_map/ppermute | solution.py:352
  51.3 3.7 %collective-permute-start.4 = (bf16[4,192,128]{2,1,0:T(8,128)(2,1)S(1)}, bf16[4,192,128]{2,1,0:T(8,128)(2,1)S(1)}, u32[]{:S(2)}, u32[]{:S(2)}) collective-permute-start(bf16[4,192,128]{2,1,0:T(8,128)(2,1)S(1)} %pad_maximum_fusion.2.n0), channel_id=1, source_target_pairs={{1,0},{2,1},{3,2},{0,3},{5,4},{6,5},{7,6},{4,7},{9,8},{10,9},{11,1... | collective-permute-start | bytes 589832 | tf_op jit(solution)/shard_map/ppermute | solution.py:48
  57.2 3.2 %collective-permute-done.4.n1 = bf16[4,192,128]{2,1,0:T(8,128)(2,1)S(1)} collective-permute-done((bf16[4,192,128]{2,1,0:T(8,128)(2,1)S(1)}, bf16[4,192,128]{2,1,0:T(8,128)(2,1)S(1)}, u32[]{:S(2)}, u32[]{:S(2)}) %collective-permute-start.4) | collective-permute-done | bytes 196640 | tf_op jit(solution)/shard_map/ppermute | solution.py:48
  67.0 5.9 %query.1.q_ref = bf16[128,1024]{1,0:T(8,128)(2,1)} custom-call(bf16[4,256,1024]{2,1,0:T(8,128)(2,1)} %copy-done, bf16[4096,1024]{1,0:T(8,128)(2,1)} %w_ref.3), custom_call_target="tpu_custom_call" | custom-call | flops 1073741824 | bytes 8388608 | tf_op jit(solution)/shard_map/query/pallas_call | solution.py:107
  73.5 10.2 %forward.1 = (bf16[512,1024]{1,0:T(8,128)(2,1)}, bf16[512,1024]{1,0:T(8,128)(2,1)}, f32[8,2,64,256]{3,2,1,0:T(8,128)}, bf16[128,1024]{1,0:T(8,128)(2,1)}) custom-call(s32[4]{0:T(128)} %pad_add_fusion.t_ref, bf16[128,1024]{1,0:T(8,128)(2,1)} %query.1.q_ref, bf16[4,192,128]{2,1,0:T(8,128)(2,1)} %copy-done.12, bf16[4,192,128]{2,1,0:T(8,128)(2,1)} %copy-done.15, ...), custom_call_target="tpu_custom_call" | custom-call | flops 1610612736 | bytes 10000000 | tf_op jit(solution)/shard_map/forward/pallas_call | solution.py:159
  86.7 3.2 %collective-permute-start.16 = (bf16[2,64,1024]{2,1,0:T(8,128)(2,1)S(1)}, bf16[2,64,1024]{2,1,0:T(8,128)(2,1)S(1)}, u32[]{:S(2)}, u32[]{:S(2)}) collective-permute-start(bf16[2,64,1024]{2,1,0:T(8,128)(2,1)S(1)} %tied.3), channel_id=1, source_target_pairs={{0,32},{32,64},{64,96},{96,128},{128,160},{160,192},{192,224},{224... | collective-permute-start | bytes 786440 | tf_op jit(solution)/shard_map/ppermute | solution.py:359
  90.6 5.2 %collective-permute-done.16.refs_2_ = bf16[2,64,1024]{2,1,0:T(8,128)(2,1)S(1)} collective-permute-done((bf16[2,64,1024]{2,1,0:T(8,128)(2,1)S(1)}, bf16[2,64,1024]{2,1,0:T(8,128)(2,1)S(1)}, u32[]{:S(2)}, u32[]{:S(2)}) %collective-permute-start.16) | collective-permute-done | bytes 262176 | tf_op jit(solution)/shard_map/ppermute | solution.py:359
  95.7 3.4 %collective-permute-done.17.refs_3_ = bf16[2,64,1024]{2,1,0:T(8,128)(2,1)S(1)} collective-permute-done((bf16[2,64,1024]{2,1,0:T(8,128)(2,1)S(1)}, bf16[2,64,1024]{2,1,0:T(8,128)(2,1)S(1)}, u32[]{:S(2)}, u32[]{:S(2)}) %collective-permute-start.17) | collective-permute-done | bytes 262176 | tf_op jit(solution)/shard_map/ppermute | solution.py:359
  100.1 6.4 %output.2 = (bf16[4,128,1024]{2,1,0:T(8,128)(2,1)S(1)}, f32[128,1024]{1,0:T(8,128)S(1)}) custom-call(s32[4]{0:T(128)S(1)} %copy-done.11, bf16[128,1024]{1,0:T(8,128)(2,1)S(1)} %copy-done.6, bf16[4,256,1024]{2,1,0:T(8,128)(2,1)S(1)} %copy-done.1, bf16[4,64,1024]{2,1,0:T(8,128)(2,1)S(1)} %pad_maximum_fusion.1.refs_0_, bf16[4,64,1024]{2,1,0:T(8,128)(2,1)S(1)} %copy-done.9, ...), custom_call_target="tpu_custom_call" | custom-call | flops 1342177280 | bytes 5242880 | tf_op jit(solution)/shard_map/output/pallas_call | solution.py:234
  106.6 7.2 %output.3 = (bf16[4,128,1024]{2,1,0:T(8,128)(2,1)}, bf16[128,1024]{1,0:T(8,128)(2,1)S(1)}) custom-call(s32[4]{0:T(128)S(1)} %copy-done.11, bf16[128,1024]{1,0:T(8,128)(2,1)S(1)} %copy-done.6, bf16[4,256,1024]{2,1,0:T(8,128)(2,1)S(1)} %copy-done.1, bf16[4,64,1024]{2,1,0:T(8,128)(2,1)S(1)} %collective-permute-done.12.refs_0_, ...), custom_call_target="tpu_custom_call" | custom-call | flops 805306368 | bytes 3145728 | tf_op jit(solution)/shard_map/output/pallas_call | solution.py:234
  114.5 3.7 %all-to-all-start.1 = ((bf16[4,128,1024]{2,1,0:T(8,128)(2,1)}), bf16[4,128,1024]{2,1,0:T(8,128)(2,1)S(1)}, u32[]{:S(2)}, u32[]{:S(2)}) async-start(bf16[4,128,1024]{2,1,0:T(8,128)(2,1)} %get-tuple-element.19), calls=%async_computation.1 | async-start | bytes 2097152 | tf_op jit(solution)/shard_map/all_to_all | solution.py:61
  118.3 11.4 %backward.1 = (bf16[128,1024]{1,0:T(8,128)(2,1)}, bf16[4,192,128]{2,1,0:T(8,128)(2,1)}, bf16[4,192,128]{2,1,0:T(8,128)(2,1)}, bf16[4,192,128]{2,1,0:T(8,128)(2,1)}, bf16[4,192,128]{2,1,0:T(8,128)(2,1)}) custom-call(s32[4]{0:T(128)} %pad_add_fusion.t_ref, bf16[128,1024]{1,0:T(8,128)(2,1)} %copy-done.10, bf16[128,1024]{1,0:T(8,128)(2,1)} %query.1.q_ref, ...), custom_call_target="tpu_custom_call" | custom-call | flops 1610612736 | bytes 10000000 | tf_op jit(solution)/shard_map/backward/pallas_call | solution.py:299
  135.6 6.6 %hidden.1.__0_ = bf16[4,128,1024]{2,1,0:T(8,128)(2,1)} custom-call(bf16[128,1024]{1,0:T(8,128)(2,1)} %get-tuple-element.24.g_ref, bf16[4096,1024]{1,0:T(8,128)(2,1)} %w_ref.3), custom_call_target="tpu_custom_call" | custom-call | flops 1073741824 | bytes 8388608 | tf_op jit(solution)/shard_map/hidden/pallas_call | solution.py:334
  144.7 3.5 %all-to-all-start.2 = ((bf16[4,128,1024]{2,1,0:T(8,128)(2,1)}), bf16[4,128,1024]{2,1,0:T(8,128)(2,1)S(1)}, u32[]{:S(2)}, u32[]{:S(2)}) async-start(bf16[4,128,1024]{2,1,0:T(8,128)(2,1)} %copy-done.3), calls=%async_computation.2 | async-start | bytes 2097152 | tf_op jit(solution)/shard_map/all_to_all | solution.py:61
  148.5 5.7 %collective-permute-start.31 = (bf16[2,192,128]{2,1,0:T(8,128)(2,1)S(1)}, bf16[2,192,128]{2,1,0:T(8,128)(2,1)S(1)}, u32[]{:S(2)}, u32[]{:S(2)}) collective-permute-start(bf16[2,192,128]{2,1,0:T(8,128)(2,1)S(1)} %get-tuple-element.36), channel_id=1, source_target_pairs={{0,12},{4,16},{8,20},{12,24},{16,28},{20,32},{24,36},{28,40},{32,4... | collective-permute-start | bytes 294920 | tf_op jit(solution)/shard_map/ppermute | solution.py:352
  156.9 4.9 %collective-permute-done.32 = bf16[2,192,128]{2,1,0:T(8,128)(2,1)S(1)} collective-permute-done((bf16[2,192,128]{2,1,0:T(8,128)(2,1)S(1)}, bf16[2,192,128]{2,1,0:T(8,128)(2,1)S(1)}, u32[]{:S(2)}, u32[]{:S(2)}) %collective-permute-start.32) | collective-permute-done | bytes 98336 | tf_op jit(solution)/shard_map/ppermute | solution.py:352
  (114 shorter events, 42.6 us)
Async XLA Ops:
  12.1 13.5 %collective-permute-start.10 = (bf16[4,64,1024]{2,1,0:T(8,128)(2,1)S(1)}, bf16[4,64,1024]{2,1,0:T(8,128)(2,1)S(1)}, u32[]{:S(2)}, u32[]{:S(2)}) collective-permute-start(bf16[4,64,1024]{2,1,0:T(8,128)(2,1)S(1)} %pad_maximum_fusion.1.refs_0_), channel_id=1, source_target_pairs={{0,32},{32,64},{64,96},{96,128},{128,160},{160,192},{192,224},{224... | collective-permute-start | bytes 1572872 | tf_op jit(solution)/shard_map/ppermute | solution.py:359
  18.0 47.6 %all-to-all-start = ((bf16[4,256,1024]{2,1,0:T(8,128)(2,1)}), bf16[4,256,1024]{2,1,0:T(8,128)(2,1)S(1)}, u32[]{:S(2)}, u32[]{:S(2)}) async-start(bf16[4,256,1024]{2,1,0:T(8,128)(2,1)} %broadcast_in_dim.3), calls=%async_computation | async-start | bytes 4194304 | tf_op jit(solution)/shard_map/all_to_all | solution.py:61
  22.6 14.5 %collective-permute-start.13 = (bf16[4,64,1024]{2,1,0:T(8,128)(2,1)S(1)}, bf16[4,64,1024]{2,1,0:T(8,128)(2,1)}, u32[]{:S(2)}, u32[]{:S(2)}) collective-permute-start(bf16[4,64,1024]{2,1,0:T(8,128)(2,1)S(1)} %pad_maximum_fusion.1.refs_0_), channel_id=1, source_target_pairs={{0,224},{32,0},{64,32},{96,64},{128,96},{160,128},{192,160},{224,1... | collective-permute-start | bytes 1572872 | tf_op jit(solution)/shard_map/ppermute | solution.py:359
  25.7 15.6 %collective-permute-start.11 = (bf16[4,64,1024]{2,1,0:T(8,128)(2,1)S(1)}, bf16[4,64,1024]{2,1,0:T(8,128)(2,1)}, u32[]{:S(2)}, u32[]{:S(2)}) collective-permute-start(bf16[4,64,1024]{2,1,0:T(8,128)(2,1)S(1)} %collective-permute-done.10.refs_1_), channel_id=1, source_target_pairs={{0,32},{32,64},{64,96},{96,128},{128,160},{160,192},{192,224},{224... | collective-permute-start | bytes 1572872 | tf_op jit(solution)/shard_map/ppermute | solution.py:359
  37.1 20.1 %collective-permute-start.14 = (bf16[4,64,1024]{2,1,0:T(8,128)(2,1)}, bf16[4,64,1024]{2,1,0:T(8,128)(2,1)}, u32[]{:S(2)}, u32[]{:S(2)}) collective-permute-start(bf16[4,64,1024]{2,1,0:T(8,128)(2,1)} %collective-permute-done.13.refs_2_), channel_id=1, source_target_pairs={{0,224},{32,0},{64,32},{96,64},{128,96},{160,128},{192,160},{224,1... | collective-permute-start | bytes 1572872 | tf_op jit(solution)/shard_map/ppermute | solution.py:359
  37.1 12.1 %collective-permute-start.1 = (bf16[2,192,128]{2,1,0:T(8,128)(2,1)S(1)}, bf16[2,192,128]{2,1,0:T(8,128)(2,1)S(1)}, u32[]{:S(2)}, u32[]{:S(2)}) collective-permute-start(bf16[2,192,128]{2,1,0:T(8,128)(2,1)S(1)} %get-tuple-element.40), channel_id=1, source_target_pairs={{0,244},{4,248},{8,252},{12,0},{16,4},{20,8},{24,12},{28,16},{32,2... | collective-permute-start | bytes 294920 | tf_op jit(solution)/shard_map/ppermute | solution.py:352
  37.1 13.1 %collective-permute-start.2 = (bf16[2,192,128]{2,1,0:T(8,128)(2,1)S(1)}, bf16[2,192,128]{2,1,0:T(8,128)(2,1)S(1)}, u32[]{:S(2)}, u32[]{:S(2)}) collective-permute-start(bf16[2,192,128]{2,1,0:T(8,128)(2,1)S(1)} %get-tuple-element.38), channel_id=1, source_target_pairs={{0,248},{4,252},{8,0},{12,4},{16,8},{20,12},{24,16},{28,20},{32,24... | collective-permute-start | bytes 294920 | tf_op jit(solution)/shard_map/ppermute | solution.py:352
  38.7 12.6 %collective-permute-start.3 = (bf16[2,192,128]{2,1,0:T(8,128)(2,1)S(1)}, bf16[2,192,128]{2,1,0:T(8,128)(2,1)S(1)}, u32[]{:S(2)}, u32[]{:S(2)}) collective-permute-start(bf16[2,192,128]{2,1,0:T(8,128)(2,1)S(1)} %get-tuple-element.37), channel_id=1, source_target_pairs={{0,252},{4,0},{8,4},{12,8},{16,12},{20,16},{24,20},{28,24},{32,28}... | collective-permute-start | bytes 294920 | tf_op jit(solution)/shard_map/ppermute | solution.py:352
  41.3 23.1 %collective-permute-start.12 = (bf16[4,64,1024]{2,1,0:T(8,128)(2,1)}, bf16[4,64,1024]{2,1,0:T(8,128)(2,1)S(1)}, u32[]{:S(2)}, u32[]{:S(2)}) collective-permute-start(bf16[4,64,1024]{2,1,0:T(8,128)(2,1)} %collective-permute-done.11.refs_3_), channel_id=1, source_target_pairs={{0,32},{32,64},{64,96},{96,128},{128,160},{160,192},{192,224},{224... | collective-permute-start | bytes 1572872 | tf_op jit(solution)/shard_map/ppermute | solution.py:359
  57.2 15.8 %collective-permute-start.15 = (bf16[4,64,1024]{2,1,0:T(8,128)(2,1)}, bf16[4,64,1024]{2,1,0:T(8,128)(2,1)}, u32[]{:S(2)}, u32[]{:S(2)}) collective-permute-start(bf16[4,64,1024]{2,1,0:T(8,128)(2,1)} %collective-permute-done.14.refs_4_), channel_id=1, source_target_pairs={{0,224},{32,0},{64,32},{96,64},{128,96},{160,128},{192,160},{224,1... | collective-permute-start | bytes 1572872 | tf_op jit(solution)/shard_map/ppermute | solution.py:359
  60.4 26.4 %collective-permute-start.22 = (bf16[4,64,1024]{2,1,0:T(8,128)(2,1)S(1)}, bf16[4,64,1024]{2,1,0:T(8,128)(2,1)}, u32[]{:S(2)}, u32[]{:S(2)}) collective-permute-start(bf16[4,64,1024]{2,1,0:T(8,128)(2,1)S(1)} %pad_maximum_fusion.1.refs_0_), channel_id=1, source_target_pairs={{0,4},{4,0},{1,5},{5,1},{2,6},{6,2},{3,7},{7,3},{8,12},{12,8},{9,1... | collective-permute-start | bytes 1572872 | tf_op jit(solution)/shard_map/ppermute | solution.py:363
  62.3 27.6 %collective-permute-start.23 = (bf16[4,64,1024]{2,1,0:T(8,128)(2,1)}, bf16[4,64,1024]{2,1,0:T(8,128)(2,1)}, u32[]{:S(2)}, u32[]{:S(2)}) collective-permute-start(bf16[4,64,1024]{2,1,0:T(8,128)(2,1)} %copy-done.8), channel_id=1, source_target_pairs={{0,4},{4,0},{1,5},{5,1},{2,6},{6,2},{3,7},{7,3},{8,12},{12,8},{9,1... | collective-permute-start | bytes 1572872 | tf_op jit(solution)/shard_map/ppermute | solution.py:363
  64.3 25.6 %collective-permute-start.24 = (bf16[4,64,1024]{2,1,0:T(8,128)(2,1)}, bf16[4,64,1024]{2,1,0:T(8,128)(2,1)}, u32[]{:S(2)}, u32[]{:S(2)}) collective-permute-start(bf16[4,64,1024]{2,1,0:T(8,128)(2,1)} %collective-permute-done.13.refs_2_), channel_id=1, source_target_pairs={{0,4},{4,0},{1,5},{5,1},{2,6},{6,2},{3,7},{7,3},{8,12},{12,8},{9,1... | collective-permute-start | bytes 1572872 | tf_op jit(solution)/shard_map/ppermute | solution.py:363
  65.0 25.1 %collective-permute-start.25 = (bf16[4,64,1024]{2,1,0:T(8,128)(2,1)}, bf16[4,64,1024]{2,1,0:T(8,128)(2,1)}, u32[]{:S(2)}, u32[]{:S(2)}) collective-permute-start(bf16[4,64,1024]{2,1,0:T(8,128)(2,1)} %collective-permute-done.11.refs_3_), channel_id=1, source_target_pairs={{0,4},{4,0},{1,5},{5,1},{2,6},{6,2},{3,7},{7,3},{8,12},{12,8},{9,1... | collective-permute-start | bytes 1572872 | tf_op jit(solution)/shard_map/ppermute | solution.py:363
  73.0 26.2 %collective-permute-start.26 = (bf16[4,64,1024]{2,1,0:T(8,128)(2,1)}, bf16[4,64,1024]{2,1,0:T(8,128)(2,1)S(1)}, u32[]{:S(2)}, u32[]{:S(2)}) collective-permute-start(bf16[4,64,1024]{2,1,0:T(8,128)(2,1)} %collective-permute-done.14.refs_4_), channel_id=1, source_target_pairs={{0,4},{4,0},{1,5},{5,1},{2,6},{6,2},{3,7},{7,3},{8,12},{12,8},{9,1... | collective-permute-start | bytes 1572872 | tf_op jit(solution)/shard_map/ppermute | solution.py:363
  90.0 9.2 %collective-permute-start.17 = (bf16[2,64,1024]{2,1,0:T(8,128)(2,1)S(1)}, bf16[2,64,1024]{2,1,0:T(8,128)(2,1)S(1)}, u32[]{:S(2)}, u32[]{:S(2)}) collective-permute-start(bf16[2,64,1024]{2,1,0:T(8,128)(2,1)S(1)} %tied.4), channel_id=1, source_target_pairs={{0,224},{32,0},{64,32},{96,64},{128,96},{160,128},{192,160},{224,1... | collective-permute-start | bytes 786440 | tf_op jit(solution)/shard_map/ppermute | solution.py:359
  90.0 16.6 %collective-permute-start.18 = (bf16[4,64,1024]{2,1,0:T(8,128)(2,1)S(1)}, bf16[4,64,1024]{2,1,0:T(8,128)(2,1)S(1)}, u32[]{:S(2)}, u32[]{:S(2)}) collective-permute-start(bf16[4,64,1024]{2,1,0:T(8,128)(2,1)S(1)} %collective-permute-done.12.refs_0_), channel_id=1, source_target_pairs={{0,4},{4,0},{1,5},{5,1},{2,6},{6,2},{3,7},{7,3},{8,12},{12,8},{9,1... | collective-permute-start | bytes 1572872 | tf_op jit(solution)/shard_map/ppermute | solution.py:363
  90.1 16.5 %collective-permute-start.19 = (bf16[4,64,1024]{2,1,0:T(8,128)(2,1)}, bf16[4,64,1024]{2,1,0:T(8,128)(2,1)S(1)}, u32[]{:S(2)}, u32[]{:S(2)}) collective-permute-start(bf16[4,64,1024]{2,1,0:T(8,128)(2,1)} %collective-permute-done.15.refs_1_), channel_id=1, source_target_pairs={{0,4},{4,0},{1,5},{5,1},{2,6},{6,2},{3,7},{7,3},{8,12},{12,8},{9,1... | collective-permute-start | bytes 1572872 | tf_op jit(solution)/shard_map/ppermute | solution.py:363
  95.7 10.8 %collective-permute-start.20 = (bf16[2,64,1024]{2,1,0:T(8,128)(2,1)S(1)}, bf16[2,64,1024]{2,1,0:T(8,128)(2,1)S(1)}, u32[]{:S(2)}, u32[]{:S(2)}) collective-permute-start(bf16[2,64,1024]{2,1,0:T(8,128)(2,1)S(1)} %collective-permute-done.16.refs_2_), channel_id=1, source_target_pairs={{0,4},{4,0},{1,5},{5,1},{2,6},{6,2},{3,7},{7,3},{8,12},{12,8},{9,1... | collective-permute-start | bytes 786440 | tf_op jit(solution)/shard_map/ppermute | solution.py:363
  114.5 27.7 %all-to-all-start.1 = ((bf16[4,128,1024]{2,1,0:T(8,128)(2,1)}), bf16[4,128,1024]{2,1,0:T(8,128)(2,1)S(1)}, u32[]{:S(2)}, u32[]{:S(2)}) async-start(bf16[4,128,1024]{2,1,0:T(8,128)(2,1)} %get-tuple-element.19), calls=%async_computation.1 | async-start | bytes 2097152 | tf_op jit(solution)/shard_map/all_to_all | solution.py:61
  129.6 18.6 %collective-permute-start.27 = (bf16[4,192,128]{2,1,0:T(8,128)(2,1)}, bf16[4,192,128]{2,1,0:T(8,128)(2,1)S(1)}, u32[]{:S(2)}, u32[]{:S(2)}) collective-permute-start(bf16[4,192,128]{2,1,0:T(8,128)(2,1)} %get-tuple-element.26), channel_id=1, source_target_pairs={{0,1},{1,2},{2,3},{3,0},{4,5},{5,6},{6,7},{7,4},{8,9},{9,10},{10,1... | collective-permute-start | bytes 589832 | tf_op jit(solution)/shard_map/ppermute | solution.py:56
  131.5 16.8 %collective-permute-start.28 = (bf16[4,192,128]{2,1,0:T(8,128)(2,1)}, bf16[4,192,128]{2,1,0:T(8,128)(2,1)S(1)}, u32[]{:S(2)}, u32[]{:S(2)}) collective-permute-start(bf16[4,192,128]{2,1,0:T(8,128)(2,1)} %get-tuple-element.27), channel_id=1, source_target_pairs={{0,2},{1,3},{2,0},{3,1},{4,6},{5,7},{6,4},{7,5},{8,10},{9,11},{10,... | collective-permute-start | bytes 589832 | tf_op jit(solution)/shard_map/ppermute | solution.py:56
  134.2 14.1 %collective-permute-start.29 = (bf16[4,192,128]{2,1,0:T(8,128)(2,1)}, bf16[4,192,128]{2,1,0:T(8,128)(2,1)S(1)}, u32[]{:S(2)}, u32[]{:S(2)}) collective-permute-start(bf16[4,192,128]{2,1,0:T(8,128)(2,1)} %get-tuple-element.28), channel_id=1, source_target_pairs={{0,3},{1,0},{2,1},{3,2},{4,7},{5,4},{6,5},{7,6},{8,11},{9,8},{10,9... | collective-permute-start | bytes 589832 | tf_op jit(solution)/shard_map/ppermute | solution.py:56
  144.7 20.1 %all-to-all-start.2 = ((bf16[4,128,1024]{2,1,0:T(8,128)(2,1)}), bf16[4,128,1024]{2,1,0:T(8,128)(2,1)S(1)}, u32[]{:S(2)}, u32[]{:S(2)}) async-start(bf16[4,128,1024]{2,1,0:T(8,128)(2,1)} %copy-done.3), calls=%async_computation.2 | async-start | bytes 2097152 | tf_op jit(solution)/shard_map/all_to_all | solution.py:61
  (32 other events, 254.1 us)

commit v3 on v0

--- a/solution.py
+++ b/solution.py
@@ -181,61 +181,71 @@
     )(t, query, *pieces, key_weight, value_weight)
 
 
-def output_kernel(t_ref, a_ref, g_ref, own, other, o_ref, ga_ref, w_ref, sems):
-    core, x = t_ref[1], t_ref[2]
-    steps, _, width = g_ref.shape
-    chips = own.shape[1]
-    deep = own.shape[0] // steps
-    copies = []
-    for i in range(steps):
-        for s in range(chips):
-            at = (x - s + chips) % chips
-            for n, (plane, c) in enumerate(((own, core), (other, 1 - core))):
-                copies.append(
-                    pltpu.make_async_copy(
-                        plane.at[pl.ds(i * deep, deep), s], w_ref.at[i, :, at, c], sems.at[i, 2 * s + n]
-                    )
-                )
-    for copy in copies:
-        copy.start()
-    total = None
-    for i in range(steps):
-        for copy in copies[i * 2 * chips : (i + 1) * 2 * chips]:
-            copy.wait()
-        w = w_ref[i].reshape(width, a_ref.shape[1])
-        part = dot(g_ref[i], w)
-        total = part if total is None else total + part
-        o_ref[i] = dot(a_ref[...], w, NT).astype(BF16)
-    ga_ref[...] = total.astype(BF16)
-
-
-def output_of(t, attended, pieces, own, other):
+def output_kernel(first, t_ref, a_ref, g_ref, w_ref, *refs):
+    if not first:
+        o_before, ga_before, *refs = refs
+    o_ref, ga_ref, pick, acc = refs
+    i, last = pl.program_id(0), pl.num_programs(0) - 1
+    deep, chips, group, cols = w_ref.shape
+    rows, width = g_ref.shape[1], chips * group
+
+    @pl.when(i == 0)
+    def _():
+        core = t_ref[1] if first else 1 - t_ref[1]
+        full = lax.broadcasted_iota(jnp.int32, pick.shape, 0)
+        part = lax.broadcasted_iota(jnp.int32, pick.shape, 1)
+        chip = (t_ref[2] - part // group + chips) % chips
+        pick[...] = jnp.where(full == chip * 2 * group + core * group + part % group, 1.0, 0.0).astype(BF16)
+        acc[...] = jnp.zeros_like(acc) if first else ga_before[...]
+
+    both = jnp.concatenate([g_ref[0, :, : 2 * width], g_ref[0, :, 2 * width :]], axis=0)
+    picked = dot(both, pick[...]).astype(BF16)
+    total, outs = acc[...], []
+    for z in range(deep):
+        w = w_ref[z].reshape(width, cols)
+        total = total + dot(picked[z * rows : (z + 1) * rows], w)
+        outs.append(dot(a_ref[...], w, NT).astype(BF16))
+    acc[...] = total
+    placed = dot(jnp.concatenate(outs, axis=0), pick[...], NT)
+    for z in range(deep):
+        at = slice(z * 2 * width, (z + 1) * 2 * width)
+        out = placed[z * rows : (z + 1) * rows]
+        o_ref[0, :, at] = (out if first else out + o_before[0, :, at].astype(F32)).astype(BF16)
+
+    @pl.when(i == last)
+    def _():
+        ga_ref[...] = total.astype(ga_ref.dtype)
+
+
+def output_of(t, attended, pieces, plane, before=()):
     rows, cols = attended.shape
     steps, _, width = pieces.shape
-    deep, chips = own.shape[0] // steps, own.shape[1]
-    return pl.pallas_call(
-        output_kernel,
+    first = not before
+    block = pl.BlockSpec((1, rows, width), lambda i: (i, 0, 0))
+    deep = plane.shape[0] // steps
+    return pl.pallas_call(
+        functools.partial(output_kernel, first),
         out_shape=(
             jax.ShapeDtypeStruct((steps, rows, width), BF16),
-            jax.ShapeDtypeStruct((rows, cols), BF16),
+            jax.ShapeDtypeStruct((rows, cols), F32 if first else BF16),
         ),
-        grid=(1,),
+        grid=(steps,),
         in_specs=[
             SMEM,
             whole((rows, cols)),
-            pl.BlockSpec((steps, rows, width), lambda i: (0, 1, 0)),
-            ANY,
-            ANY,
-        ],
-        out_specs=(whole((steps, rows, width)), whole((rows, cols))),
+            pl.BlockSpec((1, rows, width), lambda i: (i, 1, 0)),
+            pl.BlockSpec((deep, *plane.shape[1:]), lambda i: (i, 0, 0, 0)),
+        ]
+        + ([] if first else [block, whole((rows, cols))]),
+        out_specs=(block, whole((rows, cols))),
         scratch_shapes=[
-            pltpu.VMEM((steps, deep, chips, 2, *own.shape[2:]), BF16),
-            pltpu.SemaphoreType.DMA((steps, 2 * chips)),
+            pltpu.VMEM((width // deep, width // deep // 2), BF16),
+            pltpu.VMEM((rows, cols), F32),
         ],
         compiler_params=params(28),
-        cost_estimate=cost(4 * rows * steps * width * cols, 2 * steps * width * cols),
+        cost_estimate=cost(2 * rows * steps * width * cols, steps * width * cols),
         name="output",
-    )(t, attended, pieces, own, other)
+    )(t, attended, pieces, plane, *before)
 
 
 def backward_kernel(
@@ -374,7 +384,8 @@
     key, value, probs, attended = forward_of(t, query, neighbours, key_weight, value_weight)
     plane = tied(plane, attended)
     other_plane = lax.ppermute(plane, "core", [(0, 1), (1, 0)])
-    out_parts, grad_attended = output_of(t, attended, pieces, plane, other_plane)
+    before = output_of(t, attended, pieces, plane)
+    out_parts, grad_attended = output_of(t, attended, pieces, other_plane, before)
     cross_out = summed(exchanged(out_parts))
     grad_query, *state_parts = backward_of(
         t, grad_attended, query, key, value, probs, key_weight, value_weight, mine.shape

time: 157 us -> 156 us (level); the launches traced: 155 us -> 156 us
  starting transfers between devices: 41 us -> 34.3 us
  Pallas kernels: 41.1 us -> 45 us
  waiting for transfers between devices: 40.3 us -> 42 us
  local copies, waits for them, and re-layouts: 7.9 us -> 9.47 us
    ppermute x1, waiting for transfers between devices: 7.33 us -> 0.01 us  [shards(): other_plane = lax.ppermute(plane, 'core', [(0, 1), (1, 0)])]
    ppermute x3, waiting for transfers between devices: 3.84 us -> 7.79 us  [gathered_plane(): along.append(lax.ppermute(rows, 'x', [(i, (i + s) % n) for i in range(n)]))]
    pallas_call x1 -> x2, Pallas kernels: 6.95 us -> 10.8 us  [output_of(): pl.pallas_call(functools.partial(output_kernel, first), out_shape=(jax.Sh...]
    ppermute x3, waiting for transfers between devices: 0.67 us -> 3.46 us  [to_peers(): lax.ppermute(pieces[r], 'tensor', [(i, (i + r) % n) for i in range(n)])]
    ppermute x8, waiting for transfers between devices: 17.2 us -> 19.8 us  [pairs_moved(): came = lax.ppermute(sent, DP, [(i, (i + sign * by) % n) for i in range(n)])]
    all_gather x1, waiting for transfers between devices: 9.56 us -> 7.42 us  [gathered_plane(): return lax.all_gather(jnp.stack(along), 'z', axis=0)]
    all_to_all x3, waiting for transfers between devices: 1.65 us -> 3.55 us  [exchanged(): return lax.all_to_all(x, 'tensor', split_axis=0, concat_axis=0, tiled=True)]
    ppermute x3, starting transfers between devices: 6.35 us -> 4.52 us  [gathered_plane(): along.append(lax.ppermute(rows, 'x', [(i, (i + s) % n) for i in range(n)]))]
  transfers between devices with their start and end apart: 22 -> 22, of which waited for: 14 -> 15; matrix products, arithmetic and copies ran while one was open for 4% -> 4% of each run, Pallas kernels for 22% -> 25%
where the time goes in v3:
time: 156 us
  Pallas kernels  45 us (29%)
  waiting for transfers between devices  42 us (27%)
  starting transfers between devices  34.3 us (22%)
  between operations  18.9 us (12%)
  local copies, waits for them, and re-layouts  9.47 us (6%)
  other arithmetic  6.27 us (4%)
    ppermute x8, waiting for transfers between devices, pairs_moved(): came = lax.ppermute(sent, DP, [(i, (i + sign * by) % n) for i in range(n)])  19.8 us
    all_to_all x3, starting transfers between devices, exchanged(): return lax.all_to_all(x, 'tensor', split_axis=0, concat_axis=0, tiled=True)  12.3 us
    pallas_call x1, Pallas kernels, backward_of(): pl.pallas_call(functools.partial(backward_kernel, 1.0 / math.sqrt(HEAD)),...  11.4 us
    pallas_call x2, Pallas kernels, output_of(): pl.pallas_call(functools.partial(output_kernel, first), out_shape=(jax.Sh...  10.8 us
    pallas_call x1, Pallas kernels, forward_of(): pl.pallas_call(functools.partial(forward_kernel, 1.0 / math.sqrt(HEAD)),...  10.1 us
    ppermute x3, waiting for transfers between devices, gathered_plane(): along.append(lax.ppermute(rows, 'x', [(i, (i + s) % n) for i in range(n)]))  7.79 us
    all_gather x1, waiting for transfers between devices, gathered_plane(): return lax.all_gather(jnp.stack(along), 'z', axis=0)  7.42 us
    unnamed x26, local copies, waits for them, and re-layouts  7.24 us
  transfers between devices with their start and end apart: 22, of which 15 were waited for; matrix products, arithmetic and copies ran while one was open for 4% of the time, Pallas kernels for 25%

profile of v3, /device:TPU:96, one launch (start us, length us, event | category | flops | bytes accessed | tf_op | source)
XLA Modules:
  0.0 155.9 jit_solution(10600556871456005)
XLA Ops:
  7.2 2.8 %collective-permute-start.9 = (bf16[64,1024]{1,0:T(8,128)(2,1)}, bf16[64,1024]{1,0:T(8,128)(2,1)S(1)}, u32[]{:S(2)}, u32[]{:S(2)}) collective-permute-start(bf16[64,1024]{1,0:T(8,128)(2,1)} %bitcast.28), channel_id=1, source_target_pairs={{0,24},{8,0},{16,8},{24,16},{1,25},{9,1},{17,9},{25,17},{2,26},{10... | collective-permute-start | bytes 393224 | tf_op jit(solution)/shard_map/ppermute | solution.py:356
  11.7 4.2 %collective-permute-done.9 = bf16[64,1024]{1,0:T(8,128)(2,1)S(1)} collective-permute-done((bf16[64,1024]{1,0:T(8,128)(2,1)}, bf16[64,1024]{1,0:T(8,128)(2,1)S(1)}, u32[]{:S(2)}, u32[]{:S(2)}) %collective-permute-start.9) | collective-permute-done | bytes 131104 | tf_op jit(solution)/shard_map/ppermute | solution.py:356
  16.0 2.2 %collective-permute-done.8 = bf16[64,1024]{1,0:T(8,128)(2,1)S(1)} collective-permute-done((bf16[64,1024]{1,0:T(8,128)(2,1)}, bf16[64,1024]{1,0:T(8,128)(2,1)S(1)}, u32[]{:S(2)}, u32[]{:S(2)}) %collective-permute-start.8) | collective-permute-done | bytes 131104 | tf_op jit(solution)/shard_map/ppermute | solution.py:356
  19.5 1.8 %pad_maximum_fusion.1 = bf16[4,64,1024]{2,1,0:T(8,128)(2,1)} fusion(bf16[1,64,1024]{2,1,0:T(8,128)(2,1)S(1)} %bitcast.32, bf16[1,64,1024]{2,1,0:T(8,128)(2,1)S(1)} %bitcast.33, bf16[1,64,1024]{2,1,0:T(8,128)(2,1)S(1)} %bitcast.34, bf16[1,64,1024]{2,1,0:T(8,128)(2,1)} %bitcast.31), kind=kLoop, calls=%fused_computation.1 | loop fusion | flops 786432 | bytes 1048576 | tf_op jit(solution)/shard_map/stack | solution.py:357
  24.1 4.5 %all-to-all-start = ((bf16[4,256,1024]{2,1,0:T(8,128)(2,1)}), bf16[4,256,1024]{2,1,0:T(8,128)(2,1)S(1)}, u32[]{:S(2)}, u32[]{:S(2)}) async-start(bf16[4,256,1024]{2,1,0:T(8,128)(2,1)} %broadcast_in_dim.3), calls=%async_computation | async-start | bytes 4194304 | tf_op jit(solution)/shard_map/all_to_all | solution.py:61
  38.2 3.3 %collective-permute-done.1 = bf16[2,192,128]{2,1,0:T(8,128)(2,1)S(1)} collective-permute-done((bf16[2,192,128]{2,1,0:T(8,128)(2,1)S(1)}, bf16[2,192,128]{2,1,0:T(8,128)(2,1)S(1)}, u32[]{:S(2)}, u32[]{:S(2)}) %collective-permute-start.1) | collective-permute-done | bytes 98336 | tf_op jit(solution)/shard_map/ppermute | solution.py:347
  41.5 3.6 %collective-permute-done.2 = bf16[2,192,128]{2,1,0:T(8,128)(2,1)S(1)} collective-permute-done((bf16[2,192,128]{2,1,0:T(8,128)(2,1)S(1)}, bf16[2,192,128]{2,1,0:T(8,128)(2,1)S(1)}, u32[]{:S(2)}, u32[]{:S(2)}) %collective-permute-start.2) | collective-permute-done | bytes 98336 | tf_op jit(solution)/shard_map/ppermute | solution.py:347
  45.2 3.2 %collective-permute-done.3 = bf16[2,192,128]{2,1,0:T(8,128)(2,1)S(1)} collective-permute-done((bf16[2,192,128]{2,1,0:T(8,128)(2,1)S(1)}, bf16[2,192,128]{2,1,0:T(8,128)(2,1)S(1)}, u32[]{:S(2)}, u32[]{:S(2)}) %collective-permute-start.3) | collective-permute-done | bytes 98336 | tf_op jit(solution)/shard_map/ppermute | solution.py:347
  48.4 3.5 %collective-permute-start.4 = (bf16[4,192,128]{2,1,0:T(8,128)(2,1)S(1)}, bf16[4,192,128]{2,1,0:T(8,128)(2,1)S(1)}, u32[]{:S(2)}, u32[]{:S(2)}) collective-permute-start(bf16[4,192,128]{2,1,0:T(8,128)(2,1)S(1)} %pad_maximum_fusion.2.n0), channel_id=1, source_target_pairs={{1,0},{2,1},{3,2},{0,3},{5,4},{6,5},{7,6},{4,7},{9,8},{10,9},{11,1... | collective-permute-start | bytes 589832 | tf_op jit(solution)/shard_map/ppermute | solution.py:48
  54.3 2.2 %all-to-all-done.h_ref.g_ref = bf16[4,256,1024]{2,1,0:T(8,128)(2,1)S(1)} async-done(((bf16[4,256,1024]{2,1,0:T(8,128)(2,1)}), bf16[4,256,1024]{2,1,0:T(8,128)(2,1)S(1)}, u32[]{:S(2)}, u32[]{:S(2)}) %all-to-all-start) | async-done | bytes 2097184 | tf_op jit(solution)/shard_map/all_to_all | solution.py:61
  57.9 6.0 %query.1.q_ref = bf16[128,1024]{1,0:T(8,128)(2,1)} custom-call(bf16[4,256,1024]{2,1,0:T(8,128)(2,1)} %copy-done, bf16[4096,1024]{1,0:T(8,128)(2,1)} %w_ref.3), custom_call_target="tpu_custom_call" | custom-call | flops 1073741824 | bytes 8388608 | tf_op jit(solution)/shard_map/query/pallas_call | solution.py:106
  65.3 10.1 %forward.1 = (bf16[512,1024]{1,0:T(8,128)(2,1)}, bf16[512,1024]{1,0:T(8,128)(2,1)}, f32[8,2,64,256]{3,2,1,0:T(8,128)}, bf16[128,1024]{1,0:T(8,128)(2,1)}) custom-call(s32[3]{0:T(128)} %pad_add_fusion.t_ref, bf16[128,1024]{1,0:T(8,128)(2,1)} %query.1.q_ref, bf16[4,192,128]{2,1,0:T(8,128)(2,1)} %copy-done.6, bf16[4,192,128]{2,1,0:T(8,128)(2,1)} %copy-done.9, ...), custom_call_target="tpu_custom_call" | custom-call | flops 1610612736 | bytes 10000000 | tf_op jit(solution)/shard_map/forward/pallas_call | solution.py:158
  75.4 7.4 %all-gather.3.cloned.1.call-done = bf16[32,64,1024]{2,1,0:T(8,128)(2,1)} async-done(((bf16[4,64,1024]{2,1,0:T(8,128)(2,1)}), bf16[32,64,1024]{2,1,0:T(8,128)(2,1)}) %all-gather.3.cloned.1.call-update) | async-done | bytes 4194320 | tf_op jit(solution)/shard_map/all_gather | solution.py:357
  84.4 2.2 %copy-done.2 = bf16[8,4,64,1024]{3,2,1,0:T(8,128)(2,1)S(1)} copy-done((bf16[8,4,64,1024]{3,2,1,0:T(8,128)(2,1)S(1)}, bf16[8,4,64,1024]{3,2,1,0:T(8,128)(2,1)}, u32[]{:S(2)}) %copy-start.2) | copy-done | bytes 4194328
  86.6 5.0 %output.2 = (bf16[4,128,1024]{2,1,0:T(8,128)(2,1)S(1)}, f32[128,1024]{1,0:T(8,128)S(1)}) custom-call(s32[3]{0:T(128)S(1)} %copy-done.5, bf16[128,1024]{1,0:T(8,128)(2,1)S(1)} %copy-done.3, bf16[4,256,1024]{2,1,0:T(8,128)(2,1)S(1)} %copy-done.1, bf16[8,4,64,1024]{3,2,1,0:T(8,128)(2,1)S(1)} %copy-done.2), custom_call_target="tpu_custom_call" | custom-call | flops 1073741824 | bytes 4194304 | tf_op jit(solution)/shard_map/output/pallas_call | solution.py:226
  91.7 5.8 %output.3 = (bf16[4,128,1024]{2,1,0:T(8,128)(2,1)}, bf16[128,1024]{1,0:T(8,128)(2,1)S(1)}) custom-call(s32[3]{0:T(128)S(1)} %copy-done.5, bf16[128,1024]{1,0:T(8,128)(2,1)S(1)} %copy-done.3, bf16[4,256,1024]{2,1,0:T(8,128)(2,1)S(1)} %copy-done.1, bf16[8,4,64,1024]{3,2,1,0:T(8,128)(2,1)S(1)} %collective-permute-done.10.w_ref, ...), custom_call_target="tpu_custom_call" | custom-call | flops 1073741824 | bytes 4194304 | tf_op jit(solution)/shard_map/output/pallas_call | solution.py:226
  98.2 4.3 %all-to-all-start.1 = ((bf16[4,128,1024]{2,1,0:T(8,128)(2,1)}), bf16[4,128,1024]{2,1,0:T(8,128)(2,1)S(1)}, u32[]{:S(2)}, u32[]{:S(2)}) async-start(bf16[4,128,1024]{2,1,0:T(8,128)(2,1)} %get-tuple-element.19), calls=%async_computation.1 | async-start | bytes 2097152 | tf_op jit(solution)/shard_map/all_to_all | solution.py:61
  102.4 11.4 %backward.1 = (bf16[128,1024]{1,0:T(8,128)(2,1)}, bf16[4,192,128]{2,1,0:T(8,128)(2,1)}, bf16[4,192,128]{2,1,0:T(8,128)(2,1)}, bf16[4,192,128]{2,1,0:T(8,128)(2,1)}, bf16[4,192,128]{2,1,0:T(8,128)(2,1)}) custom-call(s32[3]{0:T(128)} %pad_add_fusion.t_ref, bf16[128,1024]{1,0:T(8,128)(2,1)} %copy-done.4, bf16[128,1024]{1,0:T(8,128)(2,1)} %query.1.q_ref, ...), custom_call_target="tpu_custom_call" | custom-call | flops 1610612736 | bytes 10000000 | tf_op jit(solution)/shard_map/backward/pallas_call | solution.py:294
  113.8 3.3 %collective-permute-start.13 = (bf16[4,192,128]{2,1,0:T(8,128)(2,1)}, bf16[4,192,128]{2,1,0:T(8,128)(2,1)S(1)}, u32[]{:S(2)}, u32[]{:S(2)}) collective-permute-start(bf16[4,192,128]{2,1,0:T(8,128)(2,1)} %get-tuple-element.28), channel_id=1, source_target_pairs={{0,3},{1,0},{2,1},{3,2},{4,7},{5,4},{6,5},{7,6},{8,11},{9,8},{10,9... | collective-permute-start | bytes 589832 | tf_op jit(solution)/shard_map/ppermute | solution.py:56
  118.9 6.7 %hidden.1 = bf16[4,128,1024]{2,1,0:T(8,128)(2,1)} custom-call(bf16[128,1024]{1,0:T(8,128)(2,1)} %get-tuple-element.24.g_ref, bf16[4096,1024]{1,0:T(8,128)(2,1)} %w_ref.3), custom_call_target="tpu_custom_call" | custom-call | flops 1073741824 | bytes 8388608 | tf_op jit(solution)/shard_map/hidden/pallas_call | solution.py:329
  126.7 2.3 %collective-permute-done.11 = bf16[4,192,128]{2,1,0:T(8,128)(2,1)S(1)} collective-permute-done((bf16[4,192,128]{2,1,0:T(8,128)(2,1)}, bf16[4,192,128]{2,1,0:T(8,128)(2,1)S(1)}, u32[]{:S(2)}, u32[]{:S(2)}) %collective-permute-start.11) | collective-permute-done | bytes 196640 | tf_op jit(solution)/shard_map/ppermute | solution.py:56
  129.1 3.5 %all-to-all-start.2 = ((bf16[4,128,1024]{2,1,0:T(8,128)(2,1)}), bf16[4,128,1024]{2,1,0:T(8,128)(2,1)S(1)}, u32[]{:S(2)}, u32[]{:S(2)}) async-start(bf16[4,128,1024]{2,1,0:T(8,128)(2,1)} %hidden.1), calls=%async_computation.2 | async-start | bytes 2097152 | tf_op jit(solution)/shard_map/all_to_all | solution.py:61
  132.9 2.6 %collective-permute-start.16 = (bf16[2,192,128]{2,1,0:T(8,128)(2,1)S(1)}, bf16[2,192,128]{2,1,0:T(8,128)(2,1)S(1)}, u32[]{:S(2)}, u32[]{:S(2)}) collective-permute-start(bf16[2,192,128]{2,1,0:T(8,128)(2,1)S(1)} %get-tuple-element.34), channel_id=1, source_target_pairs={{0,8},{4,12},{8,16},{12,20},{16,24},{20,28},{24,32},{28,36},{32,40... | collective-permute-start | bytes 294920 | tf_op jit(solution)/shard_map/ppermute | solution.py:347
  136.4 6.9 %collective-permute-done.14 = bf16[2,192,128]{2,1,0:T(8,128)(2,1)S(1)} collective-permute-done((bf16[2,192,128]{2,1,0:T(8,128)(2,1)S(1)}, bf16[2,192,128]{2,1,0:T(8,128)(2,1)S(1)}, u32[]{:S(2)}, u32[]{:S(2)}) %collective-permute-start.14) | collective-permute-done | bytes 98336 | tf_op jit(solution)/shard_map/ppermute | solution.py:347
  (69 shorter events, 28.2 us)
Async XLA Ops:
  7.2 75.7 %all-gather.3.cloned.1.call-start = ((), (), s32[]{:S(2)}) async-start(), calls=%async_computation.3 | async-start | bytes 4718592 | tf_op jit(solution)/shard_map/all_gather | solution.py:357
  7.2 8.7 %collective-permute-start.9 = (bf16[64,1024]{1,0:T(8,128)(2,1)}, bf16[64,1024]{1,0:T(8,128)(2,1)S(1)}, u32[]{:S(2)}, u32[]{:S(2)}) collective-permute-start(bf16[64,1024]{1,0:T(8,128)(2,1)} %bitcast.28), channel_id=1, source_target_pairs={{0,24},{8,0},{16,8},{24,16},{1,25},{9,1},{17,9},{25,17},{2,26},{10... | collective-permute-start | bytes 393224 | tf_op jit(solution)/shard_map/ppermute | solution.py:356
  10.0 8.1 %collective-permute-start.8 = (bf16[64,1024]{1,0:T(8,128)(2,1)}, bf16[64,1024]{1,0:T(8,128)(2,1)S(1)}, u32[]{:S(2)}, u32[]{:S(2)}) collective-permute-start(bf16[64,1024]{1,0:T(8,128)(2,1)} %bitcast.29), channel_id=1, source_target_pairs={{0,16},{8,24},{16,0},{24,8},{1,17},{9,25},{17,1},{25,9},{2,18},{10... | collective-permute-start | bytes 393224 | tf_op jit(solution)/shard_map/ppermute | solution.py:356
  10.8 8.7 %collective-permute-start.7 = (bf16[64,1024]{1,0:T(8,128)(2,1)}, bf16[64,1024]{1,0:T(8,128)(2,1)S(1)}, u32[]{:S(2)}, u32[]{:S(2)}) collective-permute-start(bf16[64,1024]{1,0:T(8,128)(2,1)} %bitcast.30), channel_id=1, source_target_pairs={{0,8},{8,16},{16,24},{24,0},{1,9},{9,17},{17,25},{25,1},{2,10},{10... | collective-permute-start | bytes 393224 | tf_op jit(solution)/shard_map/ppermute | solution.py:356
  21.3 10.6 %copy-start.7 = (bf16[4,128,192]{1,2,0:T(8,128)(2,1)S(1)}, bf16[4,128,192]{1,2,0:T(8,128)(2,1)}, u32[]{:S(2)}) copy-start(bf16[4,128,192]{1,2,0:T(8,128)(2,1)} %param.15) | copy-start | bytes 589828
  24.1 32.4 %all-to-all-start = ((bf16[4,256,1024]{2,1,0:T(8,128)(2,1)}), bf16[4,256,1024]{2,1,0:T(8,128)(2,1)S(1)}, u32[]{:S(2)}, u32[]{:S(2)}) async-start(bf16[4,256,1024]{2,1,0:T(8,128)(2,1)} %broadcast_in_dim.3), calls=%async_computation | async-start | bytes 4194304 | tf_op jit(solution)/shard_map/all_to_all | solution.py:61
  32.0 6.2 %collective-permute-start = (bf16[2,192,128]{2,1,0:T(8,128)(2,1)S(1)}, bf16[2,192,128]{2,1,0:T(8,128)(2,1)S(1)}, u32[]{:S(2)}, u32[]{:S(2)}) collective-permute-start(bf16[2,192,128]{2,1,0:T(8,128)(2,1)S(1)} %get-tuple-element.39), channel_id=1, source_target_pairs={{0,240},{4,244},{8,248},{12,252},{16,0},{20,4},{24,8},{28,12},{32,... | collective-permute-start | bytes 294920 | tf_op jit(solution)/shard_map/ppermute | solution.py:347
  32.4 9.1 %collective-permute-start.1 = (bf16[2,192,128]{2,1,0:T(8,128)(2,1)S(1)}, bf16[2,192,128]{2,1,0:T(8,128)(2,1)S(1)}, u32[]{:S(2)}, u32[]{:S(2)}) collective-permute-start(bf16[2,192,128]{2,1,0:T(8,128)(2,1)S(1)} %get-tuple-element.40), channel_id=1, source_target_pairs={{0,244},{4,248},{8,252},{12,0},{16,4},{20,8},{24,12},{28,16},{32,2... | collective-permute-start | bytes 294920 | tf_op jit(solution)/shard_map/ppermute | solution.py:347
  34.0 11.2 %collective-permute-start.2 = (bf16[2,192,128]{2,1,0:T(8,128)(2,1)S(1)}, bf16[2,192,128]{2,1,0:T(8,128)(2,1)S(1)}, u32[]{:S(2)}, u32[]{:S(2)}) collective-permute-start(bf16[2,192,128]{2,1,0:T(8,128)(2,1)S(1)} %get-tuple-element.38), channel_id=1, source_target_pairs={{0,248},{4,252},{8,0},{12,4},{16,8},{20,12},{24,16},{28,20},{32,24... | collective-permute-start | bytes 294920 | tf_op jit(solution)/shard_map/ppermute | solution.py:347
  34.0 14.3 %collective-permute-start.3 = (bf16[2,192,128]{2,1,0:T(8,128)(2,1)S(1)}, bf16[2,192,128]{2,1,0:T(8,128)(2,1)S(1)}, u32[]{:S(2)}, u32[]{:S(2)}) collective-permute-start(bf16[2,192,128]{2,1,0:T(8,128)(2,1)S(1)} %get-tuple-element.37), channel_id=1, source_target_pairs={{0,252},{4,0},{8,4},{12,8},{16,12},{20,16},{24,20},{28,24},{32,28}... | collective-permute-start | bytes 294920 | tf_op jit(solution)/shard_map/ppermute | solution.py:347
  48.4 15.5 %copy-start.6 = (bf16[4,192,128]{2,1,0:T(8,128)(2,1)}, bf16[4,192,128]{2,1,0:T(8,128)(2,1)S(1)}, u32[]{:S(2)}) copy-start(bf16[4,192,128]{2,1,0:T(8,128)(2,1)S(1)} %pad_maximum_fusion.2.n0) | copy-start | bytes 589828
  48.4 15.5 %collective-permute-start.4 = (bf16[4,192,128]{2,1,0:T(8,128)(2,1)S(1)}, bf16[4,192,128]{2,1,0:T(8,128)(2,1)S(1)}, u32[]{:S(2)}, u32[]{:S(2)}) collective-permute-start(bf16[4,192,128]{2,1,0:T(8,128)(2,1)S(1)} %pad_maximum_fusion.2.n0), channel_id=1, source_target_pairs={{1,0},{2,1},{3,2},{0,3},{5,4},{6,5},{7,6},{4,7},{9,8},{10,9},{11,1... | collective-permute-start | bytes 589832 | tf_op jit(solution)/shard_map/ppermute | solution.py:48
  51.9 12.0 %collective-permute-start.5 = (bf16[4,192,128]{2,1,0:T(8,128)(2,1)S(1)}, bf16[4,192,128]{2,1,0:T(8,128)(2,1)S(1)}, u32[]{:S(2)}, u32[]{:S(2)}) collective-permute-start(bf16[4,192,128]{2,1,0:T(8,128)(2,1)S(1)} %pad_maximum_fusion.2.n0), channel_id=1, source_target_pairs={{2,0},{3,1},{0,2},{1,3},{6,4},{7,5},{4,6},{5,7},{10,8},{11,9},{8,1... | collective-permute-start | bytes 589832 | tf_op jit(solution)/shard_map/ppermute | solution.py:48
  52.8 11.1 %collective-permute-start.6 = (bf16[4,192,128]{2,1,0:T(8,128)(2,1)S(1)}, bf16[4,192,128]{2,1,0:T(8,128)(2,1)S(1)}, u32[]{:S(2)}, u32[]{:S(2)}) collective-permute-start(bf16[4,192,128]{2,1,0:T(8,128)(2,1)S(1)} %pad_maximum_fusion.2.n0), channel_id=1, source_target_pairs={{3,0},{0,1},{1,2},{2,3},{7,4},{4,5},{5,6},{6,7},{11,8},{8,9},{9,10... | collective-permute-start | bytes 589832 | tf_op jit(solution)/shard_map/ppermute | solution.py:48
  82.8 8.8 %collective-permute-start.10 = (bf16[8,4,64,1024]{3,2,1,0:T(8,128)(2,1)}, bf16[8,4,64,1024]{3,2,1,0:T(8,128)(2,1)S(1)}, u32[]{:S(2)}, u32[]{:S(2)}) collective-permute-start(bf16[8,4,64,1024]{3,2,1,0:T(8,128)(2,1)} %tied.1.w_ref), channel_id=1, source_target_pairs={{0,4},{4,0},{1,5},{5,1},{2,6},{6,2},{3,7},{7,3},{8,12},{12,8},{9,1... | collective-permute-start | bytes 12582920 | tf_op jit(solution)/shard_map/ppermute | solution.py:386
  98.2 30.9 %all-to-all-start.1 = ((bf16[4,128,1024]{2,1,0:T(8,128)(2,1)}), bf16[4,128,1024]{2,1,0:T(8,128)(2,1)S(1)}, u32[]{:S(2)}, u32[]{:S(2)}) async-start(bf16[4,128,1024]{2,1,0:T(8,128)(2,1)} %get-tuple-element.19), calls=%async_computation.1 | async-start | bytes 2097152 | tf_op jit(solution)/shard_map/all_to_all | solution.py:61
  113.8 11.7 %collective-permute-start.13 = (bf16[4,192,128]{2,1,0:T(8,128)(2,1)}, bf16[4,192,128]{2,1,0:T(8,128)(2,1)S(1)}, u32[]{:S(2)}, u32[]{:S(2)}) collective-permute-start(bf16[4,192,128]{2,1,0:T(8,128)(2,1)} %get-tuple-element.28), channel_id=1, source_target_pairs={{0,3},{1,0},{2,1},{3,2},{4,7},{5,4},{6,5},{7,6},{8,11},{9,8},{10,9... | collective-permute-start | bytes 589832 | tf_op jit(solution)/shard_map/ppermute | solution.py:56
  117.1 9.6 %collective-permute-start.12 = (bf16[4,192,128]{2,1,0:T(8,128)(2,1)}, bf16[4,192,128]{2,1,0:T(8,128)(2,1)S(1)}, u32[]{:S(2)}, u32[]{:S(2)}) collective-permute-start(bf16[4,192,128]{2,1,0:T(8,128)(2,1)} %get-tuple-element.27), channel_id=1, source_target_pairs={{0,2},{1,3},{2,0},{3,1},{4,6},{5,7},{6,4},{7,5},{8,10},{9,11},{10,... | collective-permute-start | bytes 589832 | tf_op jit(solution)/shard_map/ppermute | solution.py:56
  118.0 11.0 %collective-permute-start.11 = (bf16[4,192,128]{2,1,0:T(8,128)(2,1)}, bf16[4,192,128]{2,1,0:T(8,128)(2,1)S(1)}, u32[]{:S(2)}, u32[]{:S(2)}) collective-permute-start(bf16[4,192,128]{2,1,0:T(8,128)(2,1)} %get-tuple-element.26), channel_id=1, source_target_pairs={{0,1},{1,2},{2,3},{3,0},{4,5},{5,6},{6,7},{7,4},{8,9},{9,10},{10,1... | collective-permute-start | bytes 589832 | tf_op jit(solution)/shard_map/ppermute | solution.py:56
  129.1 19.1 %all-to-all-start.2 = ((bf16[4,128,1024]{2,1,0:T(8,128)(2,1)}), bf16[4,128,1024]{2,1,0:T(8,128)(2,1)S(1)}, u32[]{:S(2)}, u32[]{:S(2)}) async-start(bf16[4,128,1024]{2,1,0:T(8,128)(2,1)} %hidden.1), calls=%async_computation.2 | async-start | bytes 2097152 | tf_op jit(solution)/shard_map/all_to_all | solution.py:61
  132.7 10.6 %collective-permute-start.14 = (bf16[2,192,128]{2,1,0:T(8,128)(2,1)S(1)}, bf16[2,192,128]{2,1,0:T(8,128)(2,1)S(1)}, u32[]{:S(2)}, u32[]{:S(2)}) collective-permute-start(bf16[2,192,128]{2,1,0:T(8,128)(2,1)S(1)} %get-tuple-element.35), channel_id=1, source_target_pairs={{0,16},{4,20},{8,24},{12,28},{16,32},{20,36},{24,40},{28,44},{32,4... | collective-permute-start | bytes 294920 | tf_op jit(solution)/shard_map/ppermute | solution.py:347
  132.8 10.7 %collective-permute-start.15 = (bf16[2,192,128]{2,1,0:T(8,128)(2,1)S(1)}, bf16[2,192,128]{2,1,0:T(8,128)(2,1)S(1)}, u32[]{:S(2)}, u32[]{:S(2)}) collective-permute-start(bf16[2,192,128]{2,1,0:T(8,128)(2,1)S(1)} %get-tuple-element.36), channel_id=1, source_target_pairs={{0,12},{4,16},{8,20},{12,24},{16,28},{20,32},{24,36},{28,40},{32,4... | collective-permute-start | bytes 294920 | tf_op jit(solution)/shard_map/ppermute | solution.py:347
  132.9 10.6 %collective-permute-start.16 = (bf16[2,192,128]{2,1,0:T(8,128)(2,1)S(1)}, bf16[2,192,128]{2,1,0:T(8,128)(2,1)S(1)}, u32[]{:S(2)}, u32[]{:S(2)}) collective-permute-start(bf16[2,192,128]{2,1,0:T(8,128)(2,1)S(1)} %get-tuple-element.34), channel_id=1, source_target_pairs={{0,8},{4,12},{8,16},{12,20},{16,24},{20,28},{24,32},{28,36},{32,40... | collective-permute-start | bytes 294920 | tf_op jit(solution)/shard_map/ppermute | solution.py:347
  135.5 9.8 %collective-permute-start.17 = (bf16[2,192,128]{2,1,0:T(8,128)(2,1)S(1)}, bf16[2,192,128]{2,1,0:T(8,128)(2,1)S(1)}, u32[]{:S(2)}, u32[]{:S(2)}) collective-permute-start(bf16[2,192,128]{2,1,0:T(8,128)(2,1)S(1)} %get-tuple-element.33), channel_id=1, source_target_pairs={{0,4},{4,8},{8,12},{12,16},{16,20},{20,24},{24,28},{28,32},{32,36}... | collective-permute-start | bytes 294920 | tf_op jit(solution)/shard_map/ppermute | solution.py:347
  (11 other events, 28.6 us)
Sparse Core Ops, SparseCore 0:
  21.5 61.3 all-gather.2

commit v4 on v0

--- a/solution.py
+++ b/solution.py
@@ -1,4 +1,5 @@
 import functools
+import itertools
 import math
 
 import jax
@@ -330,13 +331,21 @@
 
 def pairs_moved(blocks, gaps, sign):
     n = math.prod(lax.axis_size(a) for a in DP)
+    low = jnp.minimum(gaps[0], gaps[1])
+    high = jnp.maximum(gaps[0], gaps[1])
+    first_low = gaps[0] == low
     pairs = blocks[:2], blocks[2:]
-    got = [None, None]
-    for by in range(1, WINDOW + 1):
-        sent = jnp.where(gaps[0] == by, *pairs)
-        came = lax.ppermute(sent, DP, [(i, (i + sign * by) % n) for i in range(n)])
-        got = [came if g is None else jnp.where(gaps[k] == by, came, g) for k, g in enumerate(got)]
-    return jnp.concatenate(got, axis=0)
+
+    def moved(x, by):
+        return lax.ppermute(x, DP, [(i, (i + sign * by) % n) for i in range(n)])
+
+    choices = list(itertools.combinations(range(1, WINDOW + 1), 2))
+    which = sum(i * ((low == a) & (high == b)).astype(jnp.int32) for i, (a, b) in enumerate(choices))
+    branches = [lambda x, y, a=a, b=b: (moved(x, a), moved(y, b)) for a, b in choices]
+    near, far = lax.switch(
+        which, branches, jnp.where(first_low, *pairs), jnp.where(first_low, *pairs[::-1])
+    )
+    return jnp.concatenate([jnp.where(first_low, near, far), jnp.where(first_low, far, near)], axis=0)
 
 
 def gathered_plane(rows):

time: 157 us -> 152 us (0.968)
  starting transfers between devices: 41 us -> 34.5 us
  other arithmetic: 6.22 us -> 8.12 us
    all_to_all x3, waiting for transfers between devices: 1.65 us -> 7.93 us  [exchanged(): return lax.all_to_all(x, 'tensor', split_axis=0, concat_axis=0, tiled=True)]
    ppermute x8 -> x4, starting transfers between devices: 8.91 us -> 3.08 us  [moved(): return lax.ppermute(x, DP, [(i, (i + sign * by) % n) for i in range(n)])]
    all_gather x1, waiting for transfers between devices: 9.56 us -> 6.34 us  [gathered_plane(): return lax.all_gather(jnp.stack(along), 'z', axis=0)]
    select_n x4, other arithmetic: 0.12 us -> 1.96 us  [the longest x2 1.92 us: pairs_moved(): jnp.where(first_low, near, far)]
    ppermute x8 -> x4, waiting for transfers between devices: 17.2 us -> 15.9 us  [moved(): return lax.ppermute(x, DP, [(i, (i + sign * by) % n) for i in range(n)])]
  transfers between devices with their start and end apart: 22 -> 18, of which waited for: 14 -> 9; matrix products, arithmetic and copies ran while one was open for 4% -> 5% of each run, Pallas kernels for 22% -> 23%
where the time goes in v4:
time: 152 us; the launch traced here: 151 us
  waiting for transfers between devices  41.4 us (27%)
  Pallas kernels  41.1 us (27%)
  starting transfers between devices  34.5 us (23%)
  between operations  17.5 us (12%)
  other arithmetic  8.12 us (5%)
  local copies, waits for them, and re-layouts  7.89 us (5%)
    ppermute x4, waiting for transfers between devices, moved(): return lax.ppermute(x, DP, [(i, (i + sign * by) % n) for i in range(n)])  15.9 us
    all_to_all x3, starting transfers between devices, exchanged(): return lax.all_to_all(x, 'tensor', split_axis=0, concat_axis=0, tiled=True)  12.3 us
    pallas_call x1, Pallas kernels, backward_of(): pl.pallas_call(functools.partial(backward_kernel, 1.0 / math.sqrt(HEAD)),...  11.4 us
    pallas_call x1, Pallas kernels, forward_of(): pl.pallas_call(functools.partial(forward_kernel, 1.0 / math.sqrt(HEAD)),...  10.1 us
    all_to_all x3, waiting for transfers between devices, exchanged(): return lax.all_to_all(x, 'tensor', split_axis=0, concat_axis=0, tiled=True)  7.93 us
    ppermute x1, waiting for transfers between devices, shards(): other_plane = lax.ppermute(plane, 'core', [(0, 1), (1, 0)])  7.33 us
    pallas_call x1, Pallas kernels, output_of(): pl.pallas_call(output_kernel, out_shape=(jax.ShapeDtypeStruct((steps, row...  6.93 us
    pallas_call x1, Pallas kernels, hidden_of(): pl.pallas_call(hidden_kernel, out_shape=jax.ShapeDtypeStruct((4, rows, wi...  6.67 us
  transfers between devices with their start and end apart: 18, of which 9 were waited for; matrix products, arithmetic and copies ran while one was open for 5% of the time, Pallas kernels for 23%

profile of v4, /device:TPU:96, one launch (start us, length us, event | category | flops | bytes accessed | tf_op | source)
XLA Modules:
  0.0 150.9 jit_solution(10457932085833541928)
XLA Ops:
  7.2 3.1 %collective-permute-start.28 = (bf16[64,1024]{1,0:T(8,128)(2,1)}, bf16[64,1024]{1,0:T(8,128)(2,1)S(1)}, u32[]{:S(2)}, u32[]{:S(2)}) collective-permute-start(bf16[64,1024]{1,0:T(8,128)(2,1)} %bitcast.23), channel_id=1, source_target_pairs={{0,16},{8,24},{16,0},{24,8},{1,17},{9,25},{17,1},{25,9},{2,18},{10... | collective-permute-start | bytes 393224 | tf_op jit(solution)/shard_map/ppermute | solution.py:355
  10.9 2.6 %collective-permute-start.29 = (bf16[64,1024]{1,0:T(8,128)(2,1)}, bf16[64,1024]{1,0:T(8,128)(2,1)S(1)}, u32[]{:S(2)}, u32[]{:S(2)}) collective-permute-start(bf16[64,1024]{1,0:T(8,128)(2,1)} %bitcast.25), channel_id=1, source_target_pairs={{0,24},{8,0},{16,8},{24,16},{1,25},{9,1},{17,9},{25,17},{2,26},{10... | collective-permute-start | bytes 393224 | tf_op jit(solution)/shard_map/ppermute | solution.py:355
  22.0 4.5 %all-to-all-start = ((bf16[4,256,1024]{2,1,0:T(8,128)(2,1)}), bf16[4,256,1024]{2,1,0:T(8,128)(2,1)S(1)}, u32[]{:S(2)}, u32[]{:S(2)}) async-start(bf16[4,256,1024]{2,1,0:T(8,128)(2,1)} %broadcast_in_dim.3), calls=%async_computation | async-start | bytes 4194304 | tf_op jit(solution)/shard_map/all_to_all | solution.py:62
  30.4 11.0 %conditional.2 = (bf16[2,192,128]{2,1,0:T(8,128)(2,1)}, bf16[2,192,128]{2,1,0:T(8,128)(2,1)}) conditional(s32[]{:T(128)} %clamp.4, (bf16[2,192,128]{2,1,0:T(8,128)(2,1)S(1)}, bf16[2,192,128]{2,1,0:T(8,128)(2,1)S(1)}) %tuple.56, (bf16[2,192,128]{2,1,0:T(8,128)(2,1)S(1)}, bf16[2,192,128]{2,1,0:T(8,128)(2,1)S(1)}) %tuple.56, ...), branch_computations={%region_0.1_spmd, %region_1.2_spmd, %region_2.3_spmd, %region_3.4_... | conditional | bytes 786528 | solution.py:345
  30.5 2.5 %collective-permute-start.8 = (bf16[2,192,128]{2,1,0:T(8,128)(2,1)S(1)}, bf16[2,192,128]{2,1,0:T(8,128)(2,1)}, u32[]{:S(2)}, u32[]{:S(2)}) collective-permute-start(bf16[2,192,128]{2,1,0:T(8,128)(2,1)S(1)} %get-tuple-element.56), channel_id=1, source_target_pairs={{0,248},{4,252},{8,0},{12,4},{16,8},{20,12},{24,16},{28,20},{32,24... | collective-permute-start | bytes 294920 | tf_op jit(solution)/shard_map/cond/branch_4_fun/ppermute | solution.py:340
  33.4 4.8 %collective-permute-done.8 = bf16[2,192,128]{2,1,0:T(8,128)(2,1)} collective-permute-done((bf16[2,192,128]{2,1,0:T(8,128)(2,1)S(1)}, bf16[2,192,128]{2,1,0:T(8,128)(2,1)}, u32[]{:S(2)}, u32[]{:S(2)}) %collective-permute-start.8) | collective-permute-done | bytes 98336 | tf_op jit(solution)/shard_map/cond/branch_4_fun/ppermute | solution.py:340
  38.2 3.3 %collective-permute-done.9 = bf16[2,192,128]{2,1,0:T(8,128)(2,1)} collective-permute-done((bf16[2,192,128]{2,1,0:T(8,128)(2,1)S(1)}, bf16[2,192,128]{2,1,0:T(8,128)(2,1)}, u32[]{:S(2)}, u32[]{:S(2)}) %collective-permute-start.9) | collective-permute-done | bytes 98336 | tf_op jit(solution)/shard_map/cond/branch_4_fun/ppermute | solution.py:340
  42.4 2.4 %collective-permute-start.26 = (bf16[4,192,128]{2,1,0:T(8,128)(2,1)S(1)}, bf16[4,192,128]{2,1,0:T(8,128)(2,1)S(1)}, u32[]{:S(2)}, u32[]{:S(2)}) collective-permute-start(bf16[4,192,128]{2,1,0:T(8,128)(2,1)S(1)} %pad_maximum_fusion.2.n0), channel_id=1, source_target_pairs={{3,0},{0,1},{1,2},{2,3},{7,4},{4,5},{5,6},{6,7},{11,8},{8,9},{9,10... | collective-permute-start | bytes 589832 | tf_op jit(solution)/shard_map/ppermute | solution.py:49
  44.8 2.6 %collective-permute-start.25 = (bf16[4,192,128]{2,1,0:T(8,128)(2,1)S(1)}, bf16[4,192,128]{2,1,0:T(8,128)(2,1)S(1)}, u32[]{:S(2)}, u32[]{:S(2)}) collective-permute-start(bf16[4,192,128]{2,1,0:T(8,128)(2,1)S(1)} %pad_maximum_fusion.2.n0), channel_id=1, source_target_pairs={{2,0},{3,1},{0,2},{1,3},{6,4},{7,5},{4,6},{5,7},{10,8},{11,9},{8,1... | collective-permute-start | bytes 589832 | tf_op jit(solution)/shard_map/ppermute | solution.py:49
  49.6 4.7 %all-to-all-done.h_ref.g_ref = bf16[4,256,1024]{2,1,0:T(8,128)(2,1)S(1)} async-done(((bf16[4,256,1024]{2,1,0:T(8,128)(2,1)}), bf16[4,256,1024]{2,1,0:T(8,128)(2,1)S(1)}, u32[]{:S(2)}, u32[]{:S(2)}) %all-to-all-start) | async-done | bytes 2097184 | tf_op jit(solution)/shard_map/all_to_all | solution.py:62
  55.7 6.0 %query.1.q_ref = bf16[128,1024]{1,0:T(8,128)(2,1)} custom-call(bf16[4,256,1024]{2,1,0:T(8,128)(2,1)} %copy-done, bf16[4096,1024]{1,0:T(8,128)(2,1)} %w_ref.3), custom_call_target="tpu_custom_call" | custom-call | flops 1073741824 | bytes 8388608 | tf_op jit(solution)/shard_map/query/pallas_call | solution.py:107
  63.1 10.1 %forward.1 = (bf16[512,1024]{1,0:T(8,128)(2,1)}, bf16[512,1024]{1,0:T(8,128)(2,1)}, f32[8,2,64,256]{3,2,1,0:T(8,128)}, bf16[128,1024]{1,0:T(8,128)(2,1)}) custom-call(s32[3]{0:T(128)} %pad_add_fusion.t_ref, bf16[128,1024]{1,0:T(8,128)(2,1)} %query.1.q_ref, bf16[4,192,128]{2,1,0:T(8,128)(2,1)} %copy-done.7, bf16[4,192,128]{2,1,0:T(8,128)(2,1)} %copy-done.11, ...), custom_call_target="tpu_custom_call" | custom-call | flops 1610612736 | bytes 10000000 | tf_op jit(solution)/shard_map/forward/pallas_call | solution.py:159
  73.2 6.3 %all-gather.3.cloned.1.call-done = bf16[32,64,1024]{2,1,0:T(8,128)(2,1)} async-done(((bf16[4,64,1024]{2,1,0:T(8,128)(2,1)}), bf16[32,64,1024]{2,1,0:T(8,128)(2,1)}) %all-gather.3.cloned.1.call-update) | async-done | bytes 4194320 | tf_op jit(solution)/shard_map/all_gather | solution.py:356
  79.6 7.3 %collective-permute-done.30.other = bf16[8,4,64,1024]{3,2,1,0:T(8,128)(2,1)S(1)} collective-permute-done((bf16[8,4,64,1024]{3,2,1,0:T(8,128)(2,1)}, bf16[8,4,64,1024]{3,2,1,0:T(8,128)(2,1)S(1)}, u32[]{:S(2)}, u32[]{:S(2)}) %collective-permute-start.30) | collective-permute-done | bytes 4194336 | tf_op jit(solution)/shard_map/ppermute | solution.py:385
  86.9 2.2 %copy-done.2 = bf16[8,4,64,1024]{3,2,1,0:T(8,128)(2,1)S(1)} copy-done((bf16[8,4,64,1024]{3,2,1,0:T(8,128)(2,1)S(1)}, bf16[8,4,64,1024]{3,2,1,0:T(8,128)(2,1)}, u32[]{:S(2)}) %copy-start.2) | copy-done | bytes 4194328
  89.1 6.9 %output.1 = (bf16[4,128,1024]{2,1,0:T(8,128)(2,1)}, bf16[128,1024]{1,0:T(8,128)(2,1)S(1)}) custom-call(s32[3]{0:T(128)S(1)} %copy-done.5, bf16[128,1024]{1,0:T(8,128)(2,1)S(1)} %copy-done.3, bf16[4,256,1024]{2,1,0:T(8,128)(2,1)S(1)} %copy-done.1, bf16[8,4,64,1024]{3,2,1,0:T(8,128)(2,1)S(1)} %copy-done.2, ...), custom_call_target="tpu_custom_call" | custom-call | flops 2147483648 | bytes 8388608 | tf_op jit(solution)/shard_map/output/pallas_call | solution.py:217
  96.8 4.3 %all-to-all-start.1 = ((bf16[4,128,1024]{2,1,0:T(8,128)(2,1)}), bf16[4,128,1024]{2,1,0:T(8,128)(2,1)S(1)}, u32[]{:S(2)}, u32[]{:S(2)}) async-start(bf16[4,128,1024]{2,1,0:T(8,128)(2,1)} %get-tuple-element.93), calls=%async_computation.1 | async-start | bytes 2097152 | tf_op jit(solution)/shard_map/all_to_all | solution.py:62
  101.1 11.4 %backward.1 = (bf16[128,1024]{1,0:T(8,128)(2,1)}, bf16[4,192,128]{2,1,0:T(8,128)(2,1)}, bf16[4,192,128]{2,1,0:T(8,128)(2,1)}, bf16[4,192,128]{2,1,0:T(8,128)(2,1)}, bf16[4,192,128]{2,1,0:T(8,128)(2,1)}) custom-call(s32[3]{0:T(128)} %pad_add_fusion.t_ref, bf16[128,1024]{1,0:T(8,128)(2,1)} %copy-done.4, bf16[128,1024]{1,0:T(8,128)(2,1)} %query.1.q_ref, ...), custom_call_target="tpu_custom_call" | custom-call | flops 1610612736 | bytes 10000000 | tf_op jit(solution)/shard_map/backward/pallas_call | solution.py:285
  114.6 2.7 %collective-permute-start.32 = (bf16[4,192,128]{2,1,0:T(8,128)(2,1)}, bf16[4,192,128]{2,1,0:T(8,128)(2,1)S(1)}, u32[]{:S(2)}, u32[]{:S(2)}) collective-permute-start(bf16[4,192,128]{2,1,0:T(8,128)(2,1)} %get-tuple-element.101), channel_id=1, source_target_pairs={{0,2},{1,3},{2,0},{3,1},{4,6},{5,7},{6,4},{7,5},{8,10},{9,11},{10,... | collective-permute-start | bytes 589832 | tf_op jit(solution)/shard_map/ppermute | solution.py:57
  118.7 6.7 %hidden.1 = bf16[4,128,1024]{2,1,0:T(8,128)(2,1)} custom-call(bf16[128,1024]{1,0:T(8,128)(2,1)} %get-tuple-element.98.g_ref, bf16[4096,1024]{1,0:T(8,128)(2,1)} %w_ref.3), custom_call_target="tpu_custom_call" | custom-call | flops 1073741824 | bytes 8388608 | tf_op jit(solution)/shard_map/hidden/pallas_call | solution.py:320
  125.4 3.5 %all-to-all-start.2 = ((bf16[4,128,1024]{2,1,0:T(8,128)(2,1)}), bf16[4,128,1024]{2,1,0:T(8,128)(2,1)S(1)}, u32[]{:S(2)}, u32[]{:S(2)}) async-start(bf16[4,128,1024]{2,1,0:T(8,128)(2,1)} %hidden.1), calls=%async_computation.2 | async-start | bytes 2097152 | tf_op jit(solution)/shard_map/all_to_all | solution.py:62
  129.1 8.3 %conditional.3 = (bf16[2,192,128]{2,1,0:T(8,128)(2,1)}, bf16[2,192,128]{2,1,0:T(8,128)(2,1)}) conditional(s32[]{:T(128)} %clamp.4, (pred[]{:T(512)}, (), bf16[4,192,128]{2,1,0:T(8,128)(2,1)S(1)}, bf16[4,192,128]{2,1,0:T(8,128)(2,1)S(1)}, (), /*index=5*/()) %tuple.57, (pred[]{:T(512)}, (), ...), branch_computations={%region_6.7_spmd, %region_7.8_spmd, %region_8.9_spmd, %region_9.10... | conditional | flops 98304 | bytes 1179745 | solution.py:345
  129.5 7.9 %collective-permute-done.21 = bf16[2,192,128]{2,1,0:T(8,128)(2,1)} collective-permute-done((bf16[2,192,128]{2,1,0:T(8,128)(2,1)S(1)}, bf16[2,192,128]{2,1,0:T(8,128)(2,1)}, u32[]{:S(2)}, u32[]{:S(2)}) %collective-permute-start.21) | collective-permute-done | bytes 98336 | tf_op jit(solution)/shard_map/cond/branch_4_fun/ppermute | solution.py:340
  140.0 3.2 %all-to-all-done.2 = bf16[4,128,1024]{2,1,0:T(8,128)(2,1)S(1)} async-done(((bf16[4,128,1024]{2,1,0:T(8,128)(2,1)}), bf16[4,128,1024]{2,1,0:T(8,128)(2,1)S(1)}, u32[]{:S(2)}, u32[]{:S(2)}) %all-to-all-start.2) | async-done | bytes 1048608 | tf_op jit(solution)/shard_map/all_to_all | solution.py:62
  (62 shorter events, 24.0 us)
Async XLA Ops:
  7.2 72.4 %all-gather.3.cloned.1.call-start = ((), (), s32[]{:S(2)}) async-start(), calls=%async_computation.3 | async-start | bytes 4718592 | tf_op jit(solution)/shard_map/all_gather | solution.py:356
  7.2 8.1 %collective-permute-start.28 = (bf16[64,1024]{1,0:T(8,128)(2,1)}, bf16[64,1024]{1,0:T(8,128)(2,1)S(1)}, u32[]{:S(2)}, u32[]{:S(2)}) collective-permute-start(bf16[64,1024]{1,0:T(8,128)(2,1)} %bitcast.23), channel_id=1, source_target_pairs={{0,16},{8,24},{16,0},{24,8},{1,17},{9,25},{17,1},{25,9},{2,18},{10... | collective-permute-start | bytes 393224 | tf_op jit(solution)/shard_map/ppermute | solution.py:355
  10.3 7.1 %collective-permute-start.27 = (bf16[64,1024]{1,0:T(8,128)(2,1)}, bf16[64,1024]{1,0:T(8,128)(2,1)S(1)}, u32[]{:S(2)}, u32[]{:S(2)}) collective-permute-start(bf16[64,1024]{1,0:T(8,128)(2,1)} %bitcast.24), channel_id=1, source_target_pairs={{0,8},{8,16},{16,24},{24,0},{1,9},{9,17},{17,25},{25,1},{2,10},{10... | collective-permute-start | bytes 393224 | tf_op jit(solution)/shard_map/ppermute | solution.py:355
  10.9 6.5 %collective-permute-start.29 = (bf16[64,1024]{1,0:T(8,128)(2,1)}, bf16[64,1024]{1,0:T(8,128)(2,1)S(1)}, u32[]{:S(2)}, u32[]{:S(2)}) collective-permute-start(bf16[64,1024]{1,0:T(8,128)(2,1)} %bitcast.25), channel_id=1, source_target_pairs={{0,24},{8,0},{16,8},{24,16},{1,25},{9,1},{17,9},{25,17},{2,26},{10... | collective-permute-start | bytes 393224 | tf_op jit(solution)/shard_map/ppermute | solution.py:355
  19.2 11.2 %copy-start.6 = (bf16[4,128,192]{1,2,0:T(8,128)(2,1)S(1)}, bf16[4,128,192]{1,2,0:T(8,128)(2,1)}, u32[]{:S(2)}) copy-start(bf16[4,128,192]{1,2,0:T(8,128)(2,1)} %param.27) | copy-start | bytes 589828
  22.0 32.3 %all-to-all-start = ((bf16[4,256,1024]{2,1,0:T(8,128)(2,1)}), bf16[4,256,1024]{2,1,0:T(8,128)(2,1)S(1)}, u32[]{:S(2)}, u32[]{:S(2)}) async-start(bf16[4,256,1024]{2,1,0:T(8,128)(2,1)} %broadcast_in_dim.3), calls=%async_computation | async-start | bytes 4194304 | tf_op jit(solution)/shard_map/all_to_all | solution.py:62
  30.5 7.7 %collective-permute-start.8 = (bf16[2,192,128]{2,1,0:T(8,128)(2,1)S(1)}, bf16[2,192,128]{2,1,0:T(8,128)(2,1)}, u32[]{:S(2)}, u32[]{:S(2)}) collective-permute-start(bf16[2,192,128]{2,1,0:T(8,128)(2,1)S(1)} %get-tuple-element.56), channel_id=1, source_target_pairs={{0,248},{4,252},{8,0},{12,4},{16,8},{20,12},{24,16},{28,20},{32,24... | collective-permute-start | bytes 294920 | tf_op jit(solution)/shard_map/cond/branch_4_fun/ppermute | solution.py:340
  33.0 8.4 %collective-permute-start.9 = (bf16[2,192,128]{2,1,0:T(8,128)(2,1)S(1)}, bf16[2,192,128]{2,1,0:T(8,128)(2,1)}, u32[]{:S(2)}, u32[]{:S(2)}) collective-permute-start(bf16[2,192,128]{2,1,0:T(8,128)(2,1)S(1)} %get-tuple-element.57), channel_id=1, source_target_pairs={{0,240},{4,244},{8,248},{12,252},{16,0},{20,4},{24,8},{28,12},{32,... | collective-permute-start | bytes 294920 | tf_op jit(solution)/shard_map/cond/branch_4_fun/ppermute | solution.py:340
  42.4 19.3 %copy-start.7 = (bf16[4,192,128]{2,1,0:T(8,128)(2,1)}, bf16[4,192,128]{2,1,0:T(8,128)(2,1)S(1)}, u32[]{:S(2)}) copy-start(bf16[4,192,128]{2,1,0:T(8,128)(2,1)S(1)} %pad_maximum_fusion.2.n0) | copy-start | bytes 589828
  42.4 19.3 %collective-permute-start.26 = (bf16[4,192,128]{2,1,0:T(8,128)(2,1)S(1)}, bf16[4,192,128]{2,1,0:T(8,128)(2,1)S(1)}, u32[]{:S(2)}, u32[]{:S(2)}) collective-permute-start(bf16[4,192,128]{2,1,0:T(8,128)(2,1)S(1)} %pad_maximum_fusion.2.n0), channel_id=1, source_target_pairs={{3,0},{0,1},{1,2},{2,3},{7,4},{4,5},{5,6},{6,7},{11,8},{8,9},{9,10... | collective-permute-start | bytes 589832 | tf_op jit(solution)/shard_map/ppermute | solution.py:49
  44.8 16.9 %collective-permute-start.25 = (bf16[4,192,128]{2,1,0:T(8,128)(2,1)S(1)}, bf16[4,192,128]{2,1,0:T(8,128)(2,1)S(1)}, u32[]{:S(2)}, u32[]{:S(2)}) collective-permute-start(bf16[4,192,128]{2,1,0:T(8,128)(2,1)S(1)} %pad_maximum_fusion.2.n0), channel_id=1, source_target_pairs={{2,0},{3,1},{0,2},{1,3},{6,4},{7,5},{4,6},{5,7},{10,8},{11,9},{8,1... | collective-permute-start | bytes 589832 | tf_op jit(solution)/shard_map/ppermute | solution.py:49
  47.5 14.3 %collective-permute-start.24 = (bf16[4,192,128]{2,1,0:T(8,128)(2,1)S(1)}, bf16[4,192,128]{2,1,0:T(8,128)(2,1)S(1)}, u32[]{:S(2)}, u32[]{:S(2)}) collective-permute-start(bf16[4,192,128]{2,1,0:T(8,128)(2,1)S(1)} %pad_maximum_fusion.2.n0), channel_id=1, source_target_pairs={{1,0},{2,1},{3,2},{0,3},{5,4},{6,5},{7,6},{4,7},{9,8},{10,9},{11,1... | collective-permute-start | bytes 589832 | tf_op jit(solution)/shard_map/ppermute | solution.py:49
  79.5 7.4 %copy-start.1 = (bf16[4,256,1024]{2,1,0:T(8,128)(2,1)S(1)}, bf16[4,256,1024]{2,1,0:T(8,128)(2,1)}, u32[]{:S(2)}) copy-start(bf16[4,256,1024]{2,1,0:T(8,128)(2,1)} %copy-done) | copy-start | bytes 6291460
  79.6 7.4 %copy-start.3 = (bf16[128,1024]{1,0:T(8,128)(2,1)S(1)}, bf16[128,1024]{1,0:T(8,128)(2,1)}, u32[]{:S(2)}) copy-start(bf16[128,1024]{1,0:T(8,128)(2,1)} %get-tuple-element.92.__1_.a_ref) | copy-start | bytes 786436
  79.6 7.4 %copy-start.5 = (s32[3]{0:T(128)S(1)}, s32[3]{0:T(128)}, u32[]{:S(2)}) copy-start(s32[3]{0:T(128)} %pad_add_fusion.t_ref) | copy-start | bytes 40
  79.6 7.4 %collective-permute-start.30 = (bf16[8,4,64,1024]{3,2,1,0:T(8,128)(2,1)}, bf16[8,4,64,1024]{3,2,1,0:T(8,128)(2,1)S(1)}, u32[]{:S(2)}, u32[]{:S(2)}) collective-permute-start(bf16[8,4,64,1024]{3,2,1,0:T(8,128)(2,1)} %tied.1.own), channel_id=1, source_target_pairs={{0,4},{4,0},{1,5},{5,1},{2,6},{6,2},{3,7},{7,3},{8,12},{12,8},{9,1... | collective-permute-start | bytes 12582920 | tf_op jit(solution)/shard_map/ppermute | solution.py:385
  96.8 28.6 %all-to-all-start.1 = ((bf16[4,128,1024]{2,1,0:T(8,128)(2,1)}), bf16[4,128,1024]{2,1,0:T(8,128)(2,1)S(1)}, u32[]{:S(2)}, u32[]{:S(2)}) async-start(bf16[4,128,1024]{2,1,0:T(8,128)(2,1)} %get-tuple-element.93), calls=%async_computation.1 | async-start | bytes 2097152 | tf_op jit(solution)/shard_map/all_to_all | solution.py:62
  112.5 16.4 %collective-permute-start.31 = (bf16[4,192,128]{2,1,0:T(8,128)(2,1)}, bf16[4,192,128]{2,1,0:T(8,128)(2,1)S(1)}, u32[]{:S(2)}, u32[]{:S(2)}) collective-permute-start(bf16[4,192,128]{2,1,0:T(8,128)(2,1)} %get-tuple-element.100), channel_id=1, source_target_pairs={{0,1},{1,2},{2,3},{3,0},{4,5},{5,6},{6,7},{7,4},{8,9},{9,10},{10,1... | collective-permute-start | bytes 589832 | tf_op jit(solution)/shard_map/ppermute | solution.py:57
  114.6 14.3 %collective-permute-start.32 = (bf16[4,192,128]{2,1,0:T(8,128)(2,1)}, bf16[4,192,128]{2,1,0:T(8,128)(2,1)S(1)}, u32[]{:S(2)}, u32[]{:S(2)}) collective-permute-start(bf16[4,192,128]{2,1,0:T(8,128)(2,1)} %get-tuple-element.101), channel_id=1, source_target_pairs={{0,2},{1,3},{2,0},{3,1},{4,6},{5,7},{6,4},{7,5},{8,10},{9,11},{10,... | collective-permute-start | bytes 589832 | tf_op jit(solution)/shard_map/ppermute | solution.py:57
  117.3 11.7 %collective-permute-start.33 = (bf16[4,192,128]{2,1,0:T(8,128)(2,1)}, bf16[4,192,128]{2,1,0:T(8,128)(2,1)S(1)}, u32[]{:S(2)}, u32[]{:S(2)}) collective-permute-start(bf16[4,192,128]{2,1,0:T(8,128)(2,1)} %get-tuple-element.102), channel_id=1, source_target_pairs={{0,3},{1,0},{2,1},{3,2},{4,7},{5,4},{6,5},{7,6},{8,11},{9,8},{10,9... | collective-permute-start | bytes 589832 | tf_op jit(solution)/shard_map/ppermute | solution.py:57
  118.7 10.2 %copy-start.8 = (bf16[4,192,128]{2,1,0:T(8,128)(2,1)S(1)}, bf16[4,192,128]{2,1,0:T(8,128)(2,1)}, u32[]{:S(2)}) copy-start(bf16[4,192,128]{2,1,0:T(8,128)(2,1)} %get-tuple-element.99) | copy-start | bytes 589828
  125.4 17.8 %all-to-all-start.2 = ((bf16[4,128,1024]{2,1,0:T(8,128)(2,1)}), bf16[4,128,1024]{2,1,0:T(8,128)(2,1)S(1)}, u32[]{:S(2)}, u32[]{:S(2)}) async-start(bf16[4,128,1024]{2,1,0:T(8,128)(2,1)} %hidden.1), calls=%async_computation.2 | async-start | bytes 2097152 | tf_op jit(solution)/shard_map/all_to_all | solution.py:62
  129.4 8.1 %collective-permute-start.21 = (bf16[2,192,128]{2,1,0:T(8,128)(2,1)S(1)}, bf16[2,192,128]{2,1,0:T(8,128)(2,1)}, u32[]{:S(2)}, u32[]{:S(2)}) collective-permute-start(bf16[2,192,128]{2,1,0:T(8,128)(2,1)S(1)} %get-tuple-element.167), channel_id=1, source_target_pairs={{0,16},{4,20},{8,24},{12,28},{16,32},{20,36},{24,40},{28,44},{32,4... | collective-permute-start | bytes 294920 | tf_op jit(solution)/shard_map/cond/branch_4_fun/ppermute | solution.py:340
  129.5 8.0 %collective-permute-start.20 = (bf16[2,192,128]{2,1,0:T(8,128)(2,1)S(1)}, bf16[2,192,128]{2,1,0:T(8,128)(2,1)}, u32[]{:S(2)}, u32[]{:S(2)}) collective-permute-start(bf16[2,192,128]{2,1,0:T(8,128)(2,1)S(1)} %get-tuple-element.168), channel_id=1, source_target_pairs={{0,8},{4,12},{8,16},{12,20},{16,24},{20,28},{24,32},{28,36},{32,40... | collective-permute-start | bytes 294920 | tf_op jit(solution)/shard_map/cond/branch_4_fun/ppermute | solution.py:340
  (7 other events, 13.6 us)
Sparse Core Ops, SparseCore 0:
  19.3 60.1 all-gather.2

commit v5 on v3

--- a/solution.py
+++ b/solution.py
@@ -1,4 +1,5 @@
 import functools
+import itertools
 import math
 
 import jax
@@ -340,13 +341,21 @@
 
 def pairs_moved(blocks, gaps, sign):
     n = math.prod(lax.axis_size(a) for a in DP)
+    low = jnp.minimum(gaps[0], gaps[1])
+    high = jnp.maximum(gaps[0], gaps[1])
+    first_low = gaps[0] == low
     pairs = blocks[:2], blocks[2:]
-    got = [None, None]
-    for by in range(1, WINDOW + 1):
-        sent = jnp.where(gaps[0] == by, *pairs)
-        came = lax.ppermute(sent, DP, [(i, (i + sign * by) % n) for i in range(n)])
-        got = [came if g is None else jnp.where(gaps[k] == by, came, g) for k, g in enumerate(got)]
-    return jnp.concatenate(got, axis=0)
+
+    def moved(x, by):
+        return lax.ppermute(x, DP, [(i, (i + sign * by) % n) for i in range(n)])
+
+    choices = list(itertools.combinations(range(1, WINDOW + 1), 2))
+    which = sum(i * ((low == a) & (high == b)).astype(jnp.int32) for i, (a, b) in enumerate(choices))
+    branches = [lambda x, y, a=a, b=b: (moved(x, a), moved(y, b)) for a, b in choices]
+    near, far = lax.switch(
+        which, branches, jnp.where(first_low, *pairs), jnp.where(first_low, *pairs[::-1])
+    )
+    return jnp.concatenate([jnp.where(first_low, near, far), jnp.where(first_low, far, near)], axis=0)
 
 
 def gathered_plane(rows):

time: 156 us -> 148 us (0.949)
  starting transfers between devices: 34.3 us -> 27.8 us
  waiting for transfers between devices: 42 us -> 38.8 us
  other arithmetic: 6.27 us -> 8.1 us
  between operations: 18.9 us -> 17.2 us
    all_to_all x3, waiting for transfers between devices: 3.55 us -> 12.1 us  [exchanged(): return lax.all_to_all(x, 'tensor', split_axis=0, concat_axis=0, tiled=True)]
    ppermute x8 -> x4, starting transfers between devices: 7.16 us -> 0.44 us  [moved(): return lax.ppermute(x, DP, [(i, (i + sign * by) % n) for i in range(n)])]
    all_gather x1, waiting for transfers between devices: 7.42 us -> 3.21 us  [gathered_plane(): return lax.all_gather(jnp.stack(along), 'z', axis=0)]
    ppermute x8 -> x4, waiting for transfers between devices: 19.8 us -> 15.6 us  [moved(): return lax.ppermute(x, DP, [(i, (i + sign * by) % n) for i in range(n)])]
    ppermute x3, waiting for transfers between devices: 3.46 us -> 0.01 us  [to_peers(): lax.ppermute(pieces[r], 'tensor', [(i, (i + r) % n) for i in range(n)])]
    select_n x4, other arithmetic: 0.12 us -> 1.95 us  [the longest x2 1.91 us: pairs_moved(): jnp.where(first_low, near, far)]
  transfers between devices with their start and end apart: 22 -> 18, of which waited for: 15 -> 10; matrix products, arithmetic and copies ran while one was open for 4% -> 5% of each run, Pallas kernels for 25% -> 27%
where the time goes in v5:
time: 148 us; the launch traced here: 146 us
  Pallas kernels  45 us (30%)
  waiting for transfers between devices  38.8 us (26%)
  starting transfers between devices  27.8 us (19%)
  between operations  17.2 us (12%)
  local copies, waits for them, and re-layouts  9.43 us (6%)
  other arithmetic  8.1 us (5%)
    ppermute x4, waiting for transfers between devices, moved(): return lax.ppermute(x, DP, [(i, (i + sign * by) % n) for i in range(n)])  15.6 us
    all_to_all x3, starting transfers between devices, exchanged(): return lax.all_to_all(x, 'tensor', split_axis=0, concat_axis=0, tiled=True)  12.4 us
    all_to_all x3, waiting for transfers between devices, exchanged(): return lax.all_to_all(x, 'tensor', split_axis=0, concat_axis=0, tiled=True)  12.1 us
    pallas_call x1, Pallas kernels, backward_of(): pl.pallas_call(functools.partial(backward_kernel, 1.0 / math.sqrt(HEAD)),...  11.4 us
    pallas_call x2, Pallas kernels, output_of(): pl.pallas_call(functools.partial(output_kernel, first), out_shape=(jax.Sh...  10.8 us
    pallas_call x1, Pallas kernels, forward_of(): pl.pallas_call(functools.partial(forward_kernel, 1.0 / math.sqrt(HEAD)),...  10.1 us
    ppermute x3, waiting for transfers between devices, gathered_plane(): along.append(lax.ppermute(rows, 'x', [(i, (i + s) % n) for i in range(n)]))  7.79 us
    unnamed x26, local copies, waits for them, and re-layouts  7.22 us
  transfers between devices with their start and end apart: 18, of which 10 were waited for; matrix products, arithmetic and copies ran while one was open for 5% of the time, Pallas kernels for 27%

profile of v5, /device:TPU:96, one launch (start us, length us, event | category | flops | bytes accessed | tf_op | source)
XLA Modules:
  0.0 146.4 jit_solution(10692533516396343938)
XLA Ops:
  7.2 2.8 %collective-permute-start.29 = (bf16[64,1024]{1,0:T(8,128)(2,1)}, bf16[64,1024]{1,0:T(8,128)(2,1)S(1)}, u32[]{:S(2)}, u32[]{:S(2)}) collective-permute-start(bf16[64,1024]{1,0:T(8,128)(2,1)} %bitcast.23), channel_id=1, source_target_pairs={{0,24},{8,0},{16,8},{24,16},{1,25},{9,1},{17,9},{25,17},{2,26},{10... | collective-permute-start | bytes 393224 | tf_op jit(solution)/shard_map/ppermute | solution.py:365
  11.7 4.2 %collective-permute-done.29 = bf16[64,1024]{1,0:T(8,128)(2,1)S(1)} collective-permute-done((bf16[64,1024]{1,0:T(8,128)(2,1)}, bf16[64,1024]{1,0:T(8,128)(2,1)S(1)}, u32[]{:S(2)}, u32[]{:S(2)}) %collective-permute-start.29) | collective-permute-done | bytes 131104 | tf_op jit(solution)/shard_map/ppermute | solution.py:365
  16.0 2.2 %collective-permute-done.28 = bf16[64,1024]{1,0:T(8,128)(2,1)S(1)} collective-permute-done((bf16[64,1024]{1,0:T(8,128)(2,1)}, bf16[64,1024]{1,0:T(8,128)(2,1)S(1)}, u32[]{:S(2)}, u32[]{:S(2)}) %collective-permute-start.28) | collective-permute-done | bytes 131104 | tf_op jit(solution)/shard_map/ppermute | solution.py:365
  19.5 1.8 %pad_maximum_fusion.1 = bf16[4,64,1024]{2,1,0:T(8,128)(2,1)} fusion(bf16[1,64,1024]{2,1,0:T(8,128)(2,1)S(1)} %bitcast.27, bf16[1,64,1024]{2,1,0:T(8,128)(2,1)S(1)} %bitcast.28, bf16[1,64,1024]{2,1,0:T(8,128)(2,1)S(1)} %bitcast.29, bf16[1,64,1024]{2,1,0:T(8,128)(2,1)} %bitcast.26), kind=kLoop, calls=%fused_computation.13 | loop fusion | flops 786432 | bytes 1048576 | tf_op jit(solution)/shard_map/stack | solution.py:366
  24.1 4.5 %all-to-all-start = ((bf16[4,256,1024]{2,1,0:T(8,128)(2,1)}), bf16[4,256,1024]{2,1,0:T(8,128)(2,1)S(1)}, u32[]{:S(2)}, u32[]{:S(2)}) async-start(bf16[4,256,1024]{2,1,0:T(8,128)(2,1)} %broadcast_in_dim.3), calls=%async_computation | async-start | bytes 4194304 | tf_op jit(solution)/shard_map/all_to_all | solution.py:62
  32.2 8.1 %conditional.2 = (bf16[2,192,128]{2,1,0:T(8,128)(2,1)}, bf16[2,192,128]{2,1,0:T(8,128)(2,1)}) conditional(s32[]{:T(128)} %clamp.4, (bf16[2,192,128]{2,1,0:T(8,128)(2,1)S(1)}, bf16[2,192,128]{2,1,0:T(8,128)(2,1)S(1)}) %tuple.56, (bf16[2,192,128]{2,1,0:T(8,128)(2,1)S(1)}, bf16[2,192,128]{2,1,0:T(8,128)(2,1)S(1)}) %tuple.56, ...), branch_computations={%region_0.1_spmd, %region_1.2_spmd, %region_2.3_spmd, %region_3.4_... | conditional | bytes 786528 | solution.py:355
  32.5 4.7 %collective-permute-done = bf16[2,192,128]{2,1,0:T(8,128)(2,1)} collective-permute-done((bf16[2,192,128]{2,1,0:T(8,128)(2,1)S(1)}, bf16[2,192,128]{2,1,0:T(8,128)(2,1)}, u32[]{:S(2)}, u32[]{:S(2)}) %collective-permute-start) | collective-permute-done | bytes 98336 | tf_op jit(solution)/shard_map/cond/branch_0_fun/ppermute | solution.py:350
  37.2 3.2 %collective-permute-done.1 = bf16[2,192,128]{2,1,0:T(8,128)(2,1)} collective-permute-done((bf16[2,192,128]{2,1,0:T(8,128)(2,1)S(1)}, bf16[2,192,128]{2,1,0:T(8,128)(2,1)}, u32[]{:S(2)}, u32[]{:S(2)}) %collective-permute-start.1) | collective-permute-done | bytes 98336 | tf_op jit(solution)/shard_map/cond/branch_0_fun/ppermute | solution.py:350
  41.4 3.7 %collective-permute-start.24 = (bf16[4,192,128]{2,1,0:T(8,128)(2,1)S(1)}, bf16[4,192,128]{2,1,0:T(8,128)(2,1)S(1)}, u32[]{:S(2)}, u32[]{:S(2)}) collective-permute-start(bf16[4,192,128]{2,1,0:T(8,128)(2,1)S(1)} %pad_maximum_fusion.2.n0), channel_id=1, source_target_pairs={{1,0},{2,1},{3,2},{0,3},{5,4},{6,5},{7,6},{4,7},{9,8},{10,9},{11,1... | collective-permute-start | bytes 589832 | tf_op jit(solution)/shard_map/ppermute | solution.py:49
  47.4 9.0 %all-to-all-done.h_ref.g_ref = bf16[4,256,1024]{2,1,0:T(8,128)(2,1)S(1)} async-done(((bf16[4,256,1024]{2,1,0:T(8,128)(2,1)}), bf16[4,256,1024]{2,1,0:T(8,128)(2,1)S(1)}, u32[]{:S(2)}, u32[]{:S(2)}) %all-to-all-start) | async-done | bytes 2097184 | tf_op jit(solution)/shard_map/all_to_all | solution.py:62
  57.8 6.0 %query.1.q_ref = bf16[128,1024]{1,0:T(8,128)(2,1)} custom-call(bf16[4,256,1024]{2,1,0:T(8,128)(2,1)} %copy-done, bf16[4096,1024]{1,0:T(8,128)(2,1)} %w_ref.3), custom_call_target="tpu_custom_call" | custom-call | flops 1073741824 | bytes 8388608 | tf_op jit(solution)/shard_map/query/pallas_call | solution.py:107
  65.2 10.1 %forward.1 = (bf16[512,1024]{1,0:T(8,128)(2,1)}, bf16[512,1024]{1,0:T(8,128)(2,1)}, f32[8,2,64,256]{3,2,1,0:T(8,128)}, bf16[128,1024]{1,0:T(8,128)(2,1)}) custom-call(s32[3]{0:T(128)} %pad_add_fusion.t_ref, bf16[128,1024]{1,0:T(8,128)(2,1)} %query.1.q_ref, bf16[4,192,128]{2,1,0:T(8,128)(2,1)} %copy-done.7, bf16[4,192,128]{2,1,0:T(8,128)(2,1)} %copy-done.9, ...), custom_call_target="tpu_custom_call" | custom-call | flops 1610612736 | bytes 10000000 | tf_op jit(solution)/shard_map/forward/pallas_call | solution.py:159
  75.3 3.2 %all-gather.3.cloned.1.call-done = bf16[32,64,1024]{2,1,0:T(8,128)(2,1)} async-done(((bf16[4,64,1024]{2,1,0:T(8,128)(2,1)}), bf16[32,64,1024]{2,1,0:T(8,128)(2,1)}) %all-gather.3.cloned.1.call-update) | async-done | bytes 4194320 | tf_op jit(solution)/shard_map/all_gather | solution.py:366
  80.2 2.2 %copy-done.2 = bf16[8,4,64,1024]{3,2,1,0:T(8,128)(2,1)S(1)} copy-done((bf16[8,4,64,1024]{3,2,1,0:T(8,128)(2,1)S(1)}, bf16[8,4,64,1024]{3,2,1,0:T(8,128)(2,1)}, u32[]{:S(2)}) %copy-start.2) | copy-done | bytes 4194328
  82.3 5.0 %output.2 = (bf16[4,128,1024]{2,1,0:T(8,128)(2,1)S(1)}, f32[128,1024]{1,0:T(8,128)S(1)}) custom-call(s32[3]{0:T(128)S(1)} %copy-done.5, bf16[128,1024]{1,0:T(8,128)(2,1)S(1)} %copy-done.3, bf16[4,256,1024]{2,1,0:T(8,128)(2,1)S(1)} %copy-done.1, bf16[8,4,64,1024]{3,2,1,0:T(8,128)(2,1)S(1)} %copy-done.2), custom_call_target="tpu_custom_call" | custom-call | flops 1073741824 | bytes 4194304 | tf_op jit(solution)/shard_map/output/pallas_call | solution.py:227
  87.4 5.8 %output.3 = (bf16[4,128,1024]{2,1,0:T(8,128)(2,1)}, bf16[128,1024]{1,0:T(8,128)(2,1)S(1)}) custom-call(s32[3]{0:T(128)S(1)} %copy-done.5, bf16[128,1024]{1,0:T(8,128)(2,1)S(1)} %copy-done.3, bf16[4,256,1024]{2,1,0:T(8,128)(2,1)S(1)} %copy-done.1, bf16[8,4,64,1024]{3,2,1,0:T(8,128)(2,1)S(1)} %collective-permute-done.30.w_ref, ...), custom_call_target="tpu_custom_call" | custom-call | flops 1073741824 | bytes 4194304 | tf_op jit(solution)/shard_map/output/pallas_call | solution.py:227
  93.9 4.3 %all-to-all-start.1 = ((bf16[4,128,1024]{2,1,0:T(8,128)(2,1)}), bf16[4,128,1024]{2,1,0:T(8,128)(2,1)S(1)}, u32[]{:S(2)}, u32[]{:S(2)}) async-start(bf16[4,128,1024]{2,1,0:T(8,128)(2,1)} %get-tuple-element.97), calls=%async_computation.1 | async-start | bytes 2097152 | tf_op jit(solution)/shard_map/all_to_all | solution.py:62
  98.2 11.4 %backward.1 = (bf16[128,1024]{1,0:T(8,128)(2,1)}, bf16[4,192,128]{2,1,0:T(8,128)(2,1)}, bf16[4,192,128]{2,1,0:T(8,128)(2,1)}, bf16[4,192,128]{2,1,0:T(8,128)(2,1)}, bf16[4,192,128]{2,1,0:T(8,128)(2,1)}) custom-call(s32[3]{0:T(128)} %pad_add_fusion.t_ref, bf16[128,1024]{1,0:T(8,128)(2,1)} %copy-done.4, bf16[128,1024]{1,0:T(8,128)(2,1)} %query.1.q_ref, ...), custom_call_target="tpu_custom_call" | custom-call | flops 1610612736 | bytes 10000000 | tf_op jit(solution)/shard_map/backward/pallas_call | solution.py:295
  109.6 3.3 %collective-permute-start.33 = (bf16[4,192,128]{2,1,0:T(8,128)(2,1)}, bf16[4,192,128]{2,1,0:T(8,128)(2,1)S(1)}, u32[]{:S(2)}, u32[]{:S(2)}) collective-permute-start(bf16[4,192,128]{2,1,0:T(8,128)(2,1)} %get-tuple-element.106), channel_id=1, source_target_pairs={{0,3},{1,0},{2,1},{3,2},{4,7},{5,4},{6,5},{7,6},{8,11},{9,8},{10,9... | collective-permute-start | bytes 589832 | tf_op jit(solution)/shard_map/ppermute | solution.py:57
  114.6 6.7 %hidden.1 = bf16[4,128,1024]{2,1,0:T(8,128)(2,1)} custom-call(bf16[128,1024]{1,0:T(8,128)(2,1)} %get-tuple-element.102.g_ref, bf16[4096,1024]{1,0:T(8,128)(2,1)} %w_ref.3), custom_call_target="tpu_custom_call" | custom-call | flops 1073741824 | bytes 8388608 | tf_op jit(solution)/shard_map/hidden/pallas_call | solution.py:330
  121.3 3.6 %all-to-all-start.2 = ((bf16[4,128,1024]{2,1,0:T(8,128)(2,1)}), bf16[4,128,1024]{2,1,0:T(8,128)(2,1)S(1)}, u32[]{:S(2)}, u32[]{:S(2)}) async-start(bf16[4,128,1024]{2,1,0:T(8,128)(2,1)} %hidden.1), calls=%async_computation.2 | async-start | bytes 2097152 | tf_op jit(solution)/shard_map/all_to_all | solution.py:62
  125.1 8.1 %conditional.3 = (bf16[2,192,128]{2,1,0:T(8,128)(2,1)}, bf16[2,192,128]{2,1,0:T(8,128)(2,1)}) conditional(s32[]{:T(128)} %clamp.4, (pred[]{:T(512)}, (), bf16[4,192,128]{2,1,0:T(8,128)(2,1)S(1)}, bf16[4,192,128]{2,1,0:T(8,128)(2,1)S(1)}, (), /*index=5*/()) %tuple.57, (pred[]{:T(512)}, (), ...), branch_computations={%region_6.7_spmd, %region_7.8_spmd, %region_8.9_spmd, %region_9.10... | conditional | flops 98304 | bytes 1179745 | solution.py:355
  125.3 6.6 %collective-permute-done.12 = bf16[2,192,128]{2,1,0:T(8,128)(2,1)} collective-permute-done((bf16[2,192,128]{2,1,0:T(8,128)(2,1)S(1)}, bf16[2,192,128]{2,1,0:T(8,128)(2,1)}, u32[]{:S(2)}, u32[]{:S(2)}) %collective-permute-start.12) | collective-permute-done | bytes 98336 | tf_op jit(solution)/shard_map/cond/branch_0_fun/ppermute | solution.py:350
  135.6 3.1 %all-to-all-done.2 = bf16[4,128,1024]{2,1,0:T(8,128)(2,1)S(1)} async-done(((bf16[4,128,1024]{2,1,0:T(8,128)(2,1)}), bf16[4,128,1024]{2,1,0:T(8,128)(2,1)S(1)}, u32[]{:S(2)}, u32[]{:S(2)}) %all-to-all-start.2) | async-done | bytes 1048608 | tf_op jit(solution)/shard_map/all_to_all | solution.py:62
  (63 shorter events, 21.8 us)
Async XLA Ops:
  7.2 71.4 %all-gather.3.cloned.1.call-start = ((), (), s32[]{:S(2)}) async-start(), calls=%async_computation.3 | async-start | bytes 4718592 | tf_op jit(solution)/shard_map/all_gather | solution.py:366
  7.2 8.7 %collective-permute-start.29 = (bf16[64,1024]{1,0:T(8,128)(2,1)}, bf16[64,1024]{1,0:T(8,128)(2,1)S(1)}, u32[]{:S(2)}, u32[]{:S(2)}) collective-permute-start(bf16[64,1024]{1,0:T(8,128)(2,1)} %bitcast.23), channel_id=1, source_target_pairs={{0,24},{8,0},{16,8},{24,16},{1,25},{9,1},{17,9},{25,17},{2,26},{10... | collective-permute-start | bytes 393224 | tf_op jit(solution)/shard_map/ppermute | solution.py:365
  10.0 8.1 %collective-permute-start.28 = (bf16[64,1024]{1,0:T(8,128)(2,1)}, bf16[64,1024]{1,0:T(8,128)(2,1)S(1)}, u32[]{:S(2)}, u32[]{:S(2)}) collective-permute-start(bf16[64,1024]{1,0:T(8,128)(2,1)} %bitcast.24), channel_id=1, source_target_pairs={{0,16},{8,24},{16,0},{24,8},{1,17},{9,25},{17,1},{25,9},{2,18},{10... | collective-permute-start | bytes 393224 | tf_op jit(solution)/shard_map/ppermute | solution.py:365
  10.8 8.7 %collective-permute-start.27 = (bf16[64,1024]{1,0:T(8,128)(2,1)}, bf16[64,1024]{1,0:T(8,128)(2,1)S(1)}, u32[]{:S(2)}, u32[]{:S(2)}) collective-permute-start(bf16[64,1024]{1,0:T(8,128)(2,1)} %bitcast.25), channel_id=1, source_target_pairs={{0,8},{8,16},{16,24},{24,0},{1,9},{9,17},{17,25},{25,1},{2,10},{10... | collective-permute-start | bytes 393224 | tf_op jit(solution)/shard_map/ppermute | solution.py:365
  21.3 7.3 %copy-start.12 = (s32[1,4]{1,0:T(1,128)S(1)}, s32[1,4]{1,0:T(1,128)}, u32[]{:S(2)}) copy-start(s32[1,4]{1,0:T(1,128)} %param.28) | copy-start | bytes 52
  21.3 10.9 %copy-start.6 = (bf16[4,128,192]{1,2,0:T(8,128)(2,1)S(1)}, bf16[4,128,192]{1,2,0:T(8,128)(2,1)}, u32[]{:S(2)}) copy-start(bf16[4,128,192]{1,2,0:T(8,128)(2,1)} %param.27) | copy-start | bytes 589828
  24.1 32.4 %all-to-all-start = ((bf16[4,256,1024]{2,1,0:T(8,128)(2,1)}), bf16[4,256,1024]{2,1,0:T(8,128)(2,1)S(1)}, u32[]{:S(2)}, u32[]{:S(2)}) async-start(bf16[4,256,1024]{2,1,0:T(8,128)(2,1)} %broadcast_in_dim.3), calls=%async_computation | async-start | bytes 4194304 | tf_op jit(solution)/shard_map/all_to_all | solution.py:62
  32.3 4.9 %collective-permute-start = (bf16[2,192,128]{2,1,0:T(8,128)(2,1)S(1)}, bf16[2,192,128]{2,1,0:T(8,128)(2,1)}, u32[]{:S(2)}, u32[]{:S(2)}) collective-permute-start(bf16[2,192,128]{2,1,0:T(8,128)(2,1)S(1)} %get-tuple-element.48), channel_id=1, source_target_pairs={{0,252},{4,0},{8,4},{12,8},{16,12},{20,16},{24,20},{28,24},{32,28}... | collective-permute-start | bytes 294920 | tf_op jit(solution)/shard_map/cond/branch_0_fun/ppermute | solution.py:350
  32.4 8.0 %collective-permute-start.1 = (bf16[2,192,128]{2,1,0:T(8,128)(2,1)S(1)}, bf16[2,192,128]{2,1,0:T(8,128)(2,1)}, u32[]{:S(2)}, u32[]{:S(2)}) collective-permute-start(bf16[2,192,128]{2,1,0:T(8,128)(2,1)S(1)} %get-tuple-element.49), channel_id=1, source_target_pairs={{0,248},{4,252},{8,0},{12,4},{16,8},{20,12},{24,16},{28,20},{32,24... | collective-permute-start | bytes 294920 | tf_op jit(solution)/shard_map/cond/branch_0_fun/ppermute | solution.py:350
  41.3 22.5 %copy-start.7 = (bf16[4,192,128]{2,1,0:T(8,128)(2,1)}, bf16[4,192,128]{2,1,0:T(8,128)(2,1)S(1)}, u32[]{:S(2)}) copy-start(bf16[4,192,128]{2,1,0:T(8,128)(2,1)S(1)} %pad_maximum_fusion.2.n0) | copy-start | bytes 589828
  41.4 22.5 %collective-permute-start.24 = (bf16[4,192,128]{2,1,0:T(8,128)(2,1)S(1)}, bf16[4,192,128]{2,1,0:T(8,128)(2,1)S(1)}, u32[]{:S(2)}, u32[]{:S(2)}) collective-permute-start(bf16[4,192,128]{2,1,0:T(8,128)(2,1)S(1)} %pad_maximum_fusion.2.n0), channel_id=1, source_target_pairs={{1,0},{2,1},{3,2},{0,3},{5,4},{6,5},{7,6},{4,7},{9,8},{10,9},{11,1... | collective-permute-start | bytes 589832 | tf_op jit(solution)/shard_map/ppermute | solution.py:49
  45.0 18.8 %collective-permute-start.25 = (bf16[4,192,128]{2,1,0:T(8,128)(2,1)S(1)}, bf16[4,192,128]{2,1,0:T(8,128)(2,1)S(1)}, u32[]{:S(2)}, u32[]{:S(2)}) collective-permute-start(bf16[4,192,128]{2,1,0:T(8,128)(2,1)S(1)} %pad_maximum_fusion.2.n0), channel_id=1, source_target_pairs={{2,0},{3,1},{0,2},{1,3},{6,4},{7,5},{4,6},{5,7},{10,8},{11,9},{8,1... | collective-permute-start | bytes 589832 | tf_op jit(solution)/shard_map/ppermute | solution.py:49
  45.9 17.9 %collective-permute-start.26 = (bf16[4,192,128]{2,1,0:T(8,128)(2,1)S(1)}, bf16[4,192,128]{2,1,0:T(8,128)(2,1)S(1)}, u32[]{:S(2)}, u32[]{:S(2)}) collective-permute-start(bf16[4,192,128]{2,1,0:T(8,128)(2,1)S(1)} %pad_maximum_fusion.2.n0), channel_id=1, source_target_pairs={{3,0},{0,1},{1,2},{2,3},{7,4},{4,5},{5,6},{6,7},{11,8},{8,9},{9,10... | collective-permute-start | bytes 589832 | tf_op jit(solution)/shard_map/ppermute | solution.py:49
  78.6 1.6 %copy-start.5 = (s32[3]{0:T(128)S(1)}, s32[3]{0:T(128)}, u32[]{:S(2)}) copy-start(s32[3]{0:T(128)} %pad_add_fusion.t_ref) | copy-start | bytes 40
  78.6 8.8 %collective-permute-start.30 = (bf16[8,4,64,1024]{3,2,1,0:T(8,128)(2,1)}, bf16[8,4,64,1024]{3,2,1,0:T(8,128)(2,1)S(1)}, u32[]{:S(2)}, u32[]{:S(2)}) collective-permute-start(bf16[8,4,64,1024]{3,2,1,0:T(8,128)(2,1)} %tied.1.w_ref), channel_id=1, source_target_pairs={{0,4},{4,0},{1,5},{5,1},{2,6},{6,2},{3,7},{7,3},{8,12},{12,8},{9,1... | collective-permute-start | bytes 12582920 | tf_op jit(solution)/shard_map/ppermute | solution.py:395
  80.1 2.2 %copy-start.2 = (bf16[8,4,64,1024]{3,2,1,0:T(8,128)(2,1)S(1)}, bf16[8,4,64,1024]{3,2,1,0:T(8,128)(2,1)}, u32[]{:S(2)}) copy-start(bf16[8,4,64,1024]{3,2,1,0:T(8,128)(2,1)} %tied.1.w_ref) | copy-start | bytes 12582916
  93.9 27.4 %all-to-all-start.1 = ((bf16[4,128,1024]{2,1,0:T(8,128)(2,1)}), bf16[4,128,1024]{2,1,0:T(8,128)(2,1)S(1)}, u32[]{:S(2)}, u32[]{:S(2)}) async-start(bf16[4,128,1024]{2,1,0:T(8,128)(2,1)} %get-tuple-element.97), calls=%async_computation.1 | async-start | bytes 2097152 | tf_op jit(solution)/shard_map/all_to_all | solution.py:62
  109.6 15.3 %collective-permute-start.33 = (bf16[4,192,128]{2,1,0:T(8,128)(2,1)}, bf16[4,192,128]{2,1,0:T(8,128)(2,1)S(1)}, u32[]{:S(2)}, u32[]{:S(2)}) collective-permute-start(bf16[4,192,128]{2,1,0:T(8,128)(2,1)} %get-tuple-element.106), channel_id=1, source_target_pairs={{0,3},{1,0},{2,1},{3,2},{4,7},{5,4},{6,5},{7,6},{8,11},{9,8},{10,9... | collective-permute-start | bytes 589832 | tf_op jit(solution)/shard_map/ppermute | solution.py:57
  112.9 12.0 %collective-permute-start.32 = (bf16[4,192,128]{2,1,0:T(8,128)(2,1)}, bf16[4,192,128]{2,1,0:T(8,128)(2,1)S(1)}, u32[]{:S(2)}, u32[]{:S(2)}) collective-permute-start(bf16[4,192,128]{2,1,0:T(8,128)(2,1)} %get-tuple-element.105), channel_id=1, source_target_pairs={{0,2},{1,3},{2,0},{3,1},{4,6},{5,7},{6,4},{7,5},{8,10},{9,11},{10,... | collective-permute-start | bytes 589832 | tf_op jit(solution)/shard_map/ppermute | solution.py:57
  113.7 11.2 %collective-permute-start.31 = (bf16[4,192,128]{2,1,0:T(8,128)(2,1)}, bf16[4,192,128]{2,1,0:T(8,128)(2,1)S(1)}, u32[]{:S(2)}, u32[]{:S(2)}) collective-permute-start(bf16[4,192,128]{2,1,0:T(8,128)(2,1)} %get-tuple-element.104), channel_id=1, source_target_pairs={{0,1},{1,2},{2,3},{3,0},{4,5},{5,6},{6,7},{7,4},{8,9},{9,10},{10,1... | collective-permute-start | bytes 589832 | tf_op jit(solution)/shard_map/ppermute | solution.py:57
  114.6 10.3 %copy-start.8 = (bf16[4,192,128]{2,1,0:T(8,128)(2,1)S(1)}, bf16[4,192,128]{2,1,0:T(8,128)(2,1)}, u32[]{:S(2)}) copy-start(bf16[4,192,128]{2,1,0:T(8,128)(2,1)} %get-tuple-element.103) | copy-start | bytes 589828
  121.3 17.5 %all-to-all-start.2 = ((bf16[4,128,1024]{2,1,0:T(8,128)(2,1)}), bf16[4,128,1024]{2,1,0:T(8,128)(2,1)S(1)}, u32[]{:S(2)}, u32[]{:S(2)}) async-start(bf16[4,128,1024]{2,1,0:T(8,128)(2,1)} %hidden.1), calls=%async_computation.2 | async-start | bytes 2097152 | tf_op jit(solution)/shard_map/all_to_all | solution.py:62
  125.1 6.8 %collective-permute-start.12 = (bf16[2,192,128]{2,1,0:T(8,128)(2,1)S(1)}, bf16[2,192,128]{2,1,0:T(8,128)(2,1)}, u32[]{:S(2)}, u32[]{:S(2)}) collective-permute-start(bf16[2,192,128]{2,1,0:T(8,128)(2,1)S(1)} %get-tuple-element.164), channel_id=1, source_target_pairs={{0,4},{4,8},{8,12},{12,16},{16,20},{20,24},{24,28},{28,32},{32,36}... | collective-permute-start | bytes 294920 | tf_op jit(solution)/shard_map/cond/branch_0_fun/ppermute | solution.py:350
  125.2 7.9 %collective-permute-start.13 = (bf16[2,192,128]{2,1,0:T(8,128)(2,1)S(1)}, bf16[2,192,128]{2,1,0:T(8,128)(2,1)}, u32[]{:S(2)}, u32[]{:S(2)}) collective-permute-start(bf16[2,192,128]{2,1,0:T(8,128)(2,1)S(1)} %get-tuple-element.163), channel_id=1, source_target_pairs={{0,8},{4,12},{8,16},{12,20},{16,24},{20,28},{24,32},{28,36},{32,40... | collective-permute-start | bytes 294920 | tf_op jit(solution)/shard_map/cond/branch_0_fun/ppermute | solution.py:350
  (7 other events, 7.3 us)
Sparse Core Ops, SparseCore 0:
  21.5 57.0 all-gather.2

commit v6 on v5

--- a/solution.py
+++ b/solution.py
@@ -243,7 +243,7 @@
             pltpu.VMEM((width // deep, width // deep // 2), BF16),
             pltpu.VMEM((rows, cols), F32),
         ],
-        compiler_params=params(28),
+        compiler_params=params(56 if first else 28),
         cost_estimate=cost(2 * rows * steps * width * cols, steps * width * cols),
         name="output",
     )(t, attended, pieces, plane, *before)

time: 148 us -> 149 us (level); the launches traced: 146 us -> 149 us
  Pallas kernels: 45 us -> 47.2 us
  local copies, waits for them, and re-layouts: 9.43 us -> 7.93 us
    pallas_call x2, Pallas kernels: 10.8 us -> 13.1 us  [output_of(): pl.pallas_call(functools.partial(output_kernel, first), out_shape=(jax.Sh...]
    all_to_all x3, waiting for transfers between devices: 12.1 us -> 10.2 us  [exchanged(): return lax.all_to_all(x, 'tensor', split_axis=0, concat_axis=0, tiled=True)]
    unnamed x26 -> x28, local copies, waits for them, and re-layouts: 7.22 us -> 5.72 us
  transfers between devices with their start and end apart: 18 -> 18, of which waited for: 10 -> 11; matrix products, arithmetic and copies ran while one was open for 5% -> 5% of each run, Pallas kernels for 27% -> 28%
where the time goes in v6:
time: 149 us
  Pallas kernels  47.2 us (32%)
  waiting for transfers between devices  39.6 us (27%)
  starting transfers between devices  28.4 us (19%)
  between operations  17.4 us (12%)
  other arithmetic  8.09 us (5%)
  local copies, waits for them, and re-layouts  7.93 us (5%)
    ppermute x4, waiting for transfers between devices, moved(): return lax.ppermute(x, DP, [(i, (i + sign * by) % n) for i in range(n)])  17 us
    pallas_call x2, Pallas kernels, output_of(): pl.pallas_call(functools.partial(output_kernel, first), out_shape=(jax.Sh...  13.1 us
    all_to_all x3, starting transfers between devices, exchanged(): return lax.all_to_all(x, 'tensor', split_axis=0, concat_axis=0, tiled=True)  12.4 us
    pallas_call x1, Pallas kernels, backward_of(): pl.pallas_call(functools.partial(backward_kernel, 1.0 / math.sqrt(HEAD)),...  11.4 us
    all_to_all x3, waiting for transfers between devices, exchanged(): return lax.all_to_all(x, 'tensor', split_axis=0, concat_axis=0, tiled=True)  10.2 us
    pallas_call x1, Pallas kernels, forward_of(): pl.pallas_call(functools.partial(forward_kernel, 1.0 / math.sqrt(HEAD)),...  10.1 us
    ppermute x3, waiting for transfers between devices, gathered_plane(): along.append(lax.ppermute(rows, 'x', [(i, (i + s) % n) for i in range(n)]))  7.79 us
    pallas_call x1, Pallas kernels, hidden_of(): pl.pallas_call(hidden_kernel, out_shape=jax.ShapeDtypeStruct((4, rows, wi...  6.67 us
  transfers between devices with their start and end apart: 18, of which 11 were waited for; matrix products, arithmetic and copies ran while one was open for 5% of the time, Pallas kernels for 28%

profile of v6, /device:TPU:96, one launch (start us, length us, event | category | flops | bytes accessed | tf_op | source)
XLA Modules:
  0.0 149.0 jit_solution(12474364303305651040)
XLA Ops:
  7.2 2.8 %collective-permute-start.29 = (bf16[64,1024]{1,0:T(8,128)(2,1)}, bf16[64,1024]{1,0:T(8,128)(2,1)S(1)}, u32[]{:S(2)}, u32[]{:S(2)}) collective-permute-start(bf16[64,1024]{1,0:T(8,128)(2,1)} %bitcast.23), channel_id=1, source_target_pairs={{0,24},{8,0},{16,8},{24,16},{1,25},{9,1},{17,9},{25,17},{2,26},{10... | collective-permute-start | bytes 393224 | tf_op jit(solution)/shard_map/ppermute | solution.py:365
  11.7 4.2 %collective-permute-done.29 = bf16[64,1024]{1,0:T(8,128)(2,1)S(1)} collective-permute-done((bf16[64,1024]{1,0:T(8,128)(2,1)}, bf16[64,1024]{1,0:T(8,128)(2,1)S(1)}, u32[]{:S(2)}, u32[]{:S(2)}) %collective-permute-start.29) | collective-permute-done | bytes 131104 | tf_op jit(solution)/shard_map/ppermute | solution.py:365
  16.0 2.2 %collective-permute-done.28 = bf16[64,1024]{1,0:T(8,128)(2,1)S(1)} collective-permute-done((bf16[64,1024]{1,0:T(8,128)(2,1)}, bf16[64,1024]{1,0:T(8,128)(2,1)S(1)}, u32[]{:S(2)}, u32[]{:S(2)}) %collective-permute-start.28) | collective-permute-done | bytes 131104 | tf_op jit(solution)/shard_map/ppermute | solution.py:365
  19.5 1.8 %pad_maximum_fusion.1 = bf16[4,64,1024]{2,1,0:T(8,128)(2,1)} fusion(bf16[1,64,1024]{2,1,0:T(8,128)(2,1)S(1)} %bitcast.27, bf16[1,64,1024]{2,1,0:T(8,128)(2,1)S(1)} %bitcast.28, bf16[1,64,1024]{2,1,0:T(8,128)(2,1)S(1)} %bitcast.29, bf16[1,64,1024]{2,1,0:T(8,128)(2,1)} %bitcast.26), kind=kLoop, calls=%fused_computation.13 | loop fusion | flops 786432 | bytes 1048576 | tf_op jit(solution)/shard_map/stack | solution.py:366
  22.5 1.6 %broadcast_in_dim.3 = bf16[4,256,1024]{2,1,0:T(8,128)(2,1)} broadcast(bf16[256,1024]{1,0:T(8,128)(2,1)S(1)} %pad_maximum_fusion), dimensions={1,2} | broadcast | bytes 2621440 | tf_op jit(solution)/shard_map/broadcast_in_dim | solution.py:387
  24.1 4.5 %all-to-all-start = ((bf16[4,256,1024]{2,1,0:T(8,128)(2,1)}), bf16[4,256,1024]{2,1,0:T(8,128)(2,1)S(1)}, u32[]{:S(2)}, u32[]{:S(2)}) async-start(bf16[4,256,1024]{2,1,0:T(8,128)(2,1)} %broadcast_in_dim.3), calls=%async_computation | async-start | bytes 4194304 | tf_op jit(solution)/shard_map/all_to_all | solution.py:62
  32.4 9.0 %conditional.2 = (bf16[2,192,128]{2,1,0:T(8,128)(2,1)}, bf16[2,192,128]{2,1,0:T(8,128)(2,1)}) conditional(s32[]{:T(128)} %clamp.4, (bf16[2,192,128]{2,1,0:T(8,128)(2,1)S(1)}, bf16[2,192,128]{2,1,0:T(8,128)(2,1)S(1)}) %tuple.56, (bf16[2,192,128]{2,1,0:T(8,128)(2,1)S(1)}, bf16[2,192,128]{2,1,0:T(8,128)(2,1)S(1)}) %tuple.56, ...), branch_computations={%region_0.1_spmd, %region_1.2_spmd, %region_2.3_spmd, %region_3.4_... | conditional | bytes 786528 | solution.py:355
  33.4 4.2 %collective-permute-done.8 = bf16[2,192,128]{2,1,0:T(8,128)(2,1)} collective-permute-done((bf16[2,192,128]{2,1,0:T(8,128)(2,1)S(1)}, bf16[2,192,128]{2,1,0:T(8,128)(2,1)}, u32[]{:S(2)}, u32[]{:S(2)}) %collective-permute-start.8) | collective-permute-done | bytes 98336 | tf_op jit(solution)/shard_map/cond/branch_4_fun/ppermute | solution.py:350
  37.7 3.8 %collective-permute-done.9 = bf16[2,192,128]{2,1,0:T(8,128)(2,1)} collective-permute-done((bf16[2,192,128]{2,1,0:T(8,128)(2,1)S(1)}, bf16[2,192,128]{2,1,0:T(8,128)(2,1)}, u32[]{:S(2)}, u32[]{:S(2)}) %collective-permute-start.9) | collective-permute-done | bytes 98336 | tf_op jit(solution)/shard_map/cond/branch_4_fun/ppermute | solution.py:350
  42.5 3.5 %collective-permute-start.24 = (bf16[4,192,128]{2,1,0:T(8,128)(2,1)S(1)}, bf16[4,192,128]{2,1,0:T(8,128)(2,1)S(1)}, u32[]{:S(2)}, u32[]{:S(2)}) collective-permute-start(bf16[4,192,128]{2,1,0:T(8,128)(2,1)S(1)} %pad_maximum_fusion.2.n0), channel_id=1, source_target_pairs={{1,0},{2,1},{3,2},{0,3},{5,4},{6,5},{7,6},{4,7},{9,8},{10,9},{11,1... | collective-permute-start | bytes 589832 | tf_op jit(solution)/shard_map/ppermute | solution.py:49
  48.4 8.1 %all-to-all-done.h_ref.g_ref = bf16[4,256,1024]{2,1,0:T(8,128)(2,1)S(1)} async-done(((bf16[4,256,1024]{2,1,0:T(8,128)(2,1)}), bf16[4,256,1024]{2,1,0:T(8,128)(2,1)S(1)}, u32[]{:S(2)}, u32[]{:S(2)}) %all-to-all-start) | async-done | bytes 2097184 | tf_op jit(solution)/shard_map/all_to_all | solution.py:62
  57.8 6.0 %query.1.q_ref = bf16[128,1024]{1,0:T(8,128)(2,1)} custom-call(bf16[4,256,1024]{2,1,0:T(8,128)(2,1)} %copy-done, bf16[4096,1024]{1,0:T(8,128)(2,1)} %w_ref.3), custom_call_target="tpu_custom_call" | custom-call | flops 1073741824 | bytes 8388608 | tf_op jit(solution)/shard_map/query/pallas_call | solution.py:107
  65.2 10.1 %forward.1 = (bf16[512,1024]{1,0:T(8,128)(2,1)}, bf16[512,1024]{1,0:T(8,128)(2,1)}, f32[8,2,64,256]{3,2,1,0:T(8,128)}, bf16[128,1024]{1,0:T(8,128)(2,1)}) custom-call(s32[3]{0:T(128)} %pad_add_fusion.t_ref, bf16[128,1024]{1,0:T(8,128)(2,1)} %query.1.q_ref, bf16[4,192,128]{2,1,0:T(8,128)(2,1)} %copy-done.8, bf16[4,192,128]{2,1,0:T(8,128)(2,1)} %copy-done.10, ...), custom_call_target="tpu_custom_call" | custom-call | flops 1610612736 | bytes 10000000 | tf_op jit(solution)/shard_map/forward/pallas_call | solution.py:159
  75.3 4.3 %all-gather.3.cloned.1.call-done = bf16[32,64,1024]{2,1,0:T(8,128)(2,1)} async-done(((bf16[4,64,1024]{2,1,0:T(8,128)(2,1)}), bf16[32,64,1024]{2,1,0:T(8,128)(2,1)}) %all-gather.3.cloned.1.call-update) | async-done | bytes 4194320 | tf_op jit(solution)/shard_map/all_gather | solution.py:366
  79.6 7.3 %output.2 = (bf16[4,128,1024]{2,1,0:T(8,128)(2,1)}, f32[128,1024]{1,0:T(8,128)}) custom-call(s32[3]{0:T(128)} %pad_add_fusion.t_ref, bf16[128,1024]{1,0:T(8,128)(2,1)} %get-tuple-element.94.__1_.a_ref, bf16[4,256,1024]{2,1,0:T(8,128)(2,1)} %copy-done, bf16[8,4,64,1024]{3,2,1,0:T(8,128)(2,1)} %tied.1.w_ref), custom_call_target="tpu_custom_call" | custom-call | flops 1073741824 | bytes 4194304 | tf_op jit(solution)/shard_map/output/pallas_call | solution.py:227
  89.3 5.8 %output.3 = (bf16[4,128,1024]{2,1,0:T(8,128)(2,1)}, bf16[128,1024]{1,0:T(8,128)(2,1)S(1)}) custom-call(s32[3]{0:T(128)S(1)} %copy-done.6, bf16[128,1024]{1,0:T(8,128)(2,1)S(1)} %copy-done.2, bf16[4,256,1024]{2,1,0:T(8,128)(2,1)S(1)} %copy-done.1, bf16[8,4,64,1024]{3,2,1,0:T(8,128)(2,1)S(1)} %collective-permute-done.30.w_ref, ...), custom_call_target="tpu_custom_call" | custom-call | flops 1073741824 | bytes 4194304 | tf_op jit(solution)/shard_map/output/pallas_call | solution.py:227
  95.7 4.3 %all-to-all-start.1 = ((bf16[4,128,1024]{2,1,0:T(8,128)(2,1)}), bf16[4,128,1024]{2,1,0:T(8,128)(2,1)S(1)}, u32[]{:S(2)}, u32[]{:S(2)}) async-start(bf16[4,128,1024]{2,1,0:T(8,128)(2,1)} %get-tuple-element.97), calls=%async_computation.1 | async-start | bytes 2097152 | tf_op jit(solution)/shard_map/all_to_all | solution.py:62
  100.0 11.4 %backward.1 = (bf16[128,1024]{1,0:T(8,128)(2,1)}, bf16[4,192,128]{2,1,0:T(8,128)(2,1)}, bf16[4,192,128]{2,1,0:T(8,128)(2,1)}, bf16[4,192,128]{2,1,0:T(8,128)(2,1)}, bf16[4,192,128]{2,1,0:T(8,128)(2,1)}) custom-call(s32[3]{0:T(128)} %pad_add_fusion.t_ref, bf16[128,1024]{1,0:T(8,128)(2,1)} %copy-done.5, bf16[128,1024]{1,0:T(8,128)(2,1)} %query.1.q_ref, ...), custom_call_target="tpu_custom_call" | custom-call | flops 1610612736 | bytes 10000000 | tf_op jit(solution)/shard_map/backward/pallas_call | solution.py:295
  111.4 3.3 %collective-permute-start.33 = (bf16[4,192,128]{2,1,0:T(8,128)(2,1)}, bf16[4,192,128]{2,1,0:T(8,128)(2,1)S(1)}, u32[]{:S(2)}, u32[]{:S(2)}) collective-permute-start(bf16[4,192,128]{2,1,0:T(8,128)(2,1)} %get-tuple-element.106), channel_id=1, source_target_pairs={{0,3},{1,0},{2,1},{3,2},{4,7},{5,4},{6,5},{7,6},{8,11},{9,8},{10,9... | collective-permute-start | bytes 589832 | tf_op jit(solution)/shard_map/ppermute | solution.py:57
  116.4 6.7 %hidden.1 = bf16[4,128,1024]{2,1,0:T(8,128)(2,1)} custom-call(bf16[128,1024]{1,0:T(8,128)(2,1)} %get-tuple-element.102.g_ref, bf16[4096,1024]{1,0:T(8,128)(2,1)} %w_ref.3), custom_call_target="tpu_custom_call" | custom-call | flops 1073741824 | bytes 8388608 | tf_op jit(solution)/shard_map/hidden/pallas_call | solution.py:330
  123.1 3.7 %all-to-all-start.2 = ((bf16[4,128,1024]{2,1,0:T(8,128)(2,1)}), bf16[4,128,1024]{2,1,0:T(8,128)(2,1)S(1)}, u32[]{:S(2)}, u32[]{:S(2)}) async-start(bf16[4,128,1024]{2,1,0:T(8,128)(2,1)} %hidden.1), calls=%async_computation.2 | async-start | bytes 2097152 | tf_op jit(solution)/shard_map/all_to_all | solution.py:62
  127.2 9.4 %conditional.3 = (bf16[2,192,128]{2,1,0:T(8,128)(2,1)}, bf16[2,192,128]{2,1,0:T(8,128)(2,1)}) conditional(s32[]{:T(128)} %clamp.4, (pred[]{:T(512)}, (), bf16[4,192,128]{2,1,0:T(8,128)(2,1)S(1)}, bf16[4,192,128]{2,1,0:T(8,128)(2,1)S(1)}, (), /*index=5*/()) %tuple.57, (pred[]{:T(512)}, (), ...), branch_computations={%region_6.7_spmd, %region_7.8_spmd, %region_8.9_spmd, %region_9.10... | conditional | flops 98304 | bytes 1179745 | solution.py:355
  127.7 8.9 %collective-permute-done.20 = bf16[2,192,128]{2,1,0:T(8,128)(2,1)} collective-permute-done((bf16[2,192,128]{2,1,0:T(8,128)(2,1)S(1)}, bf16[2,192,128]{2,1,0:T(8,128)(2,1)}, u32[]{:S(2)}, u32[]{:S(2)}) %collective-permute-start.20) | collective-permute-done | bytes 98336 | tf_op jit(solution)/shard_map/cond/branch_4_fun/ppermute | solution.py:350
  139.2 2.1 %all-to-all-done.2 = bf16[4,128,1024]{2,1,0:T(8,128)(2,1)S(1)} async-done(((bf16[4,128,1024]{2,1,0:T(8,128)(2,1)}), bf16[4,128,1024]{2,1,0:T(8,128)(2,1)S(1)}, u32[]{:S(2)}, u32[]{:S(2)}) %all-to-all-start.2) | async-done | bytes 1048608 | tf_op jit(solution)/shard_map/all_to_all | solution.py:62
  (65 shorter events, 20.8 us)
Async XLA Ops:
  7.2 72.4 %all-gather.3.cloned.1.call-start = ((), (), s32[]{:S(2)}) async-start(), calls=%async_computation.3 | async-start | bytes 4718592 | tf_op jit(solution)/shard_map/all_gather | solution.py:366
  7.2 8.7 %collective-permute-start.29 = (bf16[64,1024]{1,0:T(8,128)(2,1)}, bf16[64,1024]{1,0:T(8,128)(2,1)S(1)}, u32[]{:S(2)}, u32[]{:S(2)}) collective-permute-start(bf16[64,1024]{1,0:T(8,128)(2,1)} %bitcast.23), channel_id=1, source_target_pairs={{0,24},{8,0},{16,8},{24,16},{1,25},{9,1},{17,9},{25,17},{2,26},{10... | collective-permute-start | bytes 393224 | tf_op jit(solution)/shard_map/ppermute | solution.py:365
  10.0 8.1 %collective-permute-start.28 = (bf16[64,1024]{1,0:T(8,128)(2,1)}, bf16[64,1024]{1,0:T(8,128)(2,1)S(1)}, u32[]{:S(2)}, u32[]{:S(2)}) collective-permute-start(bf16[64,1024]{1,0:T(8,128)(2,1)} %bitcast.24), channel_id=1, source_target_pairs={{0,16},{8,24},{16,0},{24,8},{1,17},{9,25},{17,1},{25,9},{2,18},{10... | collective-permute-start | bytes 393224 | tf_op jit(solution)/shard_map/ppermute | solution.py:365
  10.8 8.7 %collective-permute-start.27 = (bf16[64,1024]{1,0:T(8,128)(2,1)}, bf16[64,1024]{1,0:T(8,128)(2,1)S(1)}, u32[]{:S(2)}, u32[]{:S(2)}) collective-permute-start(bf16[64,1024]{1,0:T(8,128)(2,1)} %bitcast.25), channel_id=1, source_target_pairs={{0,8},{8,16},{16,24},{24,0},{1,9},{9,17},{17,25},{25,1},{2,10},{10... | collective-permute-start | bytes 393224 | tf_op jit(solution)/shard_map/ppermute | solution.py:365
  21.3 11.1 %copy-start.7 = (bf16[4,128,192]{1,2,0:T(8,128)(2,1)S(1)}, bf16[4,128,192]{1,2,0:T(8,128)(2,1)}, u32[]{:S(2)}) copy-start(bf16[4,128,192]{1,2,0:T(8,128)(2,1)} %param.27) | copy-start | bytes 589828
  24.1 32.4 %all-to-all-start = ((bf16[4,256,1024]{2,1,0:T(8,128)(2,1)}), bf16[4,256,1024]{2,1,0:T(8,128)(2,1)S(1)}, u32[]{:S(2)}, u32[]{:S(2)}) async-start(bf16[4,256,1024]{2,1,0:T(8,128)(2,1)} %broadcast_in_dim.3), calls=%async_computation | async-start | bytes 4194304 | tf_op jit(solution)/shard_map/all_to_all | solution.py:62
  32.5 5.2 %collective-permute-start.8 = (bf16[2,192,128]{2,1,0:T(8,128)(2,1)S(1)}, bf16[2,192,128]{2,1,0:T(8,128)(2,1)}, u32[]{:S(2)}, u32[]{:S(2)}) collective-permute-start(bf16[2,192,128]{2,1,0:T(8,128)(2,1)S(1)} %get-tuple-element.56), channel_id=1, source_target_pairs={{0,248},{4,252},{8,0},{12,4},{16,8},{20,12},{24,16},{28,20},{32,24... | collective-permute-start | bytes 294920 | tf_op jit(solution)/shard_map/cond/branch_4_fun/ppermute | solution.py:350
  32.6 8.8 %collective-permute-start.9 = (bf16[2,192,128]{2,1,0:T(8,128)(2,1)S(1)}, bf16[2,192,128]{2,1,0:T(8,128)(2,1)}, u32[]{:S(2)}, u32[]{:S(2)}) collective-permute-start(bf16[2,192,128]{2,1,0:T(8,128)(2,1)S(1)} %get-tuple-element.57), channel_id=1, source_target_pairs={{0,240},{4,244},{8,248},{12,252},{16,0},{20,4},{24,8},{28,12},{32,... | collective-permute-start | bytes 294920 | tf_op jit(solution)/shard_map/cond/branch_4_fun/ppermute | solution.py:350
  42.5 21.3 %copy-start.8 = (bf16[4,192,128]{2,1,0:T(8,128)(2,1)}, bf16[4,192,128]{2,1,0:T(8,128)(2,1)S(1)}, u32[]{:S(2)}) copy-start(bf16[4,192,128]{2,1,0:T(8,128)(2,1)S(1)} %pad_maximum_fusion.2.n0) | copy-start | bytes 589828
  42.5 21.3 %collective-permute-start.24 = (bf16[4,192,128]{2,1,0:T(8,128)(2,1)S(1)}, bf16[4,192,128]{2,1,0:T(8,128)(2,1)S(1)}, u32[]{:S(2)}, u32[]{:S(2)}) collective-permute-start(bf16[4,192,128]{2,1,0:T(8,128)(2,1)S(1)} %pad_maximum_fusion.2.n0), channel_id=1, source_target_pairs={{1,0},{2,1},{3,2},{0,3},{5,4},{6,5},{7,6},{4,7},{9,8},{10,9},{11,1... | collective-permute-start | bytes 589832 | tf_op jit(solution)/shard_map/ppermute | solution.py:49
  46.0 17.8 %collective-permute-start.25 = (bf16[4,192,128]{2,1,0:T(8,128)(2,1)S(1)}, bf16[4,192,128]{2,1,0:T(8,128)(2,1)S(1)}, u32[]{:S(2)}, u32[]{:S(2)}) collective-permute-start(bf16[4,192,128]{2,1,0:T(8,128)(2,1)S(1)} %pad_maximum_fusion.2.n0), channel_id=1, source_target_pairs={{2,0},{3,1},{0,2},{1,3},{6,4},{7,5},{4,6},{5,7},{10,8},{11,9},{8,1... | collective-permute-start | bytes 589832 | tf_op jit(solution)/shard_map/ppermute | solution.py:49
  46.9 16.9 %collective-permute-start.26 = (bf16[4,192,128]{2,1,0:T(8,128)(2,1)S(1)}, bf16[4,192,128]{2,1,0:T(8,128)(2,1)S(1)}, u32[]{:S(2)}, u32[]{:S(2)}) collective-permute-start(bf16[4,192,128]{2,1,0:T(8,128)(2,1)S(1)} %pad_maximum_fusion.2.n0), channel_id=1, source_target_pairs={{3,0},{0,1},{1,2},{2,3},{7,4},{4,5},{5,6},{6,7},{11,8},{8,9},{9,10... | collective-permute-start | bytes 589832 | tf_op jit(solution)/shard_map/ppermute | solution.py:49
  79.6 7.4 %copy-start.1 = (bf16[4,256,1024]{2,1,0:T(8,128)(2,1)S(1)}, bf16[4,256,1024]{2,1,0:T(8,128)(2,1)}, u32[]{:S(2)}) copy-start(bf16[4,256,1024]{2,1,0:T(8,128)(2,1)} %copy-done) | copy-start | bytes 6291460
  79.6 7.4 %copy-start.2 = (bf16[128,1024]{1,0:T(8,128)(2,1)S(1)}, bf16[128,1024]{1,0:T(8,128)(2,1)}, u32[]{:S(2)}) copy-start(bf16[128,1024]{1,0:T(8,128)(2,1)} %get-tuple-element.94.__1_.a_ref) | copy-start | bytes 786436
  79.6 7.4 %copy-start.6 = (s32[3]{0:T(128)S(1)}, s32[3]{0:T(128)}, u32[]{:S(2)}) copy-start(s32[3]{0:T(128)} %pad_add_fusion.t_ref) | copy-start | bytes 40
  79.6 7.4 %collective-permute-start.30 = (bf16[8,4,64,1024]{3,2,1,0:T(8,128)(2,1)}, bf16[8,4,64,1024]{3,2,1,0:T(8,128)(2,1)S(1)}, u32[]{:S(2)}, u32[]{:S(2)}) collective-permute-start(bf16[8,4,64,1024]{3,2,1,0:T(8,128)(2,1)} %tied.1.w_ref), channel_id=1, source_target_pairs={{0,4},{4,0},{1,5},{5,1},{2,6},{6,2},{3,7},{7,3},{8,12},{12,8},{9,1... | collective-permute-start | bytes 12582920 | tf_op jit(solution)/shard_map/ppermute | solution.py:395
  95.7 27.4 %all-to-all-start.1 = ((bf16[4,128,1024]{2,1,0:T(8,128)(2,1)}), bf16[4,128,1024]{2,1,0:T(8,128)(2,1)S(1)}, u32[]{:S(2)}, u32[]{:S(2)}) async-start(bf16[4,128,1024]{2,1,0:T(8,128)(2,1)} %get-tuple-element.97), calls=%async_computation.1 | async-start | bytes 2097152 | tf_op jit(solution)/shard_map/all_to_all | solution.py:62
  111.4 15.4 %collective-permute-start.33 = (bf16[4,192,128]{2,1,0:T(8,128)(2,1)}, bf16[4,192,128]{2,1,0:T(8,128)(2,1)S(1)}, u32[]{:S(2)}, u32[]{:S(2)}) collective-permute-start(bf16[4,192,128]{2,1,0:T(8,128)(2,1)} %get-tuple-element.106), channel_id=1, source_target_pairs={{0,3},{1,0},{2,1},{3,2},{4,7},{5,4},{6,5},{7,6},{8,11},{9,8},{10,9... | collective-permute-start | bytes 589832 | tf_op jit(solution)/shard_map/ppermute | solution.py:57
  114.7 12.1 %collective-permute-start.32 = (bf16[4,192,128]{2,1,0:T(8,128)(2,1)}, bf16[4,192,128]{2,1,0:T(8,128)(2,1)S(1)}, u32[]{:S(2)}, u32[]{:S(2)}) collective-permute-start(bf16[4,192,128]{2,1,0:T(8,128)(2,1)} %get-tuple-element.105), channel_id=1, source_target_pairs={{0,2},{1,3},{2,0},{3,1},{4,6},{5,7},{6,4},{7,5},{8,10},{9,11},{10,... | collective-permute-start | bytes 589832 | tf_op jit(solution)/shard_map/ppermute | solution.py:57
  115.6 11.5 %collective-permute-start.31 = (bf16[4,192,128]{2,1,0:T(8,128)(2,1)}, bf16[4,192,128]{2,1,0:T(8,128)(2,1)S(1)}, u32[]{:S(2)}, u32[]{:S(2)}) collective-permute-start(bf16[4,192,128]{2,1,0:T(8,128)(2,1)} %get-tuple-element.104), channel_id=1, source_target_pairs={{0,1},{1,2},{2,3},{3,0},{4,5},{5,6},{6,7},{7,4},{8,9},{9,10},{10,1... | collective-permute-start | bytes 589832 | tf_op jit(solution)/shard_map/ppermute | solution.py:57
  116.4 10.7 %copy-start.9 = (bf16[4,192,128]{2,1,0:T(8,128)(2,1)S(1)}, bf16[4,192,128]{2,1,0:T(8,128)(2,1)}, u32[]{:S(2)}) copy-start(bf16[4,192,128]{2,1,0:T(8,128)(2,1)} %get-tuple-element.103) | copy-start | bytes 589828
  123.1 18.1 %all-to-all-start.2 = ((bf16[4,128,1024]{2,1,0:T(8,128)(2,1)}), bf16[4,128,1024]{2,1,0:T(8,128)(2,1)S(1)}, u32[]{:S(2)}, u32[]{:S(2)}) async-start(bf16[4,128,1024]{2,1,0:T(8,128)(2,1)} %hidden.1), calls=%async_computation.2 | async-start | bytes 2097152 | tf_op jit(solution)/shard_map/all_to_all | solution.py:62
  127.5 9.1 %collective-permute-start.20 = (bf16[2,192,128]{2,1,0:T(8,128)(2,1)S(1)}, bf16[2,192,128]{2,1,0:T(8,128)(2,1)}, u32[]{:S(2)}, u32[]{:S(2)}) collective-permute-start(bf16[2,192,128]{2,1,0:T(8,128)(2,1)S(1)} %get-tuple-element.172), channel_id=1, source_target_pairs={{0,8},{4,12},{8,16},{12,20},{16,24},{20,28},{24,32},{28,36},{32,40... | collective-permute-start | bytes 294920 | tf_op jit(solution)/shard_map/cond/branch_4_fun/ppermute | solution.py:350
  127.6 9.0 %collective-permute-start.21 = (bf16[2,192,128]{2,1,0:T(8,128)(2,1)S(1)}, bf16[2,192,128]{2,1,0:T(8,128)(2,1)}, u32[]{:S(2)}, u32[]{:S(2)}) collective-permute-start(bf16[2,192,128]{2,1,0:T(8,128)(2,1)S(1)} %get-tuple-element.171), channel_id=1, source_target_pairs={{0,16},{4,20},{8,24},{12,28},{16,32},{20,36},{24,40},{28,44},{32,4... | collective-permute-start | bytes 294920 | tf_op jit(solution)/shard_map/cond/branch_4_fun/ppermute | solution.py:350
  (8 other events, 13.7 us)
Sparse Core Ops, SparseCore 0:
  21.5 58.0 all-gather.2
